TPU v7x, 32 devices: a whole 2x2x4 slice. The times are simulated.
32 devices in a mesh: groups: 2 (over x), seq: 16 (over z, y, core).
Axes of the slice: x: 2, y: 2, z: 4, core: 2. Of those that a mesh axis runs over, the one named last changes fastest.
Arguments:
- queries: bfloat16 [8192, 2048], P(('groups', 'seq')), parts along dimension 0, may hold values from -6 to 6
- keys: bfloat16 [8192, 2048], P(('groups', 'seq')), parts along dimension 0, may hold values from -6 to 6
- values: bfloat16 [8192, 2048], P(('groups', 'seq')), parts along dimension 0, may hold values from -6 to 6
- gain: float32 [2048], replicated, may hold values from 0.1 to 1.9
Outputs:
- attended: bfloat16 [8192, 2048], P(('groups', 'seq')), parts along dimension 0
There are 2 independent parts, one for each index of `groups`. A program takes and returns all parts, laid end to end along the dimension named above; an argument that names none is the same for every part. Nothing has to cross between parts.
All inputs are finite; a program needn't handle non-finite values.
Results may differ from a plain program's by a relative error of at most 0.01.
Values may be sent and summed in bfloat16 or wider, within the bound.
No kernel may reach another device: no remote copies, remote signals or barrier semaphores. Data moves between devices by JAX's collectives and lax.ppermute only.
A program may use at most 192 MiB of HBM per device.

v0:
```python
import jax
import jax.numpy as jnp
from jax import lax
from jax.sharding import PartitionSpec as P

HEADS = 32
HEAD_DIM = 64


def entering(shard, axis, combine, identity):
    size, here = (lax.axis_size(axis), lax.axis_index(axis))
    everything = lax.all_gather(shard.astype(jnp.bfloat16), axis)
    start = jnp.broadcast_to(jnp.asarray(identity, shard.dtype), shard.shape)

    def hop(k, before):
        reached = k < here
        new = combine(before, everything[k].astype(shard.dtype))
        return jnp.where(reached, new, before)

    return lax.fori_loop(0, size, hop, start)


def add_states(earlier, later):
    return earlier + later


def on_device(queries, keys, values, gain):
    count = queries.shape[0]
    fq = jax.nn.relu(queries).reshape(count, HEADS, HEAD_DIM)
    fk = jax.nn.relu(keys).reshape(count, HEADS, HEAD_DIM)
    vals = values.reshape(count, HEADS, HEAD_DIM)
    state = jnp.einsum("thd,the->hde", fk, vals, preferred_element_type=jnp.float32)
    zero_state = jnp.zeros_like(state)
    prior = entering(state, "seq", add_states, zero_state)
    prior_b = prior.astype(jnp.bfloat16)
    inter = jnp.einsum("thd,hde->the", fq, prior_b, preferred_element_type=jnp.float32)
    rows = jnp.arange(count)[:, None]
    cols = jnp.arange(count)[None, :]
    causal = cols <= rows
    width = HEADS // 4
    pieces = []
    for group in range(4):
        q_grp = fq[:, group * width : (group + 1) * width]
        k_grp = fk[:, group * width : (group + 1) * width]
        v_grp = vals[:, group * width : (group + 1) * width]
        scores = jnp.einsum("thd,shd->hts", q_grp, k_grp, preferred_element_type=jnp.float32)
        scores = jnp.where(causal[None], scores, 0.0).astype(jnp.bfloat16)
        pieces.append(jnp.einsum("hts,she->the", scores, v_grp, preferred_element_type=jnp.float32))
    intra = jnp.concatenate(pieces, axis=1)
    numer = inter + intra
    mean_sq = jnp.mean(numer * numer, axis=-1, keepdims=True)
    normed = numer * lax.rsqrt(mean_sq + 1e-05)
    normed = normed.reshape(count, HEADS * HEAD_DIM) * gain[None, :]
    return normed.astype(jnp.bfloat16)


def solution(mesh):
    return jax.shard_map(
        on_device,
        mesh=mesh,
        in_specs=(
            P(("groups", "seq"), None),
            P(("groups", "seq"), None),
            P(("groups", "seq"), None),
            P(),
        ),
        out_specs=P(("groups", "seq"), None),
        check_vma=False,
    )
```

profile of v0, /device:TPU:0, one launch (start us, length us, event | category | flops | bytes accessed | tf_op | source)
XLA Modules:
  0.0 127.8 jit_solution(8930667809056329429)
XLA Ops:
  6.5 0.0 all-gather.3.cloned.1.call-start
  6.5 1.5 %copy.15 = bf16[256,2048]{0,1:T(8,128)(2,1)S(1)} copy(bf16[256,2048]{1,0:T(8,128)(2,1)} %param.7) | data formatting | bytes 2097152 | tf_op args[1]
  8.0 0.1 broadcast_maximum_fusion.1
  8.1 1.5 %copy.16 = bf16[256,2048]{0,1:T(8,128)(2,1)S(1)} copy(bf16[256,2048]{1,0:T(8,128)(2,1)} %param.8) | data formatting | bytes 2097152 | tf_op args[2]
  9.6 1.3 convolution_convert_fusion
  10.8 0.0 all-gather.3.cloned.1.call-update
  10.9 2.3 %copy.17 = bf16[256,2048]{0,1:T(8,128)(2,1)} copy(bf16[256,2048]{1,0:T(8,128)(2,1)} %param.6) | data formatting | bytes 2097152 | tf_op args[0]
  13.2 1.3 %broadcast_maximum_fusion = bf16[256,2048]{0,1:T(8,128)(2,1)S(1)} fusion(bf16[256,2048]{0,1:T(8,128)(2,1)} %copy.17), kind=kLoop, calls=%fused_computation.15 | loop fusion | flops 524288 | bytes 2097152 | tf_op jit(solution)/shard_map/jit(relu)/max | solution.py:29
  14.5 0.0 copy-start
  14.5 0.5 select_convert_fusion
  15.0 1.3 %convolution_bitcast_fusion = f32[256,8,64]{0,2,1:T(8,128)} fusion(bf16[8,256,256]{2,1,0:T(8,128)(2,1)S(1)} %select_convert_fusion, bf16[256,32,64]{0,2,1:T(8,128)(2,1)S(1)} %bitcast.32), kind=kOutput, calls=%fused_computation.9 | convolution fusion | flops 67108864 | bytes 1835008 | tf_op jit(solution)/shard_map/hts,she->the/dot_general | solution.py:48
  16.2 0.5 select_convert_fusion.1
  16.7 1.3 convolution_bitcast_fusion.1
  18.0 0.5 select_convert_fusion.2
  18.5 1.2 convolution_bitcast_fusion.2
  19.7 0.0 copy-done
  19.7 0.5 select_convert_fusion.3
  20.2 1.2 convolution_bitcast_fusion.3
  21.4 66.6 %all-gather.3.cloned.1.call-done = bf16[512,64,64]{2,1,0:T(8,128)(2,1)} async-done(((bf16[32,64,64]{2,1,0:T(8,128)(2,1)}), bf16[512,64,64]{2,1,0:T(8,128)(2,1)}) %all-gather.3.cloned.1.call-update) | async-done | bytes 4194320 | tf_op jit(solution)/shard_map/all_gather | solution.py:12
  88.0 0.0 copy-start.1
  88.0 0.0 copy-start.2
  88.0 0.0 copy-start.3
  88.0 26.2 %while.14 = (s32[]{:T(128)}, f32[32,64,64]{2,1,0:T(8,128)S(1)}, s32[]{:T(128)}, bf16[16,32,64,64]{3,2,1,0:T(8,128)(2,1)}, s32[]{:T(128)}, /*index=5*/s32[]{:T(128)}) while((s32[]{:T(128)}, f32[32,64,64]{2,1,0:T(8,128)S(1)}, s32[]{:T(128)}, bf16[16,32,64,64]{3,2,1,0:T(8,128)(2,1)}, s32[]{:T(128)}, /*index=5*/s32[]{:T(128)}) %tuple.38), condition=%wide.region_1.2_spmd.clone, body=%wide.region_0.1_spmd.clone.sunk | while | flops 524292 | bytes 1310813 | solution.py:20
  88.0 1.8 %add_select_fusion.2 = f32[32,64,64]{2,1,0:T(8,128)S(1)} fusion(f32[32,64,64]{2,1,0:T(8,128)S(1)} %get-tuple-element.142, bf16[16,32,64,64]{3,2,1,0:T(8,128)(2,1)} %get-tuple-element.150, s32[]{:T(128)} %get-tuple-element.141, pred[]{:T(512)S(6)} %compare.3, pred[]{:T(512)S(6)} %lt.21), kind=kLoop, calls=%fused_computation.clone.1 | loop fusion | flops 524288 | bytes 1310726 | tf_op jit(solution)/shard_map/while/body/eval_jaxpr/jit(_where)/select_n | solution.py:18
  89.8 1.6 %add_select_fusion.2 = f32[32,64,64]{2,1,0:T(8,128)S(1)} fusion(f32[32,64,64]{2,1,0:T(8,128)S(1)} %get-tuple-element.142, bf16[16,32,64,64]{3,2,1,0:T(8,128)(2,1)} %get-tuple-element.150, s32[]{:T(128)} %get-tuple-element.141, pred[]{:T(512)S(6)} %compare.3, pred[]{:T(512)S(6)} %lt.21), kind=kLoop, calls=%fused_computation.clone.1 | loop fusion | flops 524288 | bytes 1310726 | tf_op jit(solution)/shard_map/while/body/eval_jaxpr/jit(_where)/select_n | solution.py:18
  91.5 1.6 %add_select_fusion.2 = f32[32,64,64]{2,1,0:T(8,128)S(1)} fusion(f32[32,64,64]{2,1,0:T(8,128)S(1)} %get-tuple-element.142, bf16[16,32,64,64]{3,2,1,0:T(8,128)(2,1)} %get-tuple-element.150, s32[]{:T(128)} %get-tuple-element.141, pred[]{:T(512)S(6)} %compare.3, pred[]{:T(512)S(6)} %lt.21), kind=kLoop, calls=%fused_computation.clone.1 | loop fusion | flops 524288 | bytes 1310726 | tf_op jit(solution)/shard_map/while/body/eval_jaxpr/jit(_where)/select_n | solution.py:18
  93.1 1.6 %add_select_fusion.2 = f32[32,64,64]{2,1,0:T(8,128)S(1)} fusion(f32[32,64,64]{2,1,0:T(8,128)S(1)} %get-tuple-element.142, bf16[16,32,64,64]{3,2,1,0:T(8,128)(2,1)} %get-tuple-element.150, s32[]{:T(128)} %get-tuple-element.141, pred[]{:T(512)S(6)} %compare.3, pred[]{:T(512)S(6)} %lt.21), kind=kLoop, calls=%fused_computation.clone.1 | loop fusion | flops 524288 | bytes 1310726 | tf_op jit(solution)/shard_map/while/body/eval_jaxpr/jit(_where)/select_n | solution.py:18
  94.7 1.6 %add_select_fusion.2 = f32[32,64,64]{2,1,0:T(8,128)S(1)} fusion(f32[32,64,64]{2,1,0:T(8,128)S(1)} %get-tuple-element.142, bf16[16,32,64,64]{3,2,1,0:T(8,128)(2,1)} %get-tuple-element.150, s32[]{:T(128)} %get-tuple-element.141, pred[]{:T(512)S(6)} %compare.3, pred[]{:T(512)S(6)} %lt.21), kind=kLoop, calls=%fused_computation.clone.1 | loop fusion | flops 524288 | bytes 1310726 | tf_op jit(solution)/shard_map/while/body/eval_jaxpr/jit(_where)/select_n | solution.py:18
  96.3 1.6 %add_select_fusion.2 = f32[32,64,64]{2,1,0:T(8,128)S(1)} fusion(f32[32,64,64]{2,1,0:T(8,128)S(1)} %get-tuple-element.142, bf16[16,32,64,64]{3,2,1,0:T(8,128)(2,1)} %get-tuple-element.150, s32[]{:T(128)} %get-tuple-element.141, pred[]{:T(512)S(6)} %compare.3, pred[]{:T(512)S(6)} %lt.21), kind=kLoop, calls=%fused_computation.clone.1 | loop fusion | flops 524288 | bytes 1310726 | tf_op jit(solution)/shard_map/while/body/eval_jaxpr/jit(_where)/select_n | solution.py:18
  98.0 1.6 %add_select_fusion.2 = f32[32,64,64]{2,1,0:T(8,128)S(1)} fusion(f32[32,64,64]{2,1,0:T(8,128)S(1)} %get-tuple-element.142, bf16[16,32,64,64]{3,2,1,0:T(8,128)(2,1)} %get-tuple-element.150, s32[]{:T(128)} %get-tuple-element.141, pred[]{:T(512)S(6)} %compare.3, pred[]{:T(512)S(6)} %lt.21), kind=kLoop, calls=%fused_computation.clone.1 | loop fusion | flops 524288 | bytes 1310726 | tf_op jit(solution)/shard_map/while/body/eval_jaxpr/jit(_where)/select_n | solution.py:18
  99.6 1.6 %add_select_fusion.2 = f32[32,64,64]{2,1,0:T(8,128)S(1)} fusion(f32[32,64,64]{2,1,0:T(8,128)S(1)} %get-tuple-element.142, bf16[16,32,64,64]{3,2,1,0:T(8,128)(2,1)} %get-tuple-element.150, s32[]{:T(128)} %get-tuple-element.141, pred[]{:T(512)S(6)} %compare.3, pred[]{:T(512)S(6)} %lt.21), kind=kLoop, calls=%fused_computation.clone.1 | loop fusion | flops 524288 | bytes 1310726 | tf_op jit(solution)/shard_map/while/body/eval_jaxpr/jit(_where)/select_n | solution.py:18
  101.2 1.6 %add_select_fusion.2 = f32[32,64,64]{2,1,0:T(8,128)S(1)} fusion(f32[32,64,64]{2,1,0:T(8,128)S(1)} %get-tuple-element.142, bf16[16,32,64,64]{3,2,1,0:T(8,128)(2,1)} %get-tuple-element.150, s32[]{:T(128)} %get-tuple-element.141, pred[]{:T(512)S(6)} %compare.3, pred[]{:T(512)S(6)} %lt.21), kind=kLoop, calls=%fused_computation.clone.1 | loop fusion | flops 524288 | bytes 1310726 | tf_op jit(solution)/shard_map/while/body/eval_jaxpr/jit(_where)/select_n | solution.py:18
  102.9 1.6 %add_select_fusion.2 = f32[32,64,64]{2,1,0:T(8,128)S(1)} fusion(f32[32,64,64]{2,1,0:T(8,128)S(1)} %get-tuple-element.142, bf16[16,32,64,64]{3,2,1,0:T(8,128)(2,1)} %get-tuple-element.150, s32[]{:T(128)} %get-tuple-element.141, pred[]{:T(512)S(6)} %compare.3, pred[]{:T(512)S(6)} %lt.21), kind=kLoop, calls=%fused_computation.clone.1 | loop fusion | flops 524288 | bytes 1310726 | tf_op jit(solution)/shard_map/while/body/eval_jaxpr/jit(_where)/select_n | solution.py:18
  104.5 1.6 %add_select_fusion.2 = f32[32,64,64]{2,1,0:T(8,128)S(1)} fusion(f32[32,64,64]{2,1,0:T(8,128)S(1)} %get-tuple-element.142, bf16[16,32,64,64]{3,2,1,0:T(8,128)(2,1)} %get-tuple-element.150, s32[]{:T(128)} %get-tuple-element.141, pred[]{:T(512)S(6)} %compare.3, pred[]{:T(512)S(6)} %lt.21), kind=kLoop, calls=%fused_computation.clone.1 | loop fusion | flops 524288 | bytes 1310726 | tf_op jit(solution)/shard_map/while/body/eval_jaxpr/jit(_where)/select_n | solution.py:18
  106.1 1.6 %add_select_fusion.2 = f32[32,64,64]{2,1,0:T(8,128)S(1)} fusion(f32[32,64,64]{2,1,0:T(8,128)S(1)} %get-tuple-element.142, bf16[16,32,64,64]{3,2,1,0:T(8,128)(2,1)} %get-tuple-element.150, s32[]{:T(128)} %get-tuple-element.141, pred[]{:T(512)S(6)} %compare.3, pred[]{:T(512)S(6)} %lt.21), kind=kLoop, calls=%fused_computation.clone.1 | loop fusion | flops 524288 | bytes 1310726 | tf_op jit(solution)/shard_map/while/body/eval_jaxpr/jit(_where)/select_n | solution.py:18
  107.8 1.6 %add_select_fusion.2 = f32[32,64,64]{2,1,0:T(8,128)S(1)} fusion(f32[32,64,64]{2,1,0:T(8,128)S(1)} %get-tuple-element.142, bf16[16,32,64,64]{3,2,1,0:T(8,128)(2,1)} %get-tuple-element.150, s32[]{:T(128)} %get-tuple-element.141, pred[]{:T(512)S(6)} %compare.3, pred[]{:T(512)S(6)} %lt.21), kind=kLoop, calls=%fused_computation.clone.1 | loop fusion | flops 524288 | bytes 1310726 | tf_op jit(solution)/shard_map/while/body/eval_jaxpr/jit(_where)/select_n | solution.py:18
  109.4 1.6 %add_select_fusion.2 = f32[32,64,64]{2,1,0:T(8,128)S(1)} fusion(f32[32,64,64]{2,1,0:T(8,128)S(1)} %get-tuple-element.142, bf16[16,32,64,64]{3,2,1,0:T(8,128)(2,1)} %get-tuple-element.150, s32[]{:T(128)} %get-tuple-element.141, pred[]{:T(512)S(6)} %compare.3, pred[]{:T(512)S(6)} %lt.21), kind=kLoop, calls=%fused_computation.clone.1 | loop fusion | flops 524288 | bytes 1310726 | tf_op jit(solution)/shard_map/while/body/eval_jaxpr/jit(_where)/select_n | solution.py:18
  111.0 1.6 %add_select_fusion.2 = f32[32,64,64]{2,1,0:T(8,128)S(1)} fusion(f32[32,64,64]{2,1,0:T(8,128)S(1)} %get-tuple-element.142, bf16[16,32,64,64]{3,2,1,0:T(8,128)(2,1)} %get-tuple-element.150, s32[]{:T(128)} %get-tuple-element.141, pred[]{:T(512)S(6)} %compare.3, pred[]{:T(512)S(6)} %lt.21), kind=kLoop, calls=%fused_computation.clone.1 | loop fusion | flops 524288 | bytes 1310726 | tf_op jit(solution)/shard_map/while/body/eval_jaxpr/jit(_where)/select_n | solution.py:18
  112.7 1.6 %add_select_fusion.2 = f32[32,64,64]{2,1,0:T(8,128)S(1)} fusion(f32[32,64,64]{2,1,0:T(8,128)S(1)} %get-tuple-element.142, bf16[16,32,64,64]{3,2,1,0:T(8,128)(2,1)} %get-tuple-element.150, s32[]{:T(128)} %get-tuple-element.141, pred[]{:T(512)S(6)} %compare.3, pred[]{:T(512)S(6)} %lt.21), kind=kLoop, calls=%fused_computation.clone.1 | loop fusion | flops 524288 | bytes 1310726 | tf_op jit(solution)/shard_map/while/body/eval_jaxpr/jit(_where)/select_n | solution.py:18
  114.3 0.0 copy-done.1
  114.3 0.0 copy-done.2
  114.3 0.0 copy-done.3
  114.3 1.7 %multiply_reduce_fusion = (f32[256,32]{0,1:T(8,128)S(1)}, f32[256,32,64]{0,2,1:T(8,128)S(1)}) fusion(f32[256,8,64]{0,2,1:T(8,128)S(1)} %copy-done.2, f32[256,8,64]{0,2,1:T(8,128)S(1)} %copy-done.3, f32[256,8,64]{0,2,1:T(8,128)} %convolution_bitcast_fusion.2, f32[256,8,64]{0,2,1:T(8,128)} %convolution_bitcast_fusion.3, bf16[256,32,64]{0,2,1:T(8,128)(2,1)S(1)} %bitcast.46, ...), kind=kOutput, calls=%fused_computation.3 | convolution fusion | flops 70377472 | bytes 5799936 | tf_op jit(solution)/shard_map/thd,hde->the/dot_general | solution.py:36
  116.1 0.3 broadcast_multiply_fusion
  116.4 0.0 copy-start.4
  116.4 1.9 %copy.19 = f32[256,2048]{1,0:T(8,128)} copy(f32[256,2048]{0,1:T(8,128)S(1)} %bitcast.36) | data formatting | bytes 4194304 | tf_op jit(solution)/shard_map/reshape | solution.py:53
  118.2 0.0 copy-done.4
  118.2 2.8 %multiply_convert_fusion = bf16[256,2048]{1,0:T(8,128)(2,1)} fusion(f32[256,2048]{1,0:T(8,128)} %copy.19, f32[2048]{0:T(1024)S(1)} %copy-done.4), kind=kLoop, calls=%fused_computation.2 | loop fusion | flops 1048576 | bytes 3153920 | tf_op jit(solution)/shard_map/convert_element_type | solution.py:54
  (3 shorter events, 0.0 us)
Async XLA Ops:
  6.5 81.5 %all-gather.3.cloned.1.call-start = ((), (), s32[]{:S(2)}) async-start(), calls=%async_computation | async-start | bytes 8912896 | tf_op jit(solution)/shard_map/all_gather | solution.py:12
  14.5 5.3 %copy-start = (bf16[256,2048]{0,1:T(8,128)(2,1)}, bf16[256,2048]{0,1:T(8,128)(2,1)S(1)}, u32[]{:S(2)}) copy-start(bf16[256,2048]{0,1:T(8,128)(2,1)S(1)} %broadcast_maximum_fusion) | copy-start | bytes 3145732
  88.0 26.2 %copy-start.1 = (bf16[256,2048]{0,1:T(8,128)(2,1)S(1)}, bf16[256,2048]{0,1:T(8,128)(2,1)}, u32[]{:S(2)}) copy-start(bf16[256,2048]{0,1:T(8,128)(2,1)} %copy-done) | copy-start | bytes 3145732
  88.0 26.2 %copy-start.2 = (f32[256,8,64]{0,2,1:T(8,128)S(1)}, f32[256,8,64]{0,2,1:T(8,128)}, u32[]{:S(2)}) copy-start(f32[256,8,64]{0,2,1:T(8,128)} %convolution_bitcast_fusion) | copy-start | bytes 1572868
  88.0 26.2 %copy-start.3 = (f32[256,8,64]{0,2,1:T(8,128)S(1)}, f32[256,8,64]{0,2,1:T(8,128)}, u32[]{:S(2)}) copy-start(f32[256,8,64]{0,2,1:T(8,128)} %convolution_bitcast_fusion.1) | copy-start | bytes 1572868
  116.4 1.9 %copy-start.4 = (f32[2048]{0:T(1024)S(1)}, f32[2048]{0:T(1024)}, u32[]{:S(2)}) copy-start(f32[2048]{0:T(1024)} %param.9) | copy-start | bytes 24580
Sparse Core Ops, SparseCore 0:
  11.0 77.0 all-gather.2
where the time goes:
time: 129 us; the launch traced here: 128 us
  waiting for transfers between devices  66.6 us (52%)
  other arithmetic  30.3 us (23%)
  between operations  13.5 us (10%)
  matrix products  9.9 us (8%)
  local copies, waits for them, and re-layouts  7.12 us (6%)
    all_gather x1, waiting for transfers between devices, entering(): everything = lax.all_gather(shard.astype(jnp.bfloat16), axis)  66.6 us
    select_n x16, other arithmetic, hop(): return jnp.where(reached, new, before)  25.9 us
    unnamed x13, local copies, waits for them, and re-layouts  5.24 us
    dot_general x4, matrix products, on_device(): jnp.einsum('hts,she->the', scores, v_grp, preferred_element_type=jnp.floa...  5.01 us
    convert_element_type x1, other arithmetic, on_device(): return normed.astype(jnp.bfloat16)  2.75 us
  transfers between devices with their start and end apart: 1, of which 1 were waited for; matrix products, arithmetic and copies ran while one was open for 8% of the time, Pallas kernels for 0%

commit v1 on v0

v1 whole, which is shorter than its diff:
```python
import functools

import jax
import jax.numpy as jnp
from jax import lax
from jax.experimental import pallas as pl
from jax.experimental.pallas import tpu as pltpu
from jax.sharding import PartitionSpec as P


HEAD_DIM = 64
PAIR = 2 * HEAD_DIM
QUAD = 4 * HEAD_DIM
EPS = 1e-05
AXIS = "seq"


def swap_with(x, bit, size):
    return lax.ppermute(x, AXIS, [(i, i ^ bit) for i in range(size)])


def first_lanes(shape):
    return lax.broadcasted_iota(jnp.int32, shape, len(shape) - 1) % PAIR < HEAD_DIM


def dot(a, b, dims):
    return lax.dot_general(a, b, (dims, ((), ())), preferred_element_type=jnp.float32)


def state_kernel(k_hbm, v_hbm, send_ref, keep_ref, k_ref, v_ref, sems):
    half = k_ref.shape[1] // 2
    core = lax.axis_index(AXIS) % 2
    copies = []
    for step in range(2):
        which = 1 - core if step == 0 else core
        lanes = pl.ds(pl.multiple_of(which * half, half), half)
        here = pl.ds(step * half, half)
        pair = [
            pltpu.make_async_copy(src.at[:, lanes], dst.at[:, here], sems.at[step, n])
            for n, (src, dst) in enumerate(((k_hbm, k_ref), (v_hbm, v_ref)))
        ]
        for copy in pair:
            copy.start()
        copies.append(pair)
    first = first_lanes((HEAD_DIM, PAIR))
    for step in range(2):
        for copy in copies[step]:
            copy.wait()
        for quad in range(half // QUAD):
            lanes = pl.ds(step * half + quad * QUAD, QUAD)
            fk = jnp.maximum(k_ref[:, lanes], 0)
            full = dot(fk, v_ref[:, lanes], ((0,), (0,)))
            for p in range(2):
                at = p * PAIR
                rows = full[at : at + PAIR, at : at + PAIR]
                packed = jnp.where(first, rows[:HEAD_DIM], rows[HEAD_DIM:])
                to = pl.ds((quad * 2 + p) * HEAD_DIM, HEAD_DIM)
                if step == 0:
                    send_ref[to, :] = packed.astype(jnp.bfloat16)
                else:
                    keep_ref[to, :] = packed


def intra_kernel(q_hbm, k_ref, v_ref, fq_ref, intra_ref, q_buf, sem, *, part):
    count, width = fq_ref.shape
    half = k_ref.shape[1] // 2
    core = lax.axis_index(AXIS) % 2
    which = 1 - core if part < 2 else core
    start = pl.multiple_of(which * half + (part % 2) * width, width)
    copy = pltpu.make_async_copy(q_hbm.at[:, pl.ds(start, width)], q_buf, sem)
    copy.start()
    copy.wait()
    mid = count // 2
    first = first_lanes((count, PAIR))
    rows = lax.broadcasted_iota(jnp.int32, (mid, mid), 0)
    cols = lax.broadcasted_iota(jnp.int32, (mid, mid), 1)
    causal = cols <= rows
    for p in range(width // PAIR):
        lanes = pl.ds(p * PAIR, PAIR)
        there = pl.ds(part * width + p * PAIR, PAIR)
        fq = jnp.maximum(q_buf[:, lanes], 0)
        fq_ref[:, lanes] = fq
        fk = jnp.maximum(k_ref[:, there], 0)
        val = v_ref[:, there]
        zero = jnp.zeros_like(fq)
        top, low, weights = [], [], []
        for h in range(2):
            mine = first if h == 0 else jnp.logical_not(first)
            mine_q = jnp.where(mine, fq, zero)
            s_top = dot(mine_q[:mid], fk[:mid], ((1,), (1,)))
            s_low = dot(mine_q[mid:], fk, ((1,), (1,)))
            s_top = jnp.where(causal, s_top, 0.0).astype(jnp.bfloat16)
            s_diag = jnp.where(causal, s_low[:, mid:], 0.0).astype(jnp.bfloat16)
            s_low = jnp.concatenate([s_low[:, :mid].astype(jnp.bfloat16), s_diag], axis=1)
            mine_v = jnp.where(mine, val, zero)
            top.append(s_top)
            low.append(s_low)
            weights.append(mine_v)
        w_top = jnp.concatenate([w[:mid] for w in weights], axis=0)
        intra_ref[:mid, lanes] = dot(jnp.concatenate(top, axis=1), w_top, ((1,), (0,)))
        w_low = jnp.concatenate(weights, axis=0)
        intra_ref[mid:, lanes] = dot(jnp.concatenate(low, axis=1), w_low, ((1,), (0,)))


def final_kernel(prior_ref, fq0, fq1, in0, in1, gain_ref, *rest, step):
    out_hbm, out_buf, sems = rest[-3:]
    half = out_buf.shape[1]
    width = fq0.shape[1]
    core = lax.axis_index(AXIS) % 2
    which = core if step == 0 else 1 - core
    base = pl.multiple_of(which * half, half)
    lane = lax.broadcasted_iota(jnp.int32, (QUAD, QUAD), 1) // HEAD_DIM
    row = lax.broadcasted_iota(jnp.int32, (QUAD, QUAD), 0) // HEAD_DIM
    same = lane == row
    ones = jnp.where(same, 1.0 / HEAD_DIM, 0.0).astype(jnp.bfloat16)
    copies = []
    for quad in range(half // QUAD):
        fq_ref, intra_ref = (fq0, in0) if quad * QUAD < width else (fq1, in1)
        lanes = pl.ds(quad * QUAD % width, QUAD)
        one = prior_ref[pl.ds(quad * PAIR, HEAD_DIM), :]
        two = prior_ref[pl.ds(quad * PAIR + HEAD_DIM, HEAD_DIM), :]
        wide = jnp.concatenate([one, two], axis=1)
        block = jnp.concatenate([wide] * 4, axis=0)
        block = jnp.where(same, block, jnp.zeros_like(block))
        numer = dot(fq_ref[:, lanes], block, ((1,), (0,))) + intra_ref[:, lanes]
        square = (numer * numer).astype(jnp.bfloat16)
        mean_sq = dot(square, ones, ((1,), (0,)))
        gain = gain_ref[:, pl.ds(pl.multiple_of(base + quad * QUAD, QUAD), QUAD)]
        normed = numer * lax.rsqrt(mean_sq + EPS) * gain
        out_buf[:, pl.ds(quad * QUAD, QUAD)] = normed.astype(jnp.bfloat16)
        copy = pltpu.make_async_copy(
            out_buf.at[:, pl.ds(quad * QUAD, QUAD)],
            out_hbm.at[:, pl.ds(pl.multiple_of(base + quad * QUAD, QUAD), QUAD)],
            sems.at[quad],
        )
        copy.start()
        copies.append(copy)
    for copy in copies:
        copy.wait()


ANY = pl.BlockSpec(memory_space=pl.ANY)
VMEM = pl.BlockSpec(memory_space=pltpu.VMEM)


def on_device(queries, keys, values, gain, *, size):
    count, width = queries.shape
    half, part = width // 2, width // 4
    rows = half // PAIR * HEAD_DIM
    bf16, f32 = jnp.bfloat16, jnp.float32
    here = lax.axis_index(AXIS)

    stay = lambda x: pltpu.with_memory_space_constraint(x, pltpu.VMEM)
    send, keep, k_vmem, v_vmem = pl.pallas_call(
        state_kernel,
        out_shape=(
            pltpu.VMEM((rows, PAIR), bf16),
            pltpu.VMEM((rows, PAIR), f32),
            pltpu.VMEM((count, width), bf16),
            pltpu.VMEM((count, width), bf16),
        ),
        in_specs=[ANY, ANY],
        out_specs=(VMEM, VMEM, VMEM, VMEM),
        scratch_shapes=[pltpu.SemaphoreType.DMA((2, 2))],
        name="state",
    )(keys, values)

    parts = []
    for n in range(4):
      parts.append(
          pl.pallas_call(
              functools.partial(intra_kernel, part=n),
              out_shape=(pltpu.VMEM((count, part), bf16), pltpu.VMEM((count, part), f32)),
              in_specs=[ANY, VMEM, VMEM],
              out_specs=(VMEM, VMEM),
              scratch_shapes=[pltpu.VMEM((count, part), bf16), pltpu.SemaphoreType.DMA],
              cost_estimate=pl.CostEstimate(flops=150_000_000, transcendentals=0, bytes_accessed=1_500_000),
          )(queries, stay(k_vmem), stay(v_vmem))
      )

    core, side = here % 2, here // 2 % 2
    got_core = swap_with(send, 1, size).astype(f32)
    chip = keep + got_core
    q_rows = rows // 2
    low, high = chip[:q_rows], chip[q_rows:]
    own = jnp.where(side == 0, low, high)
    other = jnp.where(side == 0, high, low)
    got_side = swap_with(other.astype(bf16), 2, size).astype(f32)
    total = own + got_side
    before = jnp.zeros_like(total)
    bit = 4
    while bit < size:
        got = swap_with(total.astype(bf16), bit, size).astype(f32)
        before = before + jnp.where(here // bit % 2 == 1, got, 0.0)
        total = total + got
        bit *= 2
    to_side = before + jnp.where(side == 0, own, 0.0)
    mine = before + jnp.where(side == 0, 0.0, got_side)
    got_base = swap_with(to_side.astype(bf16), 2, size).astype(f32)
    base = jnp.concatenate([jnp.where(side == 0, mine, got_base), jnp.where(side == 0, got_base, mine)], axis=0)
    to_core = base + jnp.where(core == 0, keep, 0.0)
    mine = (base + jnp.where(core == 0, 0.0, got_core)).astype(bf16)
    theirs = swap_with(to_core.astype(bf16), 1, size)

    gain2 = gain[None, :]
    out = None
    for step, prior in ((0, mine), (1, theirs)):
        (fq0, in0), (fq1, in1) = parts[2:] if step == 0 else parts[:2]
        args = [stay(prior), stay(fq0), stay(fq1), stay(in0), stay(in1), gain2]
        specs = [VMEM] * 6
        alias = {}
        if out is not None:
            args.append(out)
            specs.append(ANY)
            alias = {6: 0}
        out = pl.pallas_call(
            functools.partial(final_kernel, step=step),
            out_shape=jax.ShapeDtypeStruct((count, width), bf16),
            in_specs=specs,
            out_specs=ANY,
            scratch_shapes=[pltpu.VMEM((count, half), bf16), pltpu.SemaphoreType.DMA((half // QUAD,))],
            input_output_aliases=alias,
            cost_estimate=pl.CostEstimate(flops=100_000_000, transcendentals=0, bytes_accessed=2_000_000),
        )(*args)
    return out


def solution(mesh):
    return jax.shard_map(
        functools.partial(on_device, size=mesh.shape[AXIS]),
        mesh=mesh,
        in_specs=(
            P(("groups", "seq"), None),
            P(("groups", "seq"), None),
            P(("groups", "seq"), None),
            P(),
        ),
        out_specs=P(("groups", "seq"), None),
        check_vma=False,
    )
```

time: 129 us -> 44.2 us (0.34)
  waiting for transfers between devices: 66.6 us -> 10.4 us
  other arithmetic: 30.3 us -> 0.9 us
  Pallas kernels: 0 us -> 13.9 us
  between operations: 13.5 us -> 0.17 us
  starting transfers between devices: 0.01 us -> 10.4 us
  matrix products: 9.9 us -> 0 us
    all_gather x1 -> x0, waiting for transfers between devices: 66.6 us -> none  [entering(): everything = lax.all_gather(shard.astype(jnp.bfloat16), axis)]
    select_n x16 -> x1, other arithmetic: 25.9 us -> 0.05 us  [on_device(): jnp.where(side == 0, mine, got_base)]
    pallas_call x0 -> x7, Pallas kernels: none -> 13.9 us  [the longest x4 7.77 us: on_device(): pl.pallas_call(functools.partial(intra_kernel, part=n), out_shape=(pltpu....]
    ppermute x0 -> x6, waiting for transfers between devices: none -> 10.4 us  [swap_with(): return lax.ppermute(x, AXIS, [(i, i ^ bit) for i in range(size)])]
    ppermute x0 -> x6, starting transfers between devices: none -> 10.4 us  [swap_with(): return lax.ppermute(x, AXIS, [(i, i ^ bit) for i in range(size)])]
    dot_general x10 -> x0, matrix products: 9.9 us -> none  [the longest x4 5.01 us: on_device(): jnp.einsum('hts,she->the', scores, v_grp, preferred_element_type=jnp.floa...]
    unnamed x13 -> x28, local copies, waits for them, and re-layouts: 5.24 us -> 7.86 us
    convert_element_type x1 -> x5, other arithmetic: 2.75 us -> 0.82 us  [the longest x1 0.72 us: on_device(): mine = (base + jnp.where(core == 0, 0.0, got_core)).astype(bf16)]
  transfers between devices with their start and end apart: 1 -> 6, of which waited for: 1 -> 5; matrix products, arithmetic and copies ran while one was open for 8% -> 0% of each run, Pallas kernels for 0% -> 22%
where the time goes in v1:
time: 44.2 us; the launch traced here: 43.6 us
  Pallas kernels  13.9 us (31%)
  starting transfers between devices  10.4 us (24%)
  waiting for transfers between devices  10.4 us (24%)
  local copies, waits for them, and re-layouts  7.86 us (18%)
  other arithmetic  0.9 us (2%)
    ppermute x6, waiting for transfers between devices, swap_with(): return lax.ppermute(x, AXIS, [(i, i ^ bit) for i in range(size)])  10.4 us
    ppermute x6, starting transfers between devices, swap_with(): return lax.ppermute(x, AXIS, [(i, i ^ bit) for i in range(size)])  10.4 us
    unnamed x28, local copies, waits for them, and re-layouts  7.86 us
    pallas_call x4, Pallas kernels, on_device(): pl.pallas_call(functools.partial(intra_kernel, part=n), out_shape=(pltpu....  7.77 us
    pallas_call x2, Pallas kernels, on_device(): pl.pallas_call(functools.partial(final_kernel, step=step), out_shape=jax....  4.19 us
    pallas_call x1, Pallas kernels, on_device(): pl.pallas_call(state_kernel, out_shape=(pltpu.VMEM((rows, PAIR), bf16), p...  1.94 us
  transfers between devices with their start and end apart: 6, of which 5 were waited for; matrix products, arithmetic and copies ran while one was open for 0% of the time, Pallas kernels for 22%

profile of v1, /device:TPU:0, one launch (start us, length us, event | category | flops | bytes accessed | tf_op | source)
XLA Modules:
  0.0 43.6 jit_solution(5439777367955684819)
XLA Ops:
  0.0 1.9 %state.1 = (bf16[512,128]{1,0:T(8,128)(2,1)S(1)}, f32[512,128]{1,0:T(8,128)S(1)}, bf16[256,2048]{1,0:T(8,128)(2,1)S(1)}, bf16[256,2048]{1,0:T(8,128)(2,1)S(1)}) custom-call(bf16[256,2048]{1,0:T(8,128)(2,1)} %k_hbm.1, bf16[256,2048]{1,0:T(8,128)(2,1)} %v_hbm.1), custom_call_target="tpu_custom_call" | custom-call | tf_op jit(solution)/shard_map/state/pallas_call | solution.py:154
  1.9 0.0 copy-start
  2.0 0.0 copy-start.2
  2.0 0.6 %collective-permute-start = (bf16[512,128]{1,0:T(8,128)(2,1)S(1)}, bf16[512,128]{1,0:T(8,128)(2,1)S(1)}, u32[]{:S(2)}, u32[]{:S(2)}) collective-permute-start(bf16[512,128]{1,0:T(8,128)(2,1)S(1)} %get-tuple-element.18), channel_id=1, source_target_pairs={{0,1},{1,0},{2,3},{3,2},{4,5},{5,4},{6,7},{7,6},{8,9},{9,8},{10,11... | collective-permute-start | bytes 393224 | tf_op jit(solution)/shard_map/ppermute | solution.py:19
  2.5 1.0 %collective-permute-done = bf16[512,128]{1,0:T(8,128)(2,1)S(1)} collective-permute-done((bf16[512,128]{1,0:T(8,128)(2,1)S(1)}, bf16[512,128]{1,0:T(8,128)(2,1)S(1)}, u32[]{:S(2)}, u32[]{:S(2)}) %collective-permute-start) | collective-permute-done | bytes 131104 | tf_op jit(solution)/shard_map/ppermute | solution.py:19
  3.6 2.9 %collective-permute-start.1 = (bf16[256,128]{1,0:T(8,128)(2,1)S(1)}, bf16[256,128]{1,0:T(8,128)(2,1)S(1)}, u32[]{:S(2)}, u32[]{:S(2)}) collective-permute-start(bf16[256,128]{1,0:T(8,128)(2,1)S(1)} %select_convert_fusion), channel_id=1, source_target_pairs={{0,2},{1,3},{2,0},{3,1},{4,6},{5,7},{6,4},{7,5},{8,10},{9,11},{10,... | collective-permute-start | bytes 196616 | tf_op jit(solution)/shard_map/ppermute | solution.py:19
  6.5 2.4 %collective-permute-done.1 = bf16[256,128]{1,0:T(8,128)(2,1)S(1)} collective-permute-done((bf16[256,128]{1,0:T(8,128)(2,1)S(1)}, bf16[256,128]{1,0:T(8,128)(2,1)S(1)}, u32[]{:S(2)}, u32[]{:S(2)}) %collective-permute-start.1) | collective-permute-done | bytes 65568 | tf_op jit(solution)/shard_map/ppermute | solution.py:19
  8.9 2.0 %collective-permute-start.2 = (bf16[256,128]{1,0:T(8,128)(2,1)S(1)}, bf16[256,128]{1,0:T(8,128)(2,1)S(1)}, u32[]{:S(2)}, u32[]{:S(2)}) collective-permute-start(bf16[256,128]{1,0:T(8,128)(2,1)S(1)} %get-tuple-element.29), channel_id=1, source_target_pairs={{0,4},{1,5},{2,6},{3,7},{4,0},{5,1},{6,2},{7,3},{8,12},{9,13},{10,... | collective-permute-start | bytes 196616 | tf_op jit(solution)/shard_map/ppermute | solution.py:19
  10.9 2.4 %collective-permute-done.2 = bf16[256,128]{1,0:T(8,128)(2,1)S(1)} collective-permute-done((bf16[256,128]{1,0:T(8,128)(2,1)S(1)}, bf16[256,128]{1,0:T(8,128)(2,1)S(1)}, u32[]{:S(2)}, u32[]{:S(2)}) %collective-permute-start.2) | collective-permute-done | bytes 65568 | tf_op jit(solution)/shard_map/ppermute | solution.py:19
  13.3 3.0 %collective-permute-start.3 = (bf16[256,128]{1,0:T(8,128)(2,1)S(1)}, bf16[256,128]{1,0:T(8,128)(2,1)S(1)}, u32[]{:S(2)}, u32[]{:S(2)}) collective-permute-start(bf16[256,128]{1,0:T(8,128)(2,1)S(1)} %fusion.4), channel_id=1, source_target_pairs={{0,8},{1,9},{2,10},{3,11},{4,12},{5,13},{6,14},{7,15},{8,0},{9,1},... | collective-permute-start | bytes 196616 | tf_op jit(solution)/shard_map/ppermute | solution.py:19
  16.3 2.2 %collective-permute-done.3 = bf16[256,128]{1,0:T(8,128)(2,1)S(1)} collective-permute-done((bf16[256,128]{1,0:T(8,128)(2,1)S(1)}, bf16[256,128]{1,0:T(8,128)(2,1)S(1)}, u32[]{:S(2)}, u32[]{:S(2)}) %collective-permute-start.3) | collective-permute-done | bytes 65568 | tf_op jit(solution)/shard_map/ppermute | solution.py:19
  18.6 0.0 copy-done
  18.6 0.0 copy-done.2
  18.6 1.9 %collective-permute-start.4 = (bf16[256,128]{1,0:T(8,128)(2,1)S(1)}, bf16[256,128]{1,0:T(8,128)(2,1)S(1)}, u32[]{:S(2)}, u32[]{:S(2)}) collective-permute-start(bf16[256,128]{1,0:T(8,128)(2,1)S(1)} %add_convert_fusion.1), channel_id=1, source_target_pairs={{0,2},{1,3},{2,0},{3,1},{4,6},{5,7},{6,4},{7,5},{8,10},{9,11},{10,... | collective-permute-start | bytes 196616 | tf_op jit(solution)/shard_map/ppermute | solution.py:19
  20.5 0.0 copy-start.1
  20.5 2.4 %collective-permute-done.4 = bf16[256,128]{1,0:T(8,128)(2,1)S(1)} collective-permute-done((bf16[256,128]{1,0:T(8,128)(2,1)S(1)}, bf16[256,128]{1,0:T(8,128)(2,1)S(1)}, u32[]{:S(2)}, u32[]{:S(2)}) %collective-permute-start.4) | collective-permute-done | bytes 65568 | tf_op jit(solution)/shard_map/ppermute | solution.py:19
  22.9 0.1 convert_select_fusion.2
  23.0 0.7 %fusion.1 = (bf16[512,128]{1,0:T(8,128)(2,1)S(1)}, bf16[512,128]{1,0:T(8,128)(2,1)}) fusion(bf16[512,128]{1,0:T(8,128)(2,1)S(1)} %collective-permute-done, f32[256,128]{1,0:T(8,128)S(1)} %get-tuple-element.34, f32[256,128]{1,0:T(8,128)S(1)} %get-tuple-element.33, pred[]{:T(512)S(6)} %eq.26, f32[512,128]{1,0:T(8,128)S(1)} %get-tuple-element.17), kind=kLoop, calls=%fused_computation.3 | loop fusion | flops 524288 | bytes 917505 | tf_op jit(solution)/shard_map/convert_element_type | solution.py:202
  23.7 0.0 collective-permute-start.5
  23.7 0.0 copy-done.1
  23.7 0.0 copy-start.3
  23.7 1.2 %copy-done.3 = bf16[256,2048]{1,0:T(8,128)(2,1)S(1)} copy-done((bf16[256,2048]{1,0:T(8,128)(2,1)S(1)}, bf16[256,2048]{1,0:T(8,128)(2,1)}, u32[]{:S(2)}) %copy-start.3) | copy-done | bytes 1048600
  24.9 1.9 %shard_map.49 = (bf16[256,512]{1,0:T(8,128)(2,1)S(1)}, f32[256,512]{1,0:T(8,128)S(1)}) custom-call(bf16[256,2048]{1,0:T(8,128)(2,1)} %q_hbm.7, bf16[256,2048]{1,0:T(8,128)(2,1)S(1)} %copy-done.1, bf16[256,2048]{1,0:T(8,128)(2,1)S(1)} %copy-done.3), custom_call_target="tpu_custom_call" | custom-call | flops 150000000 | bytes 1500000 | tf_op jit(solution)/shard_map/pallas_call | solution.py:171
  26.9 0.0 copy-start.8
  26.9 0.7 %copy-done.8 = bf16[256,512]{1,0:T(8,128)(2,1)} copy-done((bf16[256,512]{1,0:T(8,128)(2,1)}, bf16[256,512]{1,0:T(8,128)(2,1)S(1)}, u32[]{:S(2)}) %copy-start.8) | copy-done | bytes 262168
  27.6 1.9 %shard_map.48 = (bf16[256,512]{1,0:T(8,128)(2,1)S(1)}, f32[256,512]{1,0:T(8,128)S(1)}) custom-call(bf16[256,2048]{1,0:T(8,128)(2,1)} %q_hbm.7, bf16[256,2048]{1,0:T(8,128)(2,1)S(1)} %copy-done.1, bf16[256,2048]{1,0:T(8,128)(2,1)S(1)} %copy-done.3), custom_call_target="tpu_custom_call" | custom-call | flops 150000000 | bytes 1500000 | tf_op jit(solution)/shard_map/pallas_call | solution.py:171
  29.5 0.0 copy-start.4
  29.5 0.8 %copy-done.4 = f32[256,512]{1,0:T(8,128)} copy-done((f32[256,512]{1,0:T(8,128)}, f32[256,512]{1,0:T(8,128)S(1)}, u32[]{:S(2)}) %copy-start.4) | copy-done | bytes 524312
  30.3 0.0 copy-start.10
  30.3 0.7 %copy-done.10 = bf16[256,512]{1,0:T(8,128)(2,1)} copy-done((bf16[256,512]{1,0:T(8,128)(2,1)}, bf16[256,512]{1,0:T(8,128)(2,1)S(1)}, u32[]{:S(2)}) %copy-start.10) | copy-done | bytes 262168
  31.0 1.9 %shard_map.47 = (bf16[256,512]{1,0:T(8,128)(2,1)S(1)}, f32[256,512]{1,0:T(8,128)S(1)}) custom-call(bf16[256,2048]{1,0:T(8,128)(2,1)} %q_hbm.7, bf16[256,2048]{1,0:T(8,128)(2,1)S(1)} %copy-done.1, bf16[256,2048]{1,0:T(8,128)(2,1)S(1)} %copy-done.3), custom_call_target="tpu_custom_call" | custom-call | flops 150000000 | bytes 1500000 | tf_op jit(solution)/shard_map/pallas_call | solution.py:171
  33.0 0.0 copy-start.6
  33.0 0.8 %copy-done.6 = f32[256,512]{1,0:T(8,128)} copy-done((f32[256,512]{1,0:T(8,128)}, f32[256,512]{1,0:T(8,128)S(1)}, u32[]{:S(2)}) %copy-start.6) | copy-done | bytes 524312
  33.8 0.0 copy-start.12
  33.8 0.7 %copy-done.12 = bf16[256,512]{1,0:T(8,128)(2,1)} copy-done((bf16[256,512]{1,0:T(8,128)(2,1)}, bf16[256,512]{1,0:T(8,128)(2,1)S(1)}, u32[]{:S(2)}) %copy-start.12) | copy-done | bytes 262168
  34.5 1.9 %shard_map.46 = (bf16[256,512]{1,0:T(8,128)(2,1)S(1)}, f32[256,512]{1,0:T(8,128)S(1)}) custom-call(bf16[256,2048]{1,0:T(8,128)(2,1)} %q_hbm.7, bf16[256,2048]{1,0:T(8,128)(2,1)S(1)} %copy-done.1, bf16[256,2048]{1,0:T(8,128)(2,1)S(1)} %copy-done.3), custom_call_target="tpu_custom_call" | custom-call | flops 150000000 | bytes 1500000 | tf_op jit(solution)/shard_map/pallas_call | solution.py:171
  36.4 0.0 copy-start.5
  36.4 1.0 %copy-done.5 = f32[256,512]{1,0:T(8,128)S(1)} copy-done((f32[256,512]{1,0:T(8,128)S(1)}, f32[256,512]{1,0:T(8,128)}, u32[]{:S(2)}) %copy-start.5) | copy-done | bytes 524312
  37.5 0.0 copy-start.9
  37.5 0.9 %copy-done.9 = bf16[256,512]{1,0:T(8,128)(2,1)S(1)} copy-done((bf16[256,512]{1,0:T(8,128)(2,1)S(1)}, bf16[256,512]{1,0:T(8,128)(2,1)}, u32[]{:S(2)}) %copy-start.9) | copy-done | bytes 262168
  38.4 0.0 copy-start.11
  38.4 0.9 %copy-done.11 = bf16[256,512]{1,0:T(8,128)(2,1)S(1)} copy-done((bf16[256,512]{1,0:T(8,128)(2,1)S(1)}, bf16[256,512]{1,0:T(8,128)(2,1)}, u32[]{:S(2)}) %copy-start.11) | copy-done | bytes 262168
  39.4 0.0 copy-start.7
  39.4 0.0 copy-start.13
  39.4 2.0 %shard_map.50.rest_0_ = bf16[256,2048]{1,0:T(8,128)(2,1)} custom-call(bf16[512,128]{1,0:T(8,128)(2,1)S(1)} %get-tuple-element.31.prior_ref, bf16[256,512]{1,0:T(8,128)(2,1)S(1)} %copy-done.11, bf16[256,512]{1,0:T(8,128)(2,1)S(1)} %copy-done.9, f32[256,512]{1,0:T(8,128)S(1)} %copy-done.5, f32[256,512]{1,0:T(8,128)S(1)} %get-tuple-element.28.in1, ...), custom_call_target="tpu_custom_call" | custom-call | flops 100000000 | bytes 2000000 | tf_op jit(solution)/shard_map/pallas_call | solution.py:216
  41.4 0.0 collective-permute-done.5.prior_ref
  41.4 0.0 copy-done.7
  41.4 0.0 copy-done.13
  41.4 2.2 %shard_map.51 = bf16[256,2048]{1,0:T(8,128)(2,1)} custom-call(bf16[512,128]{1,0:T(8,128)(2,1)} %collective-permute-done.5.prior_ref, bf16[256,512]{1,0:T(8,128)(2,1)S(1)} %get-tuple-element.21.fq0, bf16[256,512]{1,0:T(8,128)(2,1)S(1)} %copy-done.13, f32[256,512]{1,0:T(8,128)S(1)} %get-tuple-element.23.in0, ...), custom_call_target="tpu_custom_call", output_to_operand_aliasing={{}: (6, {})} | custom-call | flops 100000000 | bytes 2000000 | tf_op jit(solution)/shard_map/pallas_call | solution.py:216
  (5 shorter events, 0.1 us)
Async XLA Ops:
  1.9 16.6 %copy-start = (bf16[256,2048]{1,0:T(8,128)(2,1)}, bf16[256,2048]{1,0:T(8,128)(2,1)S(1)}, u32[]{:S(2)}) copy-start(bf16[256,2048]{1,0:T(8,128)(2,1)S(1)} %get-tuple-element.19.k_ref) | copy-start | bytes 3145732
  2.0 16.6 %copy-start.2 = (bf16[256,2048]{1,0:T(8,128)(2,1)}, bf16[256,2048]{1,0:T(8,128)(2,1)S(1)}, u32[]{:S(2)}) copy-start(bf16[256,2048]{1,0:T(8,128)(2,1)S(1)} %get-tuple-element.20.v_ref) | copy-start | bytes 3145732
  2.0 1.5 %collective-permute-start = (bf16[512,128]{1,0:T(8,128)(2,1)S(1)}, bf16[512,128]{1,0:T(8,128)(2,1)S(1)}, u32[]{:S(2)}, u32[]{:S(2)}) collective-permute-start(bf16[512,128]{1,0:T(8,128)(2,1)S(1)} %get-tuple-element.18), channel_id=1, source_target_pairs={{0,1},{1,0},{2,3},{3,2},{4,5},{5,4},{6,7},{7,6},{8,9},{9,8},{10,11... | collective-permute-start | bytes 393224 | tf_op jit(solution)/shard_map/ppermute | solution.py:19
  3.6 5.3 %collective-permute-start.1 = (bf16[256,128]{1,0:T(8,128)(2,1)S(1)}, bf16[256,128]{1,0:T(8,128)(2,1)S(1)}, u32[]{:S(2)}, u32[]{:S(2)}) collective-permute-start(bf16[256,128]{1,0:T(8,128)(2,1)S(1)} %select_convert_fusion), channel_id=1, source_target_pairs={{0,2},{1,3},{2,0},{3,1},{4,6},{5,7},{6,4},{7,5},{8,10},{9,11},{10,... | collective-permute-start | bytes 196616 | tf_op jit(solution)/shard_map/ppermute | solution.py:19
  8.9 4.3 %collective-permute-start.2 = (bf16[256,128]{1,0:T(8,128)(2,1)S(1)}, bf16[256,128]{1,0:T(8,128)(2,1)S(1)}, u32[]{:S(2)}, u32[]{:S(2)}) collective-permute-start(bf16[256,128]{1,0:T(8,128)(2,1)S(1)} %get-tuple-element.29), channel_id=1, source_target_pairs={{0,4},{1,5},{2,6},{3,7},{4,0},{5,1},{6,2},{7,3},{8,12},{9,13},{10,... | collective-permute-start | bytes 196616 | tf_op jit(solution)/shard_map/ppermute | solution.py:19
  13.3 5.2 %collective-permute-start.3 = (bf16[256,128]{1,0:T(8,128)(2,1)S(1)}, bf16[256,128]{1,0:T(8,128)(2,1)S(1)}, u32[]{:S(2)}, u32[]{:S(2)}) collective-permute-start(bf16[256,128]{1,0:T(8,128)(2,1)S(1)} %fusion.4), channel_id=1, source_target_pairs={{0,8},{1,9},{2,10},{3,11},{4,12},{5,13},{6,14},{7,15},{8,0},{9,1},... | collective-permute-start | bytes 196616 | tf_op jit(solution)/shard_map/ppermute | solution.py:19
  18.6 4.3 %collective-permute-start.4 = (bf16[256,128]{1,0:T(8,128)(2,1)S(1)}, bf16[256,128]{1,0:T(8,128)(2,1)S(1)}, u32[]{:S(2)}, u32[]{:S(2)}) collective-permute-start(bf16[256,128]{1,0:T(8,128)(2,1)S(1)} %add_convert_fusion.1), channel_id=1, source_target_pairs={{0,2},{1,3},{2,0},{3,1},{4,6},{5,7},{6,4},{7,5},{8,10},{9,11},{10,... | collective-permute-start | bytes 196616 | tf_op jit(solution)/shard_map/ppermute | solution.py:19
  20.5 3.2 %copy-start.1 = (bf16[256,2048]{1,0:T(8,128)(2,1)S(1)}, bf16[256,2048]{1,0:T(8,128)(2,1)}, u32[]{:S(2)}) copy-start(bf16[256,2048]{1,0:T(8,128)(2,1)} %copy-done) | copy-start | bytes 3145732
  23.7 17.7 %collective-permute-start.5 = (bf16[512,128]{1,0:T(8,128)(2,1)}, bf16[512,128]{1,0:T(8,128)(2,1)}, u32[]{:S(2)}, u32[]{:S(2)}) collective-permute-start(bf16[512,128]{1,0:T(8,128)(2,1)} %get-tuple-element.32), channel_id=1, source_target_pairs={{0,1},{1,0},{2,3},{3,2},{4,5},{5,4},{6,7},{7,6},{8,9},{9,8},{10,11... | collective-permute-start | bytes 393224 | tf_op jit(solution)/shard_map/ppermute | solution.py:19
  23.7 1.2 %copy-start.3 = (bf16[256,2048]{1,0:T(8,128)(2,1)S(1)}, bf16[256,2048]{1,0:T(8,128)(2,1)}, u32[]{:S(2)}) copy-start(bf16[256,2048]{1,0:T(8,128)(2,1)} %copy-done.2) | copy-start | bytes 3145732
  26.9 0.7 %copy-start.8 = (bf16[256,512]{1,0:T(8,128)(2,1)}, bf16[256,512]{1,0:T(8,128)(2,1)S(1)}, u32[]{:S(2)}) copy-start(bf16[256,512]{1,0:T(8,128)(2,1)S(1)} %get-tuple-element.26.fq1) | copy-start | bytes 786436
  29.5 0.8 %copy-start.4 = (f32[256,512]{1,0:T(8,128)}, f32[256,512]{1,0:T(8,128)S(1)}, u32[]{:S(2)}) copy-start(f32[256,512]{1,0:T(8,128)S(1)} %get-tuple-element.27.in0) | copy-start | bytes 1572868
  30.3 0.7 %copy-start.10 = (bf16[256,512]{1,0:T(8,128)(2,1)}, bf16[256,512]{1,0:T(8,128)(2,1)S(1)}, u32[]{:S(2)}) copy-start(bf16[256,512]{1,0:T(8,128)(2,1)S(1)} %get-tuple-element.25.fq0) | copy-start | bytes 786436
  33.0 0.8 %copy-start.6 = (f32[256,512]{1,0:T(8,128)}, f32[256,512]{1,0:T(8,128)S(1)}, u32[]{:S(2)}) copy-start(f32[256,512]{1,0:T(8,128)S(1)} %get-tuple-element.24.in1) | copy-start | bytes 1572868
  33.8 0.7 %copy-start.12 = (bf16[256,512]{1,0:T(8,128)(2,1)}, bf16[256,512]{1,0:T(8,128)(2,1)S(1)}, u32[]{:S(2)}) copy-start(bf16[256,512]{1,0:T(8,128)(2,1)S(1)} %get-tuple-element.22.fq1) | copy-start | bytes 786436
  36.4 1.0 %copy-start.5 = (f32[256,512]{1,0:T(8,128)S(1)}, f32[256,512]{1,0:T(8,128)}, u32[]{:S(2)}) copy-start(f32[256,512]{1,0:T(8,128)} %copy-done.4) | copy-start | bytes 1572868
  37.5 0.9 %copy-start.9 = (bf16[256,512]{1,0:T(8,128)(2,1)S(1)}, bf16[256,512]{1,0:T(8,128)(2,1)}, u32[]{:S(2)}) copy-start(bf16[256,512]{1,0:T(8,128)(2,1)} %copy-done.8) | copy-start | bytes 786436
  38.4 0.9 %copy-start.11 = (bf16[256,512]{1,0:T(8,128)(2,1)S(1)}, bf16[256,512]{1,0:T(8,128)(2,1)}, u32[]{:S(2)}) copy-start(bf16[256,512]{1,0:T(8,128)(2,1)} %copy-done.10) | copy-start | bytes 786436
  39.4 2.0 %copy-start.7 = (f32[256,512]{1,0:T(8,128)S(1)}, f32[256,512]{1,0:T(8,128)}, u32[]{:S(2)}) copy-start(f32[256,512]{1,0:T(8,128)} %copy-done.6) | copy-start | bytes 1572868
  39.4 2.1 %copy-start.13 = (bf16[256,512]{1,0:T(8,128)(2,1)S(1)}, bf16[256,512]{1,0:T(8,128)(2,1)}, u32[]{:S(2)}) copy-start(bf16[256,512]{1,0:T(8,128)(2,1)} %copy-done.12) | copy-start | bytes 786436

commit v2 on v1

--- a/solution.py
+++ b/solution.py
@@ -61,15 +61,16 @@
                     keep_ref[to, :] = packed
 
 
-def intra_kernel(q_hbm, k_ref, v_ref, fq_ref, intra_ref, q_buf, sem, *, part):
-    count, width = fq_ref.shape
+def intra_kernel(q_hbm, k_ref, v_ref, out, q_buf, intra_ref, sems, *, part):
+    count, width = q_buf.shape
     half = k_ref.shape[1] // 2
     core = lax.axis_index(AXIS) % 2
     which = 1 - core if part < 2 else core
     start = pl.multiple_of(which * half + (part % 2) * width, width)
-    copy = pltpu.make_async_copy(q_hbm.at[:, pl.ds(start, width)], q_buf, sem)
+    copy = pltpu.make_async_copy(q_hbm.at[:, pl.ds(start, width)], q_buf, sems.at[0])
     copy.start()
     copy.wait()
+    copies = []
     mid = count // 2
     first = first_lanes((count, PAIR))
     rows = lax.broadcasted_iota(jnp.int32, (mid, mid), 0)
@@ -79,7 +80,6 @@
         lanes = pl.ds(p * PAIR, PAIR)
         there = pl.ds(part * width + p * PAIR, PAIR)
         fq = jnp.maximum(q_buf[:, lanes], 0)
-        fq_ref[:, lanes] = fq
         fk = jnp.maximum(k_ref[:, there], 0)
         val = v_ref[:, there]
         zero = jnp.zeros_like(fq)
@@ -100,45 +100,55 @@
         intra_ref[:mid, lanes] = dot(jnp.concatenate(top, axis=1), w_top, ((1,), (0,)))
         w_low = jnp.concatenate(weights, axis=0)
         intra_ref[mid:, lanes] = dot(jnp.concatenate(low, axis=1), w_low, ((1,), (0,)))
-
-
-def final_kernel(prior_ref, fq0, fq1, in0, in1, gain_ref, *rest, step):
-    out_hbm, out_buf, sems = rest[-3:]
+        copies.append(pltpu.make_async_copy(intra_ref.at[:, lanes], out.at[:, lanes], sems.at[p + 1]))
+        copies[-1].start()
+    for copy in copies:
+        copy.wait()
+
+
+def final_kernel(prior_ref, q_hbm, in0, in1, gain_ref, *rest, step):
+    out_hbm, q_buf, in_buf, out_buf, q_sem, in_sems, sems = rest[-7:]
     half = out_buf.shape[1]
-    width = fq0.shape[1]
+    width = half // 2
     core = lax.axis_index(AXIS) % 2
     which = core if step == 0 else 1 - core
     base = pl.multiple_of(which * half, half)
+    loads = [pltpu.make_async_copy(q_hbm.at[:, pl.ds(base, half)], q_buf, q_sem)]
+    for n, src in enumerate((in0, in1)):
+        loads.append(pltpu.make_async_copy(src, in_buf.at[:, pl.ds(n * width, width)], in_sems.at[n]))
+    for load in loads:
+        load.start()
     lane = lax.broadcasted_iota(jnp.int32, (QUAD, QUAD), 1) // HEAD_DIM
     row = lax.broadcasted_iota(jnp.int32, (QUAD, QUAD), 0) // HEAD_DIM
     same = lane == row
     ones = jnp.where(same, 1.0 / HEAD_DIM, 0.0).astype(jnp.bfloat16)
     copies = []
     for quad in range(half // QUAD):
-        fq_ref, intra_ref = (fq0, in0) if quad * QUAD < width else (fq1, in1)
-        lanes = pl.ds(quad * QUAD % width, QUAD)
+        lanes = pl.ds(quad * QUAD, QUAD)
         one = prior_ref[pl.ds(quad * PAIR, HEAD_DIM), :]
         two = prior_ref[pl.ds(quad * PAIR + HEAD_DIM, HEAD_DIM), :]
         wide = jnp.concatenate([one, two], axis=1)
         block = jnp.concatenate([wide] * 4, axis=0)
         block = jnp.where(same, block, jnp.zeros_like(block))
-        numer = dot(fq_ref[:, lanes], block, ((1,), (0,))) + intra_ref[:, lanes]
+        if quad == 0:
+            loads[0].wait()
+        fq = jnp.maximum(q_buf[:, lanes], 0)
+        if quad * QUAD % width == 0:
+            loads[1 + quad * QUAD // width].wait()
+        numer = dot(fq, block, ((1,), (0,))) + in_buf[:, lanes]
         square = (numer * numer).astype(jnp.bfloat16)
         mean_sq = dot(square, ones, ((1,), (0,)))
-        gain = gain_ref[:, pl.ds(pl.multiple_of(base + quad * QUAD, QUAD), QUAD)]
-        normed = numer * lax.rsqrt(mean_sq + EPS) * gain
-        out_buf[:, pl.ds(quad * QUAD, QUAD)] = normed.astype(jnp.bfloat16)
-        copy = pltpu.make_async_copy(
-            out_buf.at[:, pl.ds(quad * QUAD, QUAD)],
-            out_hbm.at[:, pl.ds(pl.multiple_of(base + quad * QUAD, QUAD), QUAD)],
-            sems.at[quad],
-        )
+        there = pl.ds(pl.multiple_of(base + quad * QUAD, QUAD), QUAD)
+        normed = numer * lax.rsqrt(mean_sq + EPS) * gain_ref[:, there]
+        out_buf[:, lanes] = normed.astype(jnp.bfloat16)
+        copy = pltpu.make_async_copy(out_buf.at[:, lanes], out_hbm.at[:, there], sems.at[quad])
         copy.start()
         copies.append(copy)
     for copy in copies:
         copy.wait()
 
 
+PARAMS = pltpu.CompilerParams(vmem_limit_bytes=12 * 2**20)
 ANY = pl.BlockSpec(memory_space=pl.ANY)
 VMEM = pl.BlockSpec(memory_space=pltpu.VMEM)
 
@@ -162,6 +172,7 @@
         in_specs=[ANY, ANY],
         out_specs=(VMEM, VMEM, VMEM, VMEM),
         scratch_shapes=[pltpu.SemaphoreType.DMA((2, 2))],
+        compiler_params=PARAMS,
         name="state",
     )(keys, values)
 
@@ -170,11 +181,16 @@
       parts.append(
           pl.pallas_call(
               functools.partial(intra_kernel, part=n),
-              out_shape=(pltpu.VMEM((count, part), bf16), pltpu.VMEM((count, part), f32)),
+              out_shape=jax.ShapeDtypeStruct((count, part), f32),
               in_specs=[ANY, VMEM, VMEM],
-              out_specs=(VMEM, VMEM),
-              scratch_shapes=[pltpu.VMEM((count, part), bf16), pltpu.SemaphoreType.DMA],
+              out_specs=ANY,
+              scratch_shapes=[
+                  pltpu.VMEM((count, part), bf16),
+                  pltpu.VMEM((count, part), f32),
+                  pltpu.SemaphoreType.DMA((1 + part // PAIR,)),
+              ],
               cost_estimate=pl.CostEstimate(flops=150_000_000, transcendentals=0, bytes_accessed=1_500_000),
+              compiler_params=PARAMS,
           )(queries, stay(k_vmem), stay(v_vmem))
       )
 
@@ -205,22 +221,29 @@
     gain2 = gain[None, :]
     out = None
     for step, prior in ((0, mine), (1, theirs)):
-        (fq0, in0), (fq1, in1) = parts[2:] if step == 0 else parts[:2]
-        args = [stay(prior), stay(fq0), stay(fq1), stay(in0), stay(in1), gain2]
-        specs = [VMEM] * 6
+        args = [prior, queries, *(parts[2:] if step == 0 else parts[:2]), gain2]
+        specs = [VMEM, ANY, ANY, ANY, VMEM]
         alias = {}
         if out is not None:
             args.append(out)
             specs.append(ANY)
-            alias = {6: 0}
+            alias = {5: 0}
         out = pl.pallas_call(
             functools.partial(final_kernel, step=step),
             out_shape=jax.ShapeDtypeStruct((count, width), bf16),
             in_specs=specs,
             out_specs=ANY,
-            scratch_shapes=[pltpu.VMEM((count, half), bf16), pltpu.SemaphoreType.DMA((half // QUAD,))],
+            scratch_shapes=[
+                pltpu.VMEM((count, half), bf16),
+                pltpu.VMEM((count, half), f32),
+                pltpu.VMEM((count, half), bf16),
+                pltpu.SemaphoreType.DMA,
+                pltpu.SemaphoreType.DMA((2,)),
+                pltpu.SemaphoreType.DMA((half // QUAD,)),
+            ],
             input_output_aliases=alias,
             cost_estimate=pl.CostEstimate(flops=100_000_000, transcendentals=0, bytes_accessed=2_000_000),
+            compiler_params=PARAMS,
         )(*args)
     return out
 

time: 44.2 us -> 39.3 us (0.89)
  local copies, waits for them, and re-layouts: 7.86 us -> 3.1 us
  Pallas kernels: 13.9 us -> 11.2 us
  other arithmetic: 0.9 us -> 3.27 us
  waiting for transfers between devices: 10.4 us -> 10.9 us
    unnamed x28 -> x16, local copies, waits for them, and re-layouts: 7.86 us -> 3.1 us
    convert_element_type x1, other arithmetic: 0.04 us -> 1.52 us  [on_device(): got_base = swap_with(to_side.astype(bf16), 2, size).astype(f32)]
    pallas_call x1, Pallas kernels: 1.94 us -> 0.89 us  [on_device(): pl.pallas_call(state_kernel, out_shape=(pltpu.VMEM((rows, PAIR), bf16), p...]
    pallas_call x4, Pallas kernels: 7.77 us -> 6.81 us  [on_device(): pl.pallas_call(functools.partial(intra_kernel, part=n), out_shape=jax.Sha...]
    select_n x1, other arithmetic: 0.05 us -> 0.95 us  [on_device(): jnp.where(side == 0, mine, got_base)]
    pallas_call x2, Pallas kernels: 4.19 us -> 3.51 us  [on_device(): pl.pallas_call(functools.partial(final_kernel, step=step), out_shape=jax....]
    convert_element_type x1, other arithmetic: 0.72 us -> 0.08 us  [on_device(): mine = (base + jnp.where(core == 0, 0.0, got_core)).astype(bf16)]
    convert_element_type x2, other arithmetic: 0.05 us -> 0.67 us  [on_device(): got = swap_with(total.astype(bf16), bit, size).astype(f32)]
where the time goes in v2:
time: 39.3 us; the launch traced here: 38.9 us
  Pallas kernels  11.2 us (28%)
  waiting for transfers between devices  10.9 us (28%)
  starting transfers between devices  10.3 us (26%)
  other arithmetic  3.27 us (8%)
  local copies, waits for them, and re-layouts  3.1 us (8%)
    ppermute x6, waiting for transfers between devices, swap_with(): return lax.ppermute(x, AXIS, [(i, i ^ bit) for i in range(size)])  10.9 us
    ppermute x6, starting transfers between devices, swap_with(): return lax.ppermute(x, AXIS, [(i, i ^ bit) for i in range(size)])  10.3 us
    pallas_call x4, Pallas kernels, on_device(): pl.pallas_call(functools.partial(intra_kernel, part=n), out_shape=jax.Sha...  6.81 us
    pallas_call x2, Pallas kernels, on_device(): pl.pallas_call(functools.partial(final_kernel, step=step), out_shape=jax....  3.51 us
    unnamed x16, local copies, waits for them, and re-layouts  3.1 us
    convert_element_type x1, other arithmetic, on_device(): got_base = swap_with(to_side.astype(bf16), 2, size).astype(f32)  1.52 us
    select_n x1, other arithmetic, on_device(): jnp.where(side == 0, mine, got_base)  0.95 us
    pallas_call x1, Pallas kernels, on_device(): pl.pallas_call(state_kernel, out_shape=(pltpu.VMEM((rows, PAIR), bf16), p...  0.89 us
  transfers between devices with their start and end apart: 6, of which 5 were waited for; matrix products, arithmetic and copies ran while one was open for 0% of the time, Pallas kernels for 22%

profile of v2, /device:TPU:0, one launch (start us, length us, event | category | flops | bytes accessed | tf_op | source)
XLA Modules:
  0.0 38.9 jit_solution(16949781685031182918)
XLA Ops:
  0.0 0.0 copy-start.1
  0.0 1.2 %copy-done.1 = bf16[256,2048]{1,0:T(8,128)(2,1)S(1)} copy-done((bf16[256,2048]{1,0:T(8,128)(2,1)S(1)}, bf16[256,2048]{1,0:T(8,128)(2,1)}, u32[]{:S(2)}) %copy-start.1) | copy-done | bytes 1048600
  1.2 0.0 copy-start.2
  1.2 1.2 %copy-done.2 = bf16[256,2048]{1,0:T(8,128)(2,1)S(1)} copy-done((bf16[256,2048]{1,0:T(8,128)(2,1)S(1)}, bf16[256,2048]{1,0:T(8,128)(2,1)}, u32[]{:S(2)}) %copy-start.2) | copy-done | bytes 1048600
  2.5 0.9 %state.1 = (bf16[512,128]{1,0:T(8,128)(2,1)S(1)}, f32[512,128]{1,0:T(8,128)S(1)}, bf16[256,2048]{1,0:T(8,128)(2,1)S(1)}, bf16[256,2048]{1,0:T(8,128)(2,1)S(1)}) custom-call(bf16[256,2048]{1,0:T(8,128)(2,1)S(1)} %copy-done.1, bf16[256,2048]{1,0:T(8,128)(2,1)S(1)} %copy-done.2), custom_call_target="tpu_custom_call" | custom-call | tf_op jit(solution)/shard_map/state/pallas_call | solution.py:164
  3.3 0.6 %collective-permute-start = (bf16[512,128]{1,0:T(8,128)(2,1)S(1)}, bf16[512,128]{1,0:T(8,128)(2,1)S(1)}, u32[]{:S(2)}, u32[]{:S(2)}) collective-permute-start(bf16[512,128]{1,0:T(8,128)(2,1)S(1)} %get-tuple-element.10), channel_id=1, source_target_pairs={{0,1},{1,0},{2,3},{3,2},{4,5},{5,4},{6,7},{7,6},{8,9},{9,8},{10,11... | collective-permute-start | bytes 393224 | tf_op jit(solution)/shard_map/ppermute | solution.py:19
  4.0 1.0 %collective-permute-done = bf16[512,128]{1,0:T(8,128)(2,1)S(1)} collective-permute-done((bf16[512,128]{1,0:T(8,128)(2,1)S(1)}, bf16[512,128]{1,0:T(8,128)(2,1)S(1)}, u32[]{:S(2)}, u32[]{:S(2)}) %collective-permute-start) | collective-permute-done | bytes 131104 | tf_op jit(solution)/shard_map/ppermute | solution.py:19
  5.0 0.0 copy-start.6
  5.0 0.6 %copy-done.6 = bf16[512,128]{1,0:T(8,128)(2,1)} copy-done((bf16[512,128]{1,0:T(8,128)(2,1)}, bf16[512,128]{1,0:T(8,128)(2,1)S(1)}, u32[]{:S(2)}) %copy-start.6) | copy-done | bytes 131096
  5.6 2.8 %collective-permute-start.1 = (bf16[256,128]{1,0:T(8,128)(2,1)S(1)}, bf16[256,128]{1,0:T(8,128)(2,1)S(1)}, u32[]{:S(2)}, u32[]{:S(2)}) collective-permute-start(bf16[256,128]{1,0:T(8,128)(2,1)S(1)} %select_convert_fusion), channel_id=1, source_target_pairs={{0,2},{1,3},{2,0},{3,1},{4,6},{5,7},{6,4},{7,5},{8,10},{9,11},{10,... | collective-permute-start | bytes 196616 | tf_op jit(solution)/shard_map/ppermute | solution.py:19
  8.5 2.4 %collective-permute-done.1 = bf16[256,128]{1,0:T(8,128)(2,1)S(1)} collective-permute-done((bf16[256,128]{1,0:T(8,128)(2,1)S(1)}, bf16[256,128]{1,0:T(8,128)(2,1)S(1)}, u32[]{:S(2)}, u32[]{:S(2)}) %collective-permute-start.1) | collective-permute-done | bytes 65568 | tf_op jit(solution)/shard_map/ppermute | solution.py:19
  10.9 0.0 copy-start.4
  10.9 2.0 %collective-permute-start.2 = (bf16[256,128]{1,0:T(8,128)(2,1)S(1)}, bf16[256,128]{1,0:T(8,128)(2,1)S(1)}, u32[]{:S(2)}, u32[]{:S(2)}) collective-permute-start(bf16[256,128]{1,0:T(8,128)(2,1)S(1)} %get-tuple-element.13), channel_id=1, source_target_pairs={{0,4},{1,5},{2,6},{3,7},{4,0},{5,1},{6,2},{7,3},{8,12},{9,13},{10,... | collective-permute-start | bytes 196616 | tf_op jit(solution)/shard_map/ppermute | solution.py:19
  12.9 2.3 %collective-permute-done.2 = bf16[256,128]{1,0:T(8,128)(2,1)S(1)} collective-permute-done((bf16[256,128]{1,0:T(8,128)(2,1)S(1)}, bf16[256,128]{1,0:T(8,128)(2,1)S(1)}, u32[]{:S(2)}, u32[]{:S(2)}) %collective-permute-start.2) | collective-permute-done | bytes 65568 | tf_op jit(solution)/shard_map/ppermute | solution.py:19
  15.3 0.0 copy-start.5
  15.3 0.0 copy-done.4
  15.3 0.0 copy-start
  15.3 0.6 %fusion.4 = bf16[256,128]{1,0:T(8,128)(2,1)} fusion(bf16[256,128]{1,0:T(8,128)(2,1)S(1)} %collective-permute-done.2, f32[256,128]{1,0:T(8,128)S(1)} %get-tuple-element.14, bf16[256,128]{1,0:T(8,128)(2,1)S(1)} %collective-permute-done.1), kind=kLoop, calls=%fused_computation.14 | loop fusion | flops 163840 | bytes 327680 | tf_op jit(solution)/shard_map/convert_element_type | solution.py:209
  15.9 0.0 copy-done.5
  15.9 2.9 %collective-permute-start.3 = (bf16[256,128]{1,0:T(8,128)(2,1)}, bf16[256,128]{1,0:T(8,128)(2,1)}, u32[]{:S(2)}, u32[]{:S(2)}) collective-permute-start(bf16[256,128]{1,0:T(8,128)(2,1)} %fusion.4), channel_id=1, source_target_pairs={{0,8},{1,9},{2,10},{3,11},{4,12},{5,13},{6,14},{7,15},{8,0},{9,1},... | collective-permute-start | bytes 196616 | tf_op jit(solution)/shard_map/ppermute | solution.py:19
  18.8 2.6 %collective-permute-done.3 = bf16[256,128]{1,0:T(8,128)(2,1)} collective-permute-done((bf16[256,128]{1,0:T(8,128)(2,1)}, bf16[256,128]{1,0:T(8,128)(2,1)}, u32[]{:S(2)}, u32[]{:S(2)}) %collective-permute-start.3) | collective-permute-done | bytes 65568 | tf_op jit(solution)/shard_map/ppermute | solution.py:19
  21.4 1.5 %add_convert_fusion.1 = bf16[256,128]{1,0:T(8,128)(2,1)} fusion(f32[256,128]{1,0:T(8,128)S(1)} %get-tuple-element.14, bf16[256,128]{1,0:T(8,128)(2,1)} %collective-permute-done.3, bf16[256,128]{1,0:T(8,128)(2,1)} %copy-done.5, pred[]{:T(512)S(6)} %eq.25, pred[]{:T(512)S(6)} %eq.24, pred[]{:T(512)S(6)} %eq.23), kind=kLoop, calls=%fused_computation.15 | loop fusion | flops 262144 | bytes 327683 | tf_op jit(solution)/shard_map/convert_element_type | solution.py:215
  22.9 1.8 %collective-permute-start.4 = (bf16[256,128]{1,0:T(8,128)(2,1)}, bf16[256,128]{1,0:T(8,128)(2,1)S(1)}, u32[]{:S(2)}, u32[]{:S(2)}) collective-permute-start(bf16[256,128]{1,0:T(8,128)(2,1)} %add_convert_fusion.1), channel_id=1, source_target_pairs={{0,2},{1,3},{2,0},{3,1},{4,6},{5,7},{6,4},{7,5},{8,10},{9,11},{10,... | collective-permute-start | bytes 196616 | tf_op jit(solution)/shard_map/ppermute | solution.py:19
  24.8 0.0 copy-start.7
  24.8 2.6 %collective-permute-done.4 = bf16[256,128]{1,0:T(8,128)(2,1)S(1)} collective-permute-done((bf16[256,128]{1,0:T(8,128)(2,1)}, bf16[256,128]{1,0:T(8,128)(2,1)S(1)}, u32[]{:S(2)}, u32[]{:S(2)}) %collective-permute-start.4) | collective-permute-done | bytes 65568 | tf_op jit(solution)/shard_map/ppermute | solution.py:19
  27.4 1.0 %convert_select_fusion.2 = (f32[256,128]{1,0:T(8,128)S(1)}, f32[256,128]{1,0:T(8,128)S(1)}) fusion(bf16[256,128]{1,0:T(8,128)(2,1)S(1)} %collective-permute-done.4, pred[]{:T(512)S(6)} %eq.23, bf16[256,128]{1,0:T(8,128)(2,1)} %copy-done.4, bf16[256,128]{1,0:T(8,128)(2,1)} %collective-permute-done.3, pred[]{:T(512)S(6)} %eq.25, bf16[256,128]{1,0:T(8,128)(2,1)} %copy-done.5, ...), kind=kLoop, calls=%fused_computation.7 | loop fusion | flops 360448 | bytes 524291 | tf_op jit(solution)/shard_map/jit(_where)/select_n | solution.py:216
  28.4 0.0 copy-done.7
  28.4 0.1 fusion.1
  28.5 0.1 collective-permute-start.5
  28.5 0.0 copy-done
  28.5 1.7 %shard_map.49.in1 = f32[256,512]{1,0:T(8,128)S(1)} custom-call(bf16[256,2048]{1,0:T(8,128)(2,1)S(1)} %copy-done, bf16[256,2048]{1,0:T(8,128)(2,1)S(1)} %get-tuple-element.11.k_ref, bf16[256,2048]{1,0:T(8,128)(2,1)S(1)} %get-tuple-element.12.v_ref), custom_call_target="tpu_custom_call" | custom-call | flops 150000000 | bytes 1500000 | tf_op jit(solution)/shard_map/pallas_call | solution.py:182
  30.3 1.7 %shard_map.48.in0 = f32[256,512]{1,0:T(8,128)S(1)} custom-call(bf16[256,2048]{1,0:T(8,128)(2,1)S(1)} %copy-done, bf16[256,2048]{1,0:T(8,128)(2,1)S(1)} %get-tuple-element.11.k_ref, bf16[256,2048]{1,0:T(8,128)(2,1)S(1)} %get-tuple-element.12.v_ref), custom_call_target="tpu_custom_call" | custom-call | flops 150000000 | bytes 1500000 | tf_op jit(solution)/shard_map/pallas_call | solution.py:182
  32.0 1.7 %shard_map.47.in1 = f32[256,512]{1,0:T(8,128)S(1)} custom-call(bf16[256,2048]{1,0:T(8,128)(2,1)S(1)} %copy-done, bf16[256,2048]{1,0:T(8,128)(2,1)S(1)} %get-tuple-element.11.k_ref, bf16[256,2048]{1,0:T(8,128)(2,1)S(1)} %get-tuple-element.12.v_ref), custom_call_target="tpu_custom_call" | custom-call | flops 150000000 | bytes 1500000 | tf_op jit(solution)/shard_map/pallas_call | solution.py:182
  33.7 0.0 copy-start.3
  33.7 1.7 %shard_map.46.in0 = f32[256,512]{1,0:T(8,128)S(1)} custom-call(bf16[256,2048]{1,0:T(8,128)(2,1)S(1)} %copy-done, bf16[256,2048]{1,0:T(8,128)(2,1)S(1)} %get-tuple-element.11.k_ref, bf16[256,2048]{1,0:T(8,128)(2,1)S(1)} %get-tuple-element.12.v_ref), custom_call_target="tpu_custom_call" | custom-call | flops 150000000 | bytes 1500000 | tf_op jit(solution)/shard_map/pallas_call | solution.py:182
  35.4 0.0 copy-done.3
  35.4 1.8 %shard_map.50.rest_0_ = bf16[256,2048]{1,0:T(8,128)(2,1)} custom-call(bf16[512,128]{1,0:T(8,128)(2,1)S(1)} %get-tuple-element.15.prior_ref, bf16[256,2048]{1,0:T(8,128)(2,1)S(1)} %copy-done, f32[256,512]{1,0:T(8,128)S(1)} %shard_map.48.in0, f32[256,512]{1,0:T(8,128)S(1)} %shard_map.49.in1, f32[1,2048]{1,0:T(1,128)S(1)} %bitcast.1), custom_call_target="tpu_custom_call" | custom-call | flops 100000000 | bytes 2000000 | tf_op jit(solution)/shard_map/pallas_call | solution.py:231
  37.2 0.0 collective-permute-done.5.prior_ref
  37.2 1.8 %shard_map.51 = bf16[256,2048]{1,0:T(8,128)(2,1)} custom-call(bf16[512,128]{1,0:T(8,128)(2,1)S(1)} %collective-permute-done.5.prior_ref, bf16[256,2048]{1,0:T(8,128)(2,1)S(1)} %copy-done, f32[256,512]{1,0:T(8,128)S(1)} %shard_map.46.in0, f32[256,512]{1,0:T(8,128)S(1)} %shard_map.47.in1, f32[1,2048]{1,0:T(1,128)S(1)} %bitcast.2, ...), custom_call_target="tpu_custom_call", output_to_operand_aliasing={{}: (5, {})} | custom-call | flops 100000000 | bytes 2000000 | tf_op jit(solution)/shard_map/pallas_call | solution.py:231
  (3 shorter events, 0.1 us)
Async XLA Ops:
  0.0 1.2 %copy-start.1 = (bf16[256,2048]{1,0:T(8,128)(2,1)S(1)}, bf16[256,2048]{1,0:T(8,128)(2,1)}, u32[]{:S(2)}) copy-start(bf16[256,2048]{1,0:T(8,128)(2,1)} %k_hbm.1) | copy-start | bytes 3145732
  1.2 1.2 %copy-start.2 = (bf16[256,2048]{1,0:T(8,128)(2,1)S(1)}, bf16[256,2048]{1,0:T(8,128)(2,1)}, u32[]{:S(2)}) copy-start(bf16[256,2048]{1,0:T(8,128)(2,1)} %v_hbm.1) | copy-start | bytes 3145732
  3.3 1.6 %collective-permute-start = (bf16[512,128]{1,0:T(8,128)(2,1)S(1)}, bf16[512,128]{1,0:T(8,128)(2,1)S(1)}, u32[]{:S(2)}, u32[]{:S(2)}) collective-permute-start(bf16[512,128]{1,0:T(8,128)(2,1)S(1)} %get-tuple-element.10), channel_id=1, source_target_pairs={{0,1},{1,0},{2,3},{3,2},{4,5},{5,4},{6,7},{7,6},{8,9},{9,8},{10,11... | collective-permute-start | bytes 393224 | tf_op jit(solution)/shard_map/ppermute | solution.py:19
  5.0 0.7 %copy-start.6 = (bf16[512,128]{1,0:T(8,128)(2,1)}, bf16[512,128]{1,0:T(8,128)(2,1)S(1)}, u32[]{:S(2)}) copy-start(bf16[512,128]{1,0:T(8,128)(2,1)S(1)} %collective-permute-done) | copy-start | bytes 393220
  5.6 5.2 %collective-permute-start.1 = (bf16[256,128]{1,0:T(8,128)(2,1)S(1)}, bf16[256,128]{1,0:T(8,128)(2,1)S(1)}, u32[]{:S(2)}, u32[]{:S(2)}) collective-permute-start(bf16[256,128]{1,0:T(8,128)(2,1)S(1)} %select_convert_fusion), channel_id=1, source_target_pairs={{0,2},{1,3},{2,0},{3,1},{4,6},{5,7},{6,4},{7,5},{8,10},{9,11},{10,... | collective-permute-start | bytes 196616 | tf_op jit(solution)/shard_map/ppermute | solution.py:19
  10.9 4.4 %copy-start.4 = (bf16[256,128]{1,0:T(8,128)(2,1)}, bf16[256,128]{1,0:T(8,128)(2,1)S(1)}, u32[]{:S(2)}) copy-start(bf16[256,128]{1,0:T(8,128)(2,1)S(1)} %collective-permute-done.1) | copy-start | bytes 196612
  10.9 4.3 %collective-permute-start.2 = (bf16[256,128]{1,0:T(8,128)(2,1)S(1)}, bf16[256,128]{1,0:T(8,128)(2,1)S(1)}, u32[]{:S(2)}, u32[]{:S(2)}) collective-permute-start(bf16[256,128]{1,0:T(8,128)(2,1)S(1)} %get-tuple-element.13), channel_id=1, source_target_pairs={{0,4},{1,5},{2,6},{3,7},{4,0},{5,1},{6,2},{7,3},{8,12},{9,13},{10,... | collective-permute-start | bytes 196616 | tf_op jit(solution)/shard_map/ppermute | solution.py:19
  15.3 0.7 %copy-start.5 = (bf16[256,128]{1,0:T(8,128)(2,1)}, bf16[256,128]{1,0:T(8,128)(2,1)S(1)}, u32[]{:S(2)}) copy-start(bf16[256,128]{1,0:T(8,128)(2,1)S(1)} %collective-permute-done.2) | copy-start | bytes 196612
  15.3 13.3 %copy-start = (bf16[256,2048]{1,0:T(8,128)(2,1)S(1)}, bf16[256,2048]{1,0:T(8,128)(2,1)}, u32[]{:S(2)}) copy-start(bf16[256,2048]{1,0:T(8,128)(2,1)} %q_hbm.11) | copy-start | bytes 3145732
  15.9 5.5 %collective-permute-start.3 = (bf16[256,128]{1,0:T(8,128)(2,1)}, bf16[256,128]{1,0:T(8,128)(2,1)}, u32[]{:S(2)}, u32[]{:S(2)}) collective-permute-start(bf16[256,128]{1,0:T(8,128)(2,1)} %fusion.4), channel_id=1, source_target_pairs={{0,8},{1,9},{2,10},{3,11},{4,12},{5,13},{6,14},{7,15},{8,0},{9,1},... | collective-permute-start | bytes 196616 | tf_op jit(solution)/shard_map/ppermute | solution.py:19
  22.9 4.5 %collective-permute-start.4 = (bf16[256,128]{1,0:T(8,128)(2,1)}, bf16[256,128]{1,0:T(8,128)(2,1)S(1)}, u32[]{:S(2)}, u32[]{:S(2)}) collective-permute-start(bf16[256,128]{1,0:T(8,128)(2,1)} %add_convert_fusion.1), channel_id=1, source_target_pairs={{0,2},{1,3},{2,0},{3,1},{4,6},{5,7},{6,4},{7,5},{8,10},{9,11},{10,... | collective-permute-start | bytes 196616 | tf_op jit(solution)/shard_map/ppermute | solution.py:19
  24.8 3.6 %copy-start.7 = (bf16[512,128]{1,0:T(8,128)(2,1)S(1)}, bf16[512,128]{1,0:T(8,128)(2,1)}, u32[]{:S(2)}) copy-start(bf16[512,128]{1,0:T(8,128)(2,1)} %copy-done.6) | copy-start | bytes 393220
  28.5 8.7 %collective-permute-start.5 = (bf16[512,128]{1,0:T(8,128)(2,1)S(1)}, bf16[512,128]{1,0:T(8,128)(2,1)S(1)}, u32[]{:S(2)}, u32[]{:S(2)}) collective-permute-start(bf16[512,128]{1,0:T(8,128)(2,1)S(1)} %get-tuple-element.16), channel_id=1, source_target_pairs={{0,1},{1,0},{2,3},{3,2},{4,5},{5,4},{6,7},{7,6},{8,9},{9,8},{10,11... | collective-permute-start | bytes 393224 | tf_op jit(solution)/shard_map/ppermute | solution.py:19
  33.7 1.7 %copy-start.3 = (f32[2048]{0:T(1024)S(1)}, f32[2048]{0:T(1024)}, u32[]{:S(2)}) copy-start(f32[2048]{0:T(1024)} %param.7) | copy-start | bytes 24580

commit v3 on v0

v3 whole, which is shorter than its diff:
```python
import functools

import jax
import jax.numpy as jnp
from jax import lax
from jax.experimental import pallas as pl
from jax.experimental.pallas import tpu as pltpu
from jax.sharding import PartitionSpec as P


HEAD_DIM = 64
PAIR = 2 * HEAD_DIM
QUAD = 4 * HEAD_DIM
EPS = 1e-05
AXIS = "seq"
BF16, F32 = jnp.bfloat16, jnp.float32


def core_bit():
    return lax.axis_index(AXIS) & 1


def side_bit():
    return (lax.axis_index(AXIS) >> 1) & 1


def aligned(index, by):
    return pl.multiple_of(index * by, by)


def first_lanes(shape):
    return lax.broadcasted_iota(jnp.int32, shape, len(shape) - 1) % PAIR < HEAD_DIM


def dot(a, b, dims):
    return lax.dot_general(a, b, (dims, ((), ())), preferred_element_type=F32)


def states_of(k_ref, v_ref, out_ref, start, width):
    first = first_lanes((HEAD_DIM, PAIR))
    for quad in range(width // QUAD):
        lanes = pl.ds(start + quad * QUAD, QUAD)
        fk = jnp.maximum(k_ref[:, lanes], 0)
        full = dot(fk, v_ref[:, lanes], ((0,), (0,)))
        for p in range(2):
            at = p * PAIR
            rows = full[at : at + PAIR, at : at + PAIR]
            packed = jnp.where(first, rows[:HEAD_DIM], rows[HEAD_DIM:])
            out_ref[pl.ds((quad * 2 + p) * HEAD_DIM, HEAD_DIM), :] = packed.astype(out_ref.dtype)


def send_kernel(k_hbm, v_hbm, send_ref, k_ref, v_ref, sems):
    half = k_ref.shape[1] // 2
    core = core_bit()
    loads = []
    for step, which in enumerate((1 - core, core)):
        for n, (src, dst) in enumerate(((k_hbm, k_ref), (v_hbm, v_ref))):
            there, here = pl.ds(aligned(which, half), half), pl.ds(step * half, half)
            loads.append(pltpu.make_async_copy(src.at[:, there], dst.at[:, here], sems.at[step, n]))
            loads[-1].start()
    loads[0].wait()
    loads[1].wait()
    states_of(k_ref, v_ref, send_ref, 0, half)
    loads[2].wait()
    loads[3].wait()


def keep_kernel(k_ref, v_ref, q_hbm, keep_ref, q_ref, sems):
    half = k_ref.shape[1] // 2
    core = core_bit()
    loads = []
    for step, which in enumerate((1 - core, core)):
        there, here = pl.ds(aligned(which, half), half), pl.ds(step * half, half)
        loads.append(pltpu.make_async_copy(q_hbm.at[:, there], q_ref.at[:, here], sems.at[step]))
        loads[-1].start()
    states_of(k_ref, v_ref, keep_ref, half, half)
    for load in loads:
        load.wait()


def after_core(keep, got, send, own, ext):
    rows = own.shape[0]
    side = side_bit()
    mine, other = pl.ds(aligned(side, rows), rows), pl.ds(aligned(1 - side, rows), rows)
    send[...] = (keep[other, :] + got[other, :].astype(F32)).astype(BF16)
    own[...] = keep[mine, :] + got[mine, :].astype(F32)

    @pl.when(core_bit() == 0)
    def _():
        ext[...] = keep[...]

    @pl.when(core_bit() == 1)
    def _():
        ext[...] = got[...].astype(F32)


def after_side(own, got, send, total, ext):
    value = own[...] + got[...].astype(F32)
    send[...] = value.astype(BF16)
    total[...] = value
    ext[...] = jnp.where(side_bit() == 0, own[...], got[...].astype(F32))


def after_outer(total, before, got, send, total_out, before_out, *, level):
    value = got[...].astype(F32)
    new = total[...] + value
    send[...] = new.astype(BF16)
    total_out[...] = new
    upper = (lax.axis_index(AXIS) >> level) & 1
    value = jnp.where(upper == 1, value, 0.0)
    before_out[...] = value if before is None else before[...] + value


def after_last(before, got, ext, send, mine, *, level):
    upper = (lax.axis_index(AXIS) >> level) & 1
    value = jnp.where(upper == 1, got[...].astype(F32), 0.0)
    if before is not None:
        value = before[...] + value
    both = value + ext[...]
    first = side_bit() == 0
    send[...] = jnp.where(first, both, value).astype(BF16)
    mine[...] = jnp.where(first, value, both)


def after_base(mine, got, ext, send, prior):
    rows = mine.shape[0]
    side, first = side_bit(), core_bit() == 0
    for which, value in ((side, mine[...]), (1 - side, got[...].astype(F32))):
        here = pl.ds(aligned(which, rows), rows)
        both = value + ext[here, :]
        send[here, :] = jnp.where(first, both, value).astype(BF16)
        prior[here, :] = jnp.where(first, value, both).astype(BF16)


def intra_kernel(q_ref, k_ref, v_ref, out, intra_ref, sems, *, start):
    count, width = intra_ref.shape
    mid = count // 2
    first = first_lanes((count, PAIR))
    rows = lax.broadcasted_iota(jnp.int32, (mid, mid), 0)
    cols = lax.broadcasted_iota(jnp.int32, (mid, mid), 1)
    causal = cols <= rows
    copies = []
    for p in range(width // PAIR):
        lanes = pl.ds(p * PAIR, PAIR)
        there = pl.ds(start + p * PAIR, PAIR)
        fq = jnp.maximum(q_ref[:, there], 0)
        fk = jnp.maximum(k_ref[:, there], 0)
        val = v_ref[:, there]
        zero = jnp.zeros_like(fq)
        top, low, weights = [], [], []
        for h in range(2):
            mine = first if h == 0 else jnp.logical_not(first)
            mine_q = jnp.where(mine, fq, zero)
            s_top = dot(mine_q[:mid], fk[:mid], ((1,), (1,)))
            s_low = dot(mine_q[mid:], fk, ((1,), (1,)))
            s_top = jnp.where(causal, s_top, 0.0).astype(BF16)
            s_diag = jnp.where(causal, s_low[:, mid:], 0.0).astype(BF16)
            s_low = jnp.concatenate([s_low[:, :mid].astype(BF16), s_diag], axis=1)
            top.append(s_top)
            low.append(s_low)
            weights.append(jnp.where(mine, val, zero))
        w_top = jnp.concatenate([w[:mid] for w in weights], axis=0)
        intra_ref[:mid, lanes] = dot(jnp.concatenate(top, axis=1), w_top, ((1,), (0,)))
        w_low = jnp.concatenate(weights, axis=0)
        intra_ref[mid:, lanes] = dot(jnp.concatenate(low, axis=1), w_low, ((1,), (0,)))
        copies.append(pltpu.make_async_copy(intra_ref.at[:, lanes], out.at[:, lanes], sems.at[p]))
        copies[-1].start()
    for copy in copies:
        copy.wait()


def final_kernel(prior_ref, q_ref, in0, in1, gain_ref, *rest, step):
    out_hbm, in_buf, out_buf, in_sems, sems = rest[-5:]
    half = out_buf.shape[1]
    width = half // 2
    core = core_bit()
    base = aligned(core if step == 0 else 1 - core, half)
    loads = []
    for n, src in enumerate((in0, in1)):
        loads.append(pltpu.make_async_copy(src, in_buf.at[:, pl.ds(n * width, width)], in_sems.at[n]))
        loads[-1].start()
    lane = lax.broadcasted_iota(jnp.int32, (QUAD, QUAD), 1) // HEAD_DIM
    row = lax.broadcasted_iota(jnp.int32, (QUAD, QUAD), 0) // HEAD_DIM
    same = lane == row
    ones = jnp.where(same, 1.0 / HEAD_DIM, 0.0).astype(BF16)
    copies = []
    for quad in range(half // QUAD):
        lanes = pl.ds(quad * QUAD, QUAD)
        one = prior_ref[pl.ds(quad * PAIR, HEAD_DIM), :]
        two = prior_ref[pl.ds(quad * PAIR + HEAD_DIM, HEAD_DIM), :]
        wide = jnp.concatenate([one, two], axis=1)
        block = jnp.concatenate([wide] * 4, axis=0)
        block = jnp.where(same, block, jnp.zeros_like(block))
        q_lanes = pl.ds((0 if step == 1 else half) + quad * QUAD, QUAD)
        fq = jnp.maximum(q_ref[:, q_lanes], 0)
        if quad * QUAD % width == 0:
            loads[quad * QUAD // width].wait()
        numer = dot(fq, block, ((1,), (0,))) + in_buf[:, lanes]
        square = (numer * numer).astype(BF16)
        mean_sq = dot(square, ones, ((1,), (0,)))
        there = pl.ds(pl.multiple_of(base + quad * QUAD, QUAD), QUAD)
        normed = numer * lax.rsqrt(mean_sq + EPS) * gain_ref[:, there]
        out_buf[:, lanes] = normed.astype(BF16)
        copies.append(pltpu.make_async_copy(out_buf.at[:, lanes], out_hbm.at[:, there], sems.at[quad]))
        copies[-1].start()
    for copy in copies:
        copy.wait()


ANY = pl.BlockSpec(memory_space=pl.ANY)
HBM = pl.BlockSpec(memory_space=pltpu.HBM)
VMEM = pl.BlockSpec(memory_space=pltpu.VMEM)
DMA = pltpu.SemaphoreType.DMA


def call(kernel, outs, args, specs=None, out_specs=None, scratch=(), alias=None, cost=(10_000, 10_000)):
    specs = [VMEM] * len(args) if specs is None else specs
    args = [a if s is ANY else pltpu.with_memory_space_constraint(a, s.memory_space) for a, s in zip(args, specs)]
    many = isinstance(outs, (tuple, list))
    return pl.pallas_call(
        kernel,
        out_shape=outs,
        in_specs=specs,
        out_specs=([VMEM] * len(outs) if many else VMEM) if out_specs is None else out_specs,
        scratch_shapes=scratch,
        input_output_aliases=alias or {},
        compiler_params=pltpu.CompilerParams(vmem_limit_bytes=12 * 2**20),
        cost_estimate=pl.CostEstimate(flops=cost[0], transcendentals=0, bytes_accessed=cost[1]),
    )(*args)


def on_device(queries, keys, values, gain, *, size):
    count, width = queries.shape
    half, part = width // 2, width // 4
    rows = half // PAIR * HEAD_DIM
    quarter = rows // 2
    wide = pltpu.VMEM((count, width), BF16)

    def swap(x, level):
        return lax.ppermute(x, AXIS, [(i, i ^ (1 << level)) for i in range(size)])

    def small(dtype, n=quarter):
        return pltpu.VMEM((n, PAIR), dtype)

    send, k_vmem, v_vmem = call(
        send_kernel,
        (small(BF16, rows), wide, wide),
        (keys, values),
        specs=[HBM, HBM],
        scratch=[DMA((2, 2))],
        cost=(150_000_000, 2_000_000),
    )
    got = swap(send, 0)
    keep, q_vmem = call(
        keep_kernel,
        (small(F32, rows), wide),
        (k_vmem, v_vmem, queries),
        specs=[VMEM, VMEM, HBM],
        scratch=[DMA((2,))],
        cost=(150_000_000, 1_000_000),
    )
    parts = [
        call(
            functools.partial(intra_kernel, start=n * part),
            jax.ShapeDtypeStruct((count, part), F32),
            (q_vmem, k_vmem, v_vmem),
            out_specs=ANY,
            scratch=[pltpu.VMEM((count, part), F32), DMA((part // PAIR,))],
            cost=(150_000_000, 1_500_000),
        )
        for n in range(4)
    ]
    send, own, ext_core = call(after_core, (small(BF16), small(F32), small(F32, rows)), (keep, got))
    got = swap(send, 1)
    send, total, ext_side = call(after_side, (small(BF16), small(F32), small(F32)), (own, got))
    before = None
    level = 2
    while 1 << level < size:
        got = swap(send, level)
        last = 1 << (level + 1) >= size
        kernel = functools.partial(after_last if last else after_outer, level=level)
        args = [got, ext_side] if last else [got]
        if before is None:
            kernel = functools.partial(lambda k, *a: k(a[0], None, *a[1:]), kernel) if not last else functools.partial(lambda k, *a: k(None, *a), kernel)
        else:
            args = [before, *args]
        if last:
            send, mine = call(kernel, (small(BF16), small(F32)), args)
        else:
            send, total, before = call(kernel, (small(BF16), small(F32), small(F32)), [total, *args])
        level += 1
    got = swap(send, 1)
    send, prior = call(after_base, (small(BF16, rows), small(BF16, rows)), (mine, got, ext_core))
    got = swap(send, 0)

    out = None
    for step, prior in ((0, prior), (1, got)):
        args = [prior, q_vmem, *(parts[2:] if step == 0 else parts[:2]), gain[None, :]]
        specs = [VMEM, VMEM, ANY, ANY, VMEM]
        if out is not None:
            args.append(out)
            specs.append(ANY)
        out = call(
            functools.partial(final_kernel, step=step),
            jax.ShapeDtypeStruct((count, width), BF16),
            args,
            specs=specs,
            out_specs=ANY,
            scratch=[
                pltpu.VMEM((count, half), F32),
                pltpu.VMEM((count, half), BF16),
                DMA((2,)),
                DMA((half // QUAD,)),
            ],
            alias={} if out is None else {5: 0},
            cost=(100_000_000, 2_000_000),
        )
    return out


def solution(mesh):
    return jax.shard_map(
        functools.partial(on_device, size=mesh.shape[AXIS]),
        mesh=mesh,
        in_specs=(
            P(("groups", "seq"), None),
            P(("groups", "seq"), None),
            P(("groups", "seq"), None),
            P(),
        ),
        out_specs=P(("groups", "seq"), None),
        check_vma=False,
    )
```

time: 129 us -> 33.8 us (0.26)
  waiting for transfers between devices: 66.6 us -> 10.1 us
  other arithmetic: 30.3 us -> 0 us
  Pallas kernels: 0 us -> 13.8 us
  between operations: 13.5 us -> 0.12 us
  matrix products: 9.9 us -> 0 us
  starting transfers between devices: 0.01 us -> 9.69 us
  local copies, waits for them, and re-layouts: 7.12 us -> 0.01 us
    all_gather x1 -> x0, waiting for transfers between devices: 66.6 us -> none  [entering(): everything = lax.all_gather(shard.astype(jnp.bfloat16), axis)]
    select_n x16 -> x0, other arithmetic: 25.9 us -> none  [hop(): return jnp.where(reached, new, before)]
    pallas_call x0 -> x13, Pallas kernels: none -> 13.8 us  [call(): pl.pallas_call(kernel, out_shape=outs, in_specs=specs, out_specs=([VMEM]...]
    ppermute x0 -> x6, waiting for transfers between devices: none -> 10.1 us  [swap(): return lax.ppermute(x, AXIS, [(i, i ^ 1 << level) for i in range(size)])]
    dot_general x10 -> x0, matrix products: 9.9 us -> none  [the longest x4 5.01 us: on_device(): jnp.einsum('hts,she->the', scores, v_grp, preferred_element_type=jnp.floa...]
    ppermute x0 -> x6, starting transfers between devices: none -> 9.69 us  [swap(): return lax.ppermute(x, AXIS, [(i, i ^ 1 << level) for i in range(size)])]
    unnamed x13 -> x2, local copies, waits for them, and re-layouts: 5.24 us -> 0.01 us
    convert_element_type x1 -> x0, other arithmetic: 2.75 us -> none  [on_device(): return normed.astype(jnp.bfloat16)]
  transfers between devices with their start and end apart: 1 -> 6, of which waited for: 1 -> 4; matrix products, arithmetic and copies ran while one was open for 8% -> 0% of each run, Pallas kernels for 0% -> 29%
where the time goes in v3:
time: 33.8 us; the launch traced here: 33.7 us
  Pallas kernels  13.8 us (41%)
  waiting for transfers between devices  10.1 us (30%)
  starting transfers between devices  9.69 us (29%)
    pallas_call x13, Pallas kernels, call(): pl.pallas_call(kernel, out_shape=outs, in_specs=specs, out_specs=([VMEM]...  13.8 us
    ppermute x6, waiting for transfers between devices, swap(): return lax.ppermute(x, AXIS, [(i, i ^ 1 << level) for i in range(size)])  10.1 us
    ppermute x6, starting transfers between devices, swap(): return lax.ppermute(x, AXIS, [(i, i ^ 1 << level) for i in range(size)])  9.69 us
  transfers between devices with their start and end apart: 6, of which 4 were waited for; matrix products, arithmetic and copies ran while one was open for 0% of the time, Pallas kernels for 29%

profile of v3, /device:TPU:0, one launch (start us, length us, event | category | flops | bytes accessed | tf_op | source)
XLA Modules:
  0.0 33.7 jit_solution(6113915804908810376)
XLA Ops:
  0.0 1.6 %shard_map.46 = (bf16[512,128]{1,0:T(8,128)(2,1)S(1)}, bf16[256,2048]{1,0:T(8,128)(2,1)S(1)}, bf16[256,2048]{1,0:T(8,128)(2,1)S(1)}) custom-call(bf16[256,2048]{1,0:T(8,128)(2,1)} %k_hbm.1, bf16[256,2048]{1,0:T(8,128)(2,1)} %v_hbm.1), custom_call_target="tpu_custom_call" | custom-call | flops 150000000 | bytes 2000000 | tf_op jit(solution)/shard_map/pallas_call | solution.py:220
  1.6 0.6 %collective-permute-start = (bf16[512,128]{1,0:T(8,128)(2,1)S(1)}, bf16[512,128]{1,0:T(8,128)(2,1)S(1)}, u32[]{:S(2)}, u32[]{:S(2)}) collective-permute-start(bf16[512,128]{1,0:T(8,128)(2,1)S(1)} %get-tuple-element.25), channel_id=1, source_target_pairs={{0,1},{1,0},{2,3},{3,2},{4,5},{5,4},{6,7},{7,6},{8,9},{9,8},{10,11... | collective-permute-start | bytes 393224 | tf_op jit(solution)/shard_map/ppermute | solution.py:240
  2.2 1.3 %shard_map.47 = (f32[512,128]{1,0:T(8,128)S(1)}, bf16[256,2048]{1,0:T(8,128)(2,1)S(1)}) custom-call(bf16[256,2048]{1,0:T(8,128)(2,1)S(1)} %get-tuple-element.22.k_ref, bf16[256,2048]{1,0:T(8,128)(2,1)S(1)} %get-tuple-element.23.v_ref, bf16[256,2048]{1,0:T(8,128)(2,1)} %q_hbm.1), custom_call_target="tpu_custom_call" | custom-call | flops 150000000 | bytes 1000000 | tf_op jit(solution)/shard_map/pallas_call | solution.py:220
  3.5 0.0 collective-permute-done.got
  3.5 0.1 shard_map.48
  3.6 2.6 %collective-permute-start.1 = (bf16[256,128]{1,0:T(8,128)(2,1)S(1)}, bf16[256,128]{1,0:T(8,128)(2,1)S(1)}, u32[]{:S(2)}, u32[]{:S(2)}) collective-permute-start(bf16[256,128]{1,0:T(8,128)(2,1)S(1)} %get-tuple-element.27), channel_id=1, source_target_pairs={{0,2},{1,3},{2,0},{3,1},{4,6},{5,7},{6,4},{7,5},{8,10},{9,11},{10,... | collective-permute-start | bytes 196616 | tf_op jit(solution)/shard_map/ppermute | solution.py:240
  6.2 2.7 %collective-permute-done.1.got = bf16[256,128]{1,0:T(8,128)(2,1)S(1)} collective-permute-done((bf16[256,128]{1,0:T(8,128)(2,1)S(1)}, bf16[256,128]{1,0:T(8,128)(2,1)S(1)}, u32[]{:S(2)}, u32[]{:S(2)}) %collective-permute-start.1) | collective-permute-done | bytes 65568 | tf_op jit(solution)/shard_map/ppermute | solution.py:240
  8.9 1.9 %collective-permute-start.2 = (bf16[256,128]{1,0:T(8,128)(2,1)S(1)}, bf16[256,128]{1,0:T(8,128)(2,1)S(1)}, u32[]{:S(2)}, u32[]{:S(2)}) collective-permute-start(bf16[256,128]{1,0:T(8,128)(2,1)S(1)} %get-tuple-element.29), channel_id=1, source_target_pairs={{0,4},{1,5},{2,6},{3,7},{4,0},{5,1},{6,2},{7,3},{8,12},{9,13},{10,... | collective-permute-start | bytes 196616 | tf_op jit(solution)/shard_map/ppermute | solution.py:240
  10.8 2.5 %collective-permute-done.2.a_1_ = bf16[256,128]{1,0:T(8,128)(2,1)S(1)} collective-permute-done((bf16[256,128]{1,0:T(8,128)(2,1)S(1)}, bf16[256,128]{1,0:T(8,128)(2,1)S(1)}, u32[]{:S(2)}, u32[]{:S(2)}) %collective-permute-start.2) | collective-permute-done | bytes 65568 | tf_op jit(solution)/shard_map/ppermute | solution.py:240
  13.3 0.7 %shard_map.50 = (bf16[256,128]{1,0:T(8,128)(2,1)S(1)}, f32[256,128]{1,0:T(8,128)}, f32[256,128]{1,0:T(8,128)S(1)}) custom-call(f32[256,128]{1,0:T(8,128)S(1)} %get-tuple-element.28.a_0_, bf16[256,128]{1,0:T(8,128)(2,1)S(1)} %collective-permute-done.2.a_1_), custom_call_target="tpu_custom_call" | custom-call | flops 10000 | bytes 10000 | tf_op jit(solution)/shard_map/pallas_call | solution.py:220
  13.9 2.8 %collective-permute-start.3 = (bf16[256,128]{1,0:T(8,128)(2,1)S(1)}, bf16[256,128]{1,0:T(8,128)(2,1)S(1)}, u32[]{:S(2)}, u32[]{:S(2)}) collective-permute-start(bf16[256,128]{1,0:T(8,128)(2,1)S(1)} %get-tuple-element.31), channel_id=1, source_target_pairs={{0,8},{1,9},{2,10},{3,11},{4,12},{5,13},{6,14},{7,15},{8,0},{9,1},... | collective-permute-start | bytes 196616 | tf_op jit(solution)/shard_map/ppermute | solution.py:240
  16.8 2.4 %collective-permute-done.3.got = bf16[256,128]{1,0:T(8,128)(2,1)S(1)} collective-permute-done((bf16[256,128]{1,0:T(8,128)(2,1)S(1)}, bf16[256,128]{1,0:T(8,128)(2,1)S(1)}, u32[]{:S(2)}, u32[]{:S(2)}) %collective-permute-start.3) | collective-permute-done | bytes 65568 | tf_op jit(solution)/shard_map/ppermute | solution.py:240
  19.1 1.8 %collective-permute-start.4 = (bf16[256,128]{1,0:T(8,128)(2,1)S(1)}, bf16[256,128]{1,0:T(8,128)(2,1)S(1)}, u32[]{:S(2)}, u32[]{:S(2)}) collective-permute-start(bf16[256,128]{1,0:T(8,128)(2,1)S(1)} %get-tuple-element.34), channel_id=1, source_target_pairs={{0,2},{1,3},{2,0},{3,1},{4,6},{5,7},{6,4},{7,5},{8,10},{9,11},{10,... | collective-permute-start | bytes 196616 | tf_op jit(solution)/shard_map/ppermute | solution.py:240
  21.0 2.5 %collective-permute-done.4.got = bf16[256,128]{1,0:T(8,128)(2,1)S(1)} collective-permute-done((bf16[256,128]{1,0:T(8,128)(2,1)S(1)}, bf16[256,128]{1,0:T(8,128)(2,1)S(1)}, u32[]{:S(2)}, u32[]{:S(2)}) %collective-permute-start.4) | collective-permute-done | bytes 65568 | tf_op jit(solution)/shard_map/ppermute | solution.py:240
  23.5 0.1 shard_map.52
  23.5 0.1 collective-permute-start.5
  23.6 1.7 %shard_map.56.in1 = f32[256,512]{1,0:T(8,128)S(1)} custom-call(bf16[256,2048]{1,0:T(8,128)(2,1)S(1)} %get-tuple-element.37.q_ref, bf16[256,2048]{1,0:T(8,128)(2,1)S(1)} %get-tuple-element.22.k_ref, bf16[256,2048]{1,0:T(8,128)(2,1)S(1)} %get-tuple-element.23.v_ref), custom_call_target="tpu_custom_call" | custom-call | flops 150000000 | bytes 1500000 | tf_op jit(solution)/shard_map/pallas_call | solution.py:220
  25.3 1.7 %shard_map.55.in0 = f32[256,512]{1,0:T(8,128)S(1)} custom-call(bf16[256,2048]{1,0:T(8,128)(2,1)S(1)} %get-tuple-element.37.q_ref, bf16[256,2048]{1,0:T(8,128)(2,1)S(1)} %get-tuple-element.22.k_ref, bf16[256,2048]{1,0:T(8,128)(2,1)S(1)} %get-tuple-element.23.v_ref), custom_call_target="tpu_custom_call" | custom-call | flops 150000000 | bytes 1500000 | tf_op jit(solution)/shard_map/pallas_call | solution.py:220
  26.9 1.7 %shard_map.54.in1 = f32[256,512]{1,0:T(8,128)S(1)} custom-call(bf16[256,2048]{1,0:T(8,128)(2,1)S(1)} %get-tuple-element.37.q_ref, bf16[256,2048]{1,0:T(8,128)(2,1)S(1)} %get-tuple-element.22.k_ref, bf16[256,2048]{1,0:T(8,128)(2,1)S(1)} %get-tuple-element.23.v_ref), custom_call_target="tpu_custom_call" | custom-call | flops 150000000 | bytes 1500000 | tf_op jit(solution)/shard_map/pallas_call | solution.py:220
  28.6 0.0 copy-start
  28.6 1.7 %shard_map.53.in0 = f32[256,512]{1,0:T(8,128)S(1)} custom-call(bf16[256,2048]{1,0:T(8,128)(2,1)S(1)} %get-tuple-element.37.q_ref, bf16[256,2048]{1,0:T(8,128)(2,1)S(1)} %get-tuple-element.22.k_ref, bf16[256,2048]{1,0:T(8,128)(2,1)S(1)} %get-tuple-element.23.v_ref), custom_call_target="tpu_custom_call" | custom-call | flops 150000000 | bytes 1500000 | tf_op jit(solution)/shard_map/pallas_call | solution.py:220
  30.3 0.0 copy-done
  30.3 1.7 %shard_map.57.rest_0_ = bf16[256,2048]{1,0:T(8,128)(2,1)} custom-call(bf16[512,128]{1,0:T(8,128)(2,1)S(1)} %get-tuple-element.38.prior_ref, bf16[256,2048]{1,0:T(8,128)(2,1)S(1)} %get-tuple-element.37.q_ref, f32[256,512]{1,0:T(8,128)S(1)} %shard_map.55.in0, f32[256,512]{1,0:T(8,128)S(1)} %shard_map.56.in1, f32[1,2048]{1,0:T(1,128)S(1)} %bitcast.1), custom_call_target="tpu_custom_call" | custom-call | flops 100000000 | bytes 2000000 | tf_op jit(solution)/shard_map/pallas_call | solution.py:220
  32.0 0.0 collective-permute-done.5.prior_ref
  32.0 1.7 %shard_map.58 = bf16[256,2048]{1,0:T(8,128)(2,1)} custom-call(bf16[512,128]{1,0:T(8,128)(2,1)S(1)} %collective-permute-done.5.prior_ref, bf16[256,2048]{1,0:T(8,128)(2,1)S(1)} %get-tuple-element.37.q_ref, f32[256,512]{1,0:T(8,128)S(1)} %shard_map.53.in0, f32[256,512]{1,0:T(8,128)S(1)} %shard_map.54.in1, ...), custom_call_target="tpu_custom_call", output_to_operand_aliasing={{}: (5, {})} | custom-call | flops 100000000 | bytes 2000000 | tf_op jit(solution)/shard_map/pallas_call | solution.py:220
  (2 shorter events, 0.1 us)
Async XLA Ops:
  1.6 1.9 %collective-permute-start = (bf16[512,128]{1,0:T(8,128)(2,1)S(1)}, bf16[512,128]{1,0:T(8,128)(2,1)S(1)}, u32[]{:S(2)}, u32[]{:S(2)}) collective-permute-start(bf16[512,128]{1,0:T(8,128)(2,1)S(1)} %get-tuple-element.25), channel_id=1, source_target_pairs={{0,1},{1,0},{2,3},{3,2},{4,5},{5,4},{6,7},{7,6},{8,9},{9,8},{10,11... | collective-permute-start | bytes 393224 | tf_op jit(solution)/shard_map/ppermute | solution.py:240
  3.6 5.3 %collective-permute-start.1 = (bf16[256,128]{1,0:T(8,128)(2,1)S(1)}, bf16[256,128]{1,0:T(8,128)(2,1)S(1)}, u32[]{:S(2)}, u32[]{:S(2)}) collective-permute-start(bf16[256,128]{1,0:T(8,128)(2,1)S(1)} %get-tuple-element.27), channel_id=1, source_target_pairs={{0,2},{1,3},{2,0},{3,1},{4,6},{5,7},{6,4},{7,5},{8,10},{9,11},{10,... | collective-permute-start | bytes 196616 | tf_op jit(solution)/shard_map/ppermute | solution.py:240
  8.9 4.3 %collective-permute-start.2 = (bf16[256,128]{1,0:T(8,128)(2,1)S(1)}, bf16[256,128]{1,0:T(8,128)(2,1)S(1)}, u32[]{:S(2)}, u32[]{:S(2)}) collective-permute-start(bf16[256,128]{1,0:T(8,128)(2,1)S(1)} %get-tuple-element.29), channel_id=1, source_target_pairs={{0,4},{1,5},{2,6},{3,7},{4,0},{5,1},{6,2},{7,3},{8,12},{9,13},{10,... | collective-permute-start | bytes 196616 | tf_op jit(solution)/shard_map/ppermute | solution.py:240
  13.9 5.2 %collective-permute-start.3 = (bf16[256,128]{1,0:T(8,128)(2,1)S(1)}, bf16[256,128]{1,0:T(8,128)(2,1)S(1)}, u32[]{:S(2)}, u32[]{:S(2)}) collective-permute-start(bf16[256,128]{1,0:T(8,128)(2,1)S(1)} %get-tuple-element.31), channel_id=1, source_target_pairs={{0,8},{1,9},{2,10},{3,11},{4,12},{5,13},{6,14},{7,15},{8,0},{9,1},... | collective-permute-start | bytes 196616 | tf_op jit(solution)/shard_map/ppermute | solution.py:240
  19.1 4.3 %collective-permute-start.4 = (bf16[256,128]{1,0:T(8,128)(2,1)S(1)}, bf16[256,128]{1,0:T(8,128)(2,1)S(1)}, u32[]{:S(2)}, u32[]{:S(2)}) collective-permute-start(bf16[256,128]{1,0:T(8,128)(2,1)S(1)} %get-tuple-element.34), channel_id=1, source_target_pairs={{0,2},{1,3},{2,0},{3,1},{4,6},{5,7},{6,4},{7,5},{8,10},{9,11},{10,... | collective-permute-start | bytes 196616 | tf_op jit(solution)/shard_map/ppermute | solution.py:240
  23.5 8.5 %collective-permute-start.5 = (bf16[512,128]{1,0:T(8,128)(2,1)S(1)}, bf16[512,128]{1,0:T(8,128)(2,1)S(1)}, u32[]{:S(2)}, u32[]{:S(2)}) collective-permute-start(bf16[512,128]{1,0:T(8,128)(2,1)S(1)} %get-tuple-element.36), channel_id=1, source_target_pairs={{0,1},{1,0},{2,3},{3,2},{4,5},{5,4},{6,7},{7,6},{8,9},{9,8},{10,11... | collective-permute-start | bytes 393224 | tf_op jit(solution)/shard_map/ppermute | solution.py:240
  28.6 1.7 %copy-start = (f32[2048]{0:T(1024)S(1)}, f32[2048]{0:T(1024)}, u32[]{:S(2)}) copy-start(f32[2048]{0:T(1024)} %param.7) | copy-start | bytes 24580

commit v4 on v3

v4 whole, which is shorter than its diff:
```python
import functools

import jax
import jax.numpy as jnp
from jax import lax
from jax.experimental import pallas as pl
from jax.experimental.pallas import tpu as pltpu
from jax.sharding import PartitionSpec as P


HEAD_DIM = 64
PAIR = 2 * HEAD_DIM
QUAD = 4 * HEAD_DIM
EPS = 1e-05
AXIS = "seq"
BF16, F32 = jnp.bfloat16, jnp.float32


def core_bit():
    return lax.axis_index(AXIS) & 1


def side_bit():
    return (lax.axis_index(AXIS) >> 1) & 1


def aligned(index, by):
    return pl.multiple_of(index * by, by)


def first_lanes(shape):
    return lax.broadcasted_iota(jnp.int32, shape, len(shape) - 1) % PAIR < HEAD_DIM


def dot(a, b, dims):
    return lax.dot_general(a, b, (dims, ((), ())), preferred_element_type=F32)


def slot_start(slot, part):
    core, side = core_bit(), side_bit()
    quarter = 2 * (core if slot >= 2 else 1 - core) + (side if slot % 2 else 1 - side)
    return aligned(quarter, part)


def load_slot(src, dst, slot, at, part, sem):
    there, here = pl.ds(slot_start(slot, part), part), pl.ds(at * part, part)
    load = pltpu.make_async_copy(src.at[:, there], dst.at[:, here], sem)
    load.start()
    return load


def states_of(k_ref, v_ref, out_ref, at, part):
    first = first_lanes((HEAD_DIM, PAIR))
    base = at * part // PAIR * HEAD_DIM
    for quad in range(part // QUAD):
        lanes = pl.ds(at * part + quad * QUAD, QUAD)
        fk = jnp.maximum(k_ref[:, lanes], 0)
        full = dot(fk, v_ref[:, lanes], ((0,), (0,)))
        for p in range(2):
            top = p * PAIR
            rows = full[top : top + PAIR, top : top + PAIR]
            packed = jnp.where(first, rows[:HEAD_DIM], rows[HEAD_DIM:])
            out_ref[pl.ds(base + (quad * 2 + p) * HEAD_DIM, HEAD_DIM), :] = packed.astype(out_ref.dtype)


def state_kernel(k_hbm, v_hbm, *rest, slots, extra):
    sources, rest = rest[: len(extra)], rest[len(extra) :]
    state_ref, k_ref, v_ref, *more, sems, more_sems = rest
    part = k_ref.shape[1] // 2
    loads = []
    for at, slot in enumerate(slots):
        for n, (src, dst) in enumerate(((k_hbm, k_ref), (v_hbm, v_ref))):
            loads.append(load_slot(src, dst, slot, at, part, sems.at[at, n]))
    late = []
    for n, (src, dst, kind) in enumerate(zip(sources, more, extra)):
        if kind == "slots":
            for at, slot in enumerate(slots):
                late.append(load_slot(src, dst, slot, at, part, more_sems.at[n, at]))
        else:
            late.append(pltpu.make_async_copy(src, dst, more_sems.at[n, 0]))
            late[-1].start()
    for at in range(2):
        loads[2 * at].wait()
        loads[2 * at + 1].wait()
        states_of(k_ref, v_ref, state_ref, at, part)
    for load in late:
        load.wait()


def after_core(keep, got, send, own, ext):
    rows = own.shape[0]
    state, other = keep[...], got[...].astype(F32)
    both = state + other
    send[...] = both[:rows].astype(BF16)
    own[...] = both[rows:]
    ext[...] = jnp.where(core_bit() == 0, state, other)


def after_side(own, got, send, total, ext):
    value = own[...] + got[...].astype(F32)
    send[...] = value.astype(BF16)
    total[...] = value
    ext[...] = jnp.where(side_bit() == 0, own[...], got[...].astype(F32))


def upper_part(before, got, level):
    upper = (lax.axis_index(AXIS) >> level) & 1
    value = jnp.where(upper == 1, got[...].astype(F32), 0.0)
    return value if before is None else before[...] + value


def after_outer(refs, *, level, start, more):
    refs = list(refs)
    total = refs.pop(0)
    before = None if start else refs.pop(0)
    got, send, before_out, *total_out = refs
    new = total[...] + got[...].astype(F32)
    send[...] = new.astype(BF16)
    before_out[...] = upper_part(before, got, level)
    if more:
        total_out[0][...] = new


def after_last(refs, *, level, start):
    refs = list(refs)
    before = None if start else refs.pop(0)
    got, ext_side, ext_core, send, send_core, prior = refs
    value = upper_part(before, got, level)
    both = value + ext_side[...]
    first = side_bit() == 0
    send[...] = jnp.where(first, both, value).astype(BF16)
    split_cores(jnp.where(first, value, both), ext_core[value.shape[0] :, :], send_core, prior)


def split_cores(base, ext, send_core, prior):
    both = base + ext
    first = core_bit() == 0
    send_core[...] = jnp.where(first, both, base).astype(BF16)
    prior[...] = jnp.where(first, base, both).astype(BF16)


def after_base(got, ext_core, send_core, prior):
    split_cores(got[...].astype(F32), ext_core[: got.shape[0], :], send_core, prior)


def intra_kernel(refs, *, pairs, load):
    refs = list(refs)
    if load:
        q_hbm, q_hi, k_lo, v_lo, k_hi, v_hi, intra_ref, q_lo, sems = refs
        half = k_hi.shape[1]
        loads = [load_slot(q_hbm, q_lo, slot, slot, half // 2, sems.at[slot]) for slot in (1, 0)]
    else:
        q_lo, q_hi, k_lo, v_lo, k_hi, v_hi, intra_ref = refs
        half = k_hi.shape[1]
        loads = []
    count = intra_ref.shape[0]
    mid = count // 2
    first = first_lanes((count, PAIR))
    rows = lax.broadcasted_iota(jnp.int32, (mid, mid), 0)
    cols = lax.broadcasted_iota(jnp.int32, (mid, mid), 1)
    causal = cols <= rows
    for p in pairs:
        lanes = pl.ds((p - min(pairs)) * PAIR, PAIR)
        high = p * PAIR >= half
        q_ref, k_ref, v_ref = (q_hi, k_hi, v_hi) if high else (q_lo, k_lo, v_lo)
        if loads and not high:
            for copy in loads:
                copy.wait()
            loads = []
        there = pl.ds(p * PAIR % half, PAIR)
        fq = jnp.maximum(q_ref[:, there], 0)
        fk = jnp.maximum(k_ref[:, there], 0)
        val = v_ref[:, there]
        zero = jnp.zeros_like(fq)
        top, low, weights = [], [], []
        for h in range(2):
            mine = first if h == 0 else jnp.logical_not(first)
            mine_q = jnp.where(mine, fq, zero)
            s_top = dot(mine_q[:mid], fk[:mid], ((1,), (1,)))
            s_low = dot(mine_q[mid:], fk, ((1,), (1,)))
            s_top = jnp.where(causal, s_top, 0.0).astype(BF16)
            s_diag = jnp.where(causal, s_low[:, mid:], 0.0).astype(BF16)
            s_low = jnp.concatenate([s_low[:, :mid].astype(BF16), s_diag], axis=1)
            top.append(s_top)
            low.append(s_low)
            weights.append(jnp.where(mine, val, zero))
        w_top = jnp.concatenate([w[:mid] for w in weights], axis=0)
        intra_ref[:mid, lanes] = dot(jnp.concatenate(top, axis=1), w_top, ((1,), (0,)))
        w_low = jnp.concatenate(weights, axis=0)
        intra_ref[mid:, lanes] = dot(jnp.concatenate(low, axis=1), w_low, ((1,), (0,)))
    for copy in loads:
        copy.wait()


def final_kernel(refs, *, slot, places, aliased):
    refs = list(refs)
    prior_ref, q_ref, gain_ref = refs[:3]
    intra_refs = refs[3 : 3 + len(places)]
    out_hbm, out_buf, sems = refs[-3:]
    count, part = out_buf.shape
    base = slot_start(slot, part)
    lane = lax.broadcasted_iota(jnp.int32, (QUAD, QUAD), 1) // HEAD_DIM
    row = lax.broadcasted_iota(jnp.int32, (QUAD, QUAD), 0) // HEAD_DIM
    same = lane == row
    ones = jnp.where(same, 1.0 / HEAD_DIM, 0.0).astype(BF16)
    blocks = 2
    step = count // blocks
    copies = []
    for quad in range(part // QUAD):
        lanes = pl.ds(quad * QUAD, QUAD)
        one = prior_ref[pl.ds(quad * PAIR, HEAD_DIM), :]
        two = prior_ref[pl.ds(quad * PAIR + HEAD_DIM, HEAD_DIM), :]
        wide = jnp.concatenate([one, two], axis=1)
        block = jnp.concatenate([wide] * 4, axis=0)
        block = jnp.where(same, block, jnp.zeros_like(block))
        there = pl.ds(pl.multiple_of(base + quad * QUAD, QUAD), QUAD)
        gain = gain_ref[:, there]
        for n in range(blocks):
            tokens = pl.ds(n * step, step)
            fq = jnp.maximum(q_ref[tokens, pl.ds(slot % 2 * part + quad * QUAD, QUAD)], 0)
            intra = intra_refs[quad][tokens, pl.ds(places[quad], QUAD)]
            numer = dot(fq, block, ((1,), (0,))) + intra
            square = (numer * numer).astype(BF16)
            mean_sq = dot(square, ones, ((1,), (0,)))
            normed = numer * lax.rsqrt(mean_sq + EPS) * gain
            out_buf[tokens, lanes] = normed.astype(BF16)
            copies.append(
                pltpu.make_async_copy(out_buf.at[tokens, lanes], out_hbm.at[tokens, there], sems.at[quad, n])
            )
            copies[-1].start()
    for copy in copies:
        copy.wait()


ANY = pl.BlockSpec(memory_space=pl.ANY)
HBM = pl.BlockSpec(memory_space=pltpu.HBM)
VMEM = pl.BlockSpec(memory_space=pltpu.VMEM)
DMA = pltpu.SemaphoreType.DMA


def call(kernel, outs, args, specs=None, out_specs=None, scratch=(), alias=None, cost=(10_000, 10_000)):
    specs = [VMEM] * len(args) if specs is None else specs
    args = [a if s is ANY else pltpu.with_memory_space_constraint(a, s.memory_space) for a, s in zip(args, specs)]
    many = isinstance(outs, (tuple, list))
    return pl.pallas_call(
        kernel,
        out_shape=outs,
        in_specs=specs,
        out_specs=([VMEM] * len(outs) if many else VMEM) if out_specs is None else out_specs,
        scratch_shapes=scratch,
        input_output_aliases=alias or {},
        compiler_params=pltpu.CompilerParams(vmem_limit_bytes=12 * 2**20),
        cost_estimate=pl.CostEstimate(flops=cost[0], transcendentals=0, bytes_accessed=cost[1]),
    )(*args)


def packed(kernel, **static):
    return lambda *refs: kernel(refs, **static)


def on_device(queries, keys, values, gain, *, size):
    count, width = queries.shape
    half, part = width // 2, width // 4
    rows = half // PAIR * HEAD_DIM
    quarter = rows // 2
    columns = pltpu.VMEM((count, half), BF16)

    def swap(x, level):
        return lax.ppermute(x, AXIS, [(i, i ^ (1 << level)) for i in range(size)])

    def small(dtype, n=quarter):
        return pltpu.VMEM((n, PAIR), dtype)

    send, k_lo, v_lo = call(
        functools.partial(state_kernel, slots=(0, 1), extra=()),
        (small(BF16, rows), columns, columns),
        (keys, values),
        specs=[HBM] * 2,
        scratch=[DMA((2, 2)), DMA((1, 1))],
        cost=(150_000_000, 2_000_000),
    )
    got = swap(send, 0)
    keep, k_hi, v_hi, q_hi, gain_vmem = call(
        functools.partial(state_kernel, slots=(2, 3), extra=("slots", "whole")),
        (small(F32, rows), columns, columns, columns, pltpu.VMEM((1, width), F32)),
        (keys, values, queries, gain[None, :]),
        specs=[HBM] * 4,
        scratch=[DMA((2, 2)), DMA((2, 2))],
        cost=(150_000_000, 2_000_000),
    )
    pairs = width // PAIR
    cuts = (pairs // 2 + pairs // 8, pairs // 2 - pairs // 4, 0)
    groups = ((cuts[0], pairs), (cuts[1], cuts[0]), (cuts[2], cuts[1]))
    tiles = (k_lo, v_lo, k_hi, v_hi)
    q_lo, parts = queries, []
    for n, (low, high) in enumerate(groups):
        load = n == 1
        order = tuple(range(low, high)) if n != 1 else tuple(range(high - 1, low - 1, -1))
        buffer = pltpu.VMEM((count, (high - low) * PAIR), F32)
        outs = call(
            packed(intra_kernel, pairs=order, load=load) if n else packed(lambda r, **kw: intra_kernel((None, *r), **kw), pairs=order, load=False),
            (buffer, columns) if load else buffer,
            (q_lo, q_hi, *tiles) if n else (q_hi, *tiles),
            specs=[HBM] + [VMEM] * 5 if load else None,
            scratch=[DMA((2,))] if load else (),
            cost=(200_000_000, 1_500_000),
        )
        if load:
            outs, q_lo = outs
        parts.append(outs)

    send, own, ext_core = call(after_core, (small(BF16), small(F32), small(F32, rows)), (keep, got))
    got = swap(send, 1)
    send, total, ext_side = call(after_side, (small(BF16), small(F32), small(F32)), (own, got))
    before = []
    level = 2
    while 1 << level < size:
        got = swap(send, level)
        if 1 << (level + 1) < size:
            more = 1 << (level + 2) < size
            send, *before = call(
                packed(after_outer, level=level, start=not before, more=more),
                (small(BF16), *[small(F32)] * (1 + more)),
                [total, *before, got],
            )
            if more:
                total = before.pop()
        else:
            send, send_core, prior3 = call(
                packed(after_last, level=level, start=not before),
                (small(BF16), small(BF16), small(BF16)),
                [*before, got, ext_side, ext_core],
            )
        level += 1
    got = swap(send, 1)
    prior1 = swap(send_core, 0)
    send_core, prior2 = call(after_base, (small(BF16), small(BF16)), (got, ext_core))
    prior0 = swap(send_core, 0)

    out = None
    for slot, prior in ((3, prior3), (1, prior1), (2, prior2), (0, prior0)):
        used, places = [], []
        for quad in range(part // QUAD):
            pair = (slot * part + quad * QUAD) // PAIR
            n = next(i for i, (low, high) in enumerate(groups) if low <= pair < high)
            used.append(parts[n])
            places.append((pair - groups[n][0]) * PAIR)
        args = [prior, q_hi if slot >= 2 else q_lo, gain_vmem, *used]
        specs = [VMEM] * len(args)
        if out is not None:
            args.append(out)
            specs.append(ANY)
        out = call(
            packed(final_kernel, slot=slot, places=tuple(places), aliased=out is not None),
            jax.ShapeDtypeStruct((count, width), BF16),
            args,
            specs=specs,
            out_specs=ANY,
            scratch=[pltpu.VMEM((count, part), BF16), DMA((part // QUAD, 2))],
            alias={} if out is None else {len(args) - 1: 0},
            cost=(50_000_000, 1_000_000),
        )
    return out


def solution(mesh):
    return jax.shard_map(
        functools.partial(on_device, size=mesh.shape[AXIS]),
        mesh=mesh,
        in_specs=(
            P(("groups", "seq"), None),
            P(("groups", "seq"), None),
            P(("groups", "seq"), None),
            P(),
        ),
        out_specs=P(("groups", "seq"), None),
        check_vma=False,
    )
```

time: 33.8 us -> 32.8 us (0.970)
  Pallas kernels: 13.8 us -> 12.6 us
    pallas_call x13 -> x14, Pallas kernels: 13.8 us -> 12.6 us  [call(): pl.pallas_call(kernel, out_shape=outs, in_specs=specs, out_specs=([VMEM]...]
    ppermute x6 -> x7, starting transfers between devices: 9.69 us -> 9.77 us  [swap(): return lax.ppermute(x, AXIS, [(i, i ^ 1 << level) for i in range(size)])]
    ppermute x6 -> x7, waiting for transfers between devices: 10.1 us -> 10.1 us  [swap(): return lax.ppermute(x, AXIS, [(i, i ^ 1 << level) for i in range(size)])]
  transfers between devices with their start and end apart: 6 -> 7, of which waited for: 4 -> 4; matrix products, arithmetic and copies ran while one was open for 0% -> 0% of each run, Pallas kernels for 29% -> 30%
where the time goes in v4:
time: 32.8 us; the launch traced here: 32.6 us
  Pallas kernels  12.6 us (38%)
  waiting for transfers between devices  10.1 us (31%)
  starting transfers between devices  9.77 us (30%)
    pallas_call x14, Pallas kernels, call(): pl.pallas_call(kernel, out_shape=outs, in_specs=specs, out_specs=([VMEM]...  12.6 us
    ppermute x7, waiting for transfers between devices, swap(): return lax.ppermute(x, AXIS, [(i, i ^ 1 << level) for i in range(size)])  10.1 us
    ppermute x7, starting transfers between devices, swap(): return lax.ppermute(x, AXIS, [(i, i ^ 1 << level) for i in range(size)])  9.77 us
  transfers between devices with their start and end apart: 7, of which 4 were waited for; matrix products, arithmetic and copies ran while one was open for 0% of the time, Pallas kernels for 30%

profile of v4, /device:TPU:0, one launch (start us, length us, event | category | flops | bytes accessed | tf_op | source)
XLA Modules:
  0.0 32.6 jit_solution(11535240195621765454)
XLA Ops:
  0.0 1.6 %shard_map.47 = (bf16[512,128]{1,0:T(8,128)(2,1)S(1)}, bf16[256,1024]{1,0:T(8,128)(2,1)S(1)}, bf16[256,1024]{1,0:T(8,128)(2,1)S(1)}) custom-call(bf16[256,2048]{1,0:T(8,128)(2,1)} %k_hbm.3, bf16[256,2048]{1,0:T(8,128)(2,1)} %v_hbm.3), custom_call_target="tpu_custom_call" | custom-call | flops 150000000 | bytes 2000000 | tf_op jit(solution)/shard_map/pallas_call | solution.py:245
  1.6 0.6 %collective-permute-start = (bf16[512,128]{1,0:T(8,128)(2,1)S(1)}, bf16[512,128]{1,0:T(8,128)(2,1)S(1)}, u32[]{:S(2)}, u32[]{:S(2)}) collective-permute-start(bf16[512,128]{1,0:T(8,128)(2,1)S(1)} %get-tuple-element.29), channel_id=1, source_target_pairs={{0,1},{1,0},{2,3},{3,2},{4,5},{5,4},{6,7},{7,6},{8,9},{9,8},{10,11... | collective-permute-start | bytes 393224 | tf_op jit(solution)/shard_map/ppermute | solution.py:269
  2.2 1.7 %shard_map.46 = (f32[512,128]{1,0:T(8,128)S(1)}, bf16[256,1024]{1,0:T(8,128)(2,1)S(1)}, bf16[256,1024]{1,0:T(8,128)(2,1)S(1)}, bf16[256,1024]{1,0:T(8,128)(2,1)S(1)}, f32[1,2048]{1,0:T(1,128)S(1)}) custom-call(bf16[256,2048]{1,0:T(8,128)(2,1)} %k_hbm.3, bf16[256,2048]{1,0:T(8,128)(2,1)} %v_hbm.3, bf16[256,2048]{1,0:T(8,128)(2,1)} %refs_0_.1, f32[1,2048]{1,0:T(1,128)} %bitcast.1), custom_call_target="tpu_custom_call" | custom-call | flops 150000000 | bytes 2000000 | tf_op jit(solution)/shard_map/pallas_call | solution.py:245
  3.9 0.0 collective-permute-done.got
  3.9 0.1 shard_map.48
  4.0 2.6 %collective-permute-start.1 = (bf16[256,128]{1,0:T(8,128)(2,1)S(1)}, bf16[256,128]{1,0:T(8,128)(2,1)S(1)}, u32[]{:S(2)}, u32[]{:S(2)}) collective-permute-start(bf16[256,128]{1,0:T(8,128)(2,1)S(1)} %get-tuple-element.31), channel_id=1, source_target_pairs={{0,2},{1,3},{2,0},{3,1},{4,6},{5,7},{6,4},{7,5},{8,10},{9,11},{10,... | collective-permute-start | bytes 196616 | tf_op jit(solution)/shard_map/ppermute | solution.py:269
  6.6 2.7 %collective-permute-done.1.got = bf16[256,128]{1,0:T(8,128)(2,1)S(1)} collective-permute-done((bf16[256,128]{1,0:T(8,128)(2,1)S(1)}, bf16[256,128]{1,0:T(8,128)(2,1)S(1)}, u32[]{:S(2)}, u32[]{:S(2)}) %collective-permute-start.1) | collective-permute-done | bytes 65568 | tf_op jit(solution)/shard_map/ppermute | solution.py:269
  9.3 1.9 %collective-permute-start.2 = (bf16[256,128]{1,0:T(8,128)(2,1)S(1)}, bf16[256,128]{1,0:T(8,128)(2,1)S(1)}, u32[]{:S(2)}, u32[]{:S(2)}) collective-permute-start(bf16[256,128]{1,0:T(8,128)(2,1)S(1)} %get-tuple-element.33), channel_id=1, source_target_pairs={{0,4},{1,5},{2,6},{3,7},{4,0},{5,1},{6,2},{7,3},{8,12},{9,13},{10,... | collective-permute-start | bytes 196616 | tf_op jit(solution)/shard_map/ppermute | solution.py:269
  11.2 2.5 %collective-permute-done.2.refs_1_ = bf16[256,128]{1,0:T(8,128)(2,1)S(1)} collective-permute-done((bf16[256,128]{1,0:T(8,128)(2,1)S(1)}, bf16[256,128]{1,0:T(8,128)(2,1)S(1)}, u32[]{:S(2)}, u32[]{:S(2)}) %collective-permute-start.2) | collective-permute-done | bytes 65568 | tf_op jit(solution)/shard_map/ppermute | solution.py:269
  13.7 2.9 %collective-permute-start.3 = (bf16[256,128]{1,0:T(8,128)(2,1)S(1)}, bf16[256,128]{1,0:T(8,128)(2,1)S(1)}, u32[]{:S(2)}, u32[]{:S(2)}) collective-permute-start(bf16[256,128]{1,0:T(8,128)(2,1)S(1)} %get-tuple-element.35), channel_id=1, source_target_pairs={{0,8},{1,9},{2,10},{3,11},{4,12},{5,13},{6,14},{7,15},{8,0},{9,1},... | collective-permute-start | bytes 196616 | tf_op jit(solution)/shard_map/ppermute | solution.py:269
  16.6 2.4 %collective-permute-done.3.refs_1_ = bf16[256,128]{1,0:T(8,128)(2,1)S(1)} collective-permute-done((bf16[256,128]{1,0:T(8,128)(2,1)S(1)}, bf16[256,128]{1,0:T(8,128)(2,1)S(1)}, u32[]{:S(2)}, u32[]{:S(2)}) %collective-permute-start.3) | collective-permute-done | bytes 65568 | tf_op jit(solution)/shard_map/ppermute | solution.py:269
  18.9 0.1 shard_map.51
  19.0 1.8 %collective-permute-start.4 = (bf16[256,128]{1,0:T(8,128)(2,1)S(1)}, bf16[256,128]{1,0:T(8,128)(2,1)S(1)}, u32[]{:S(2)}, u32[]{:S(2)}) collective-permute-start(bf16[256,128]{1,0:T(8,128)(2,1)S(1)} %get-tuple-element.38), channel_id=1, source_target_pairs={{0,2},{1,3},{2,0},{3,1},{4,6},{5,7},{6,4},{7,5},{8,10},{9,11},{10,... | collective-permute-start | bytes 196616 | tf_op jit(solution)/shard_map/ppermute | solution.py:269
  20.8 0.0 collective-permute-start.6
  20.8 2.5 %collective-permute-done.4.got = bf16[256,128]{1,0:T(8,128)(2,1)S(1)} collective-permute-done((bf16[256,128]{1,0:T(8,128)(2,1)S(1)}, bf16[256,128]{1,0:T(8,128)(2,1)S(1)}, u32[]{:S(2)}, u32[]{:S(2)}) %collective-permute-start.4) | collective-permute-done | bytes 65568 | tf_op jit(solution)/shard_map/ppermute | solution.py:269
  23.3 0.1 collective-permute-start.5
  23.4 2.4 %shard_map.53 = (f32[256,768]{1,0:T(8,128)S(1)}, bf16[256,1024]{1,0:T(8,128)(2,1)S(1)}) custom-call(bf16[256,2048]{1,0:T(8,128)(2,1)} %refs_0_.1, bf16[256,1024]{1,0:T(8,128)(2,1)S(1)} %get-tuple-element.40.refs_1_.refs_0_, bf16[256,1024]{1,0:T(8,128)(2,1)S(1)} %get-tuple-element.41.refs_2_.refs_1_, bf16[256,1024]{1,0:T(8,128)(2,1)S(1)} %get-tuple-element.42.refs_3_.refs_2_, ...), custom_call_target="tpu_custom_call" | custom-call | flops 200000000 | bytes 1500000 | tf_op jit(solution)/shard_map/pallas_call | solution.py:245
  25.8 1.4 %shard_map.55.refs_3_.refs_4_ = f32[256,768]{1,0:T(8,128)S(1)} custom-call(bf16[256,1024]{1,0:T(8,128)(2,1)S(1)} %get-tuple-element.40.refs_1_.refs_0_, bf16[256,1024]{1,0:T(8,128)(2,1)S(1)} %get-tuple-element.41.refs_2_.refs_1_, bf16[256,1024]{1,0:T(8,128)(2,1)S(1)} %get-tuple-element.42.refs_3_.refs_2_, ...), custom_call_target="tpu_custom_call" | custom-call | flops 200000000 | bytes 1500000 | tf_op jit(solution)/shard_map/pallas_call | solution.py:245
  27.2 1.0 %shard_map.54.refs_3_.refs_4_ = f32[256,512]{1,0:T(8,128)S(1)} custom-call(bf16[256,1024]{1,0:T(8,128)(2,1)S(1)} %get-tuple-element.45.refs_0_.refs_1_, bf16[256,1024]{1,0:T(8,128)(2,1)S(1)} %get-tuple-element.40.refs_1_.refs_0_, bf16[256,1024]{1,0:T(8,128)(2,1)S(1)} %get-tuple-element.41.refs_2_.refs_1_, ...), custom_call_target="tpu_custom_call" | custom-call | flops 200000000 | bytes 1500000 | tf_op jit(solution)/shard_map/pallas_call | solution.py:245
  28.2 1.1 %shard_map.56.refs_5_ = bf16[256,2048]{1,0:T(8,128)(2,1)} custom-call(bf16[256,128]{1,0:T(8,128)(2,1)S(1)} %get-tuple-element.50.refs_0_, bf16[256,1024]{1,0:T(8,128)(2,1)S(1)} %get-tuple-element.40.refs_1_.refs_0_, f32[1,2048]{1,0:T(1,128)S(1)} %get-tuple-element.46.refs_2_, f32[256,768]{1,0:T(8,128)S(1)} %shard_map.55.refs_3_.refs_4_, ...), custom_call_target="tpu_custom_call" | custom-call | flops 50000000 | bytes 1000000 | tf_op jit(solution)/shard_map/pallas_call | solution.py:245
  29.3 0.0 collective-permute-done.6.refs_0_
  29.3 1.1 %shard_map.57.refs_5_ = bf16[256,2048]{1,0:T(8,128)(2,1)} custom-call(bf16[256,128]{1,0:T(8,128)(2,1)S(1)} %collective-permute-done.6.refs_0_, bf16[256,1024]{1,0:T(8,128)(2,1)S(1)} %get-tuple-element.45.refs_0_.refs_1_, f32[1,2048]{1,0:T(1,128)S(1)} %get-tuple-element.46.refs_2_, ...), custom_call_target="tpu_custom_call", output_to_operand_aliasing={{}: (5, {})} | custom-call | flops 50000000 | bytes 1000000 | tf_op jit(solution)/shard_map/pallas_call | solution.py:245
  30.4 1.1 %shard_map.58.refs_5_ = bf16[256,2048]{1,0:T(8,128)(2,1)} custom-call(bf16[256,128]{1,0:T(8,128)(2,1)S(1)} %get-tuple-element.47.refs_0_, bf16[256,1024]{1,0:T(8,128)(2,1)S(1)} %get-tuple-element.40.refs_1_.refs_0_, f32[1,2048]{1,0:T(1,128)S(1)} %get-tuple-element.46.refs_2_, ...), custom_call_target="tpu_custom_call", output_to_operand_aliasing={{}: (5, {})} | custom-call | flops 50000000 | bytes 1000000 | tf_op jit(solution)/shard_map/pallas_call | solution.py:245
  31.5 0.0 collective-permute-done.5.refs_0_
  31.5 1.1 %shard_map.59 = bf16[256,2048]{1,0:T(8,128)(2,1)} custom-call(bf16[256,128]{1,0:T(8,128)(2,1)S(1)} %collective-permute-done.5.refs_0_, bf16[256,1024]{1,0:T(8,128)(2,1)S(1)} %get-tuple-element.45.refs_0_.refs_1_, f32[1,2048]{1,0:T(1,128)S(1)} %get-tuple-element.46.refs_2_, f32[256,512]{1,0:T(8,128)S(1)} %shard_map.54.refs_3_.refs_4_, ...), custom_call_target="tpu_custom_call", output_to_operand_aliasing={{}: (5, {})} | custom-call | flops 50000000 | bytes 1000000 | tf_op jit(solution)/shard_map/pallas_call | solution.py:245
  (3 shorter events, 0.1 us)
Async XLA Ops:
  1.6 2.3 %collective-permute-start = (bf16[512,128]{1,0:T(8,128)(2,1)S(1)}, bf16[512,128]{1,0:T(8,128)(2,1)S(1)}, u32[]{:S(2)}, u32[]{:S(2)}) collective-permute-start(bf16[512,128]{1,0:T(8,128)(2,1)S(1)} %get-tuple-element.29), channel_id=1, source_target_pairs={{0,1},{1,0},{2,3},{3,2},{4,5},{5,4},{6,7},{7,6},{8,9},{9,8},{10,11... | collective-permute-start | bytes 393224 | tf_op jit(solution)/shard_map/ppermute | solution.py:269
  4.0 5.3 %collective-permute-start.1 = (bf16[256,128]{1,0:T(8,128)(2,1)S(1)}, bf16[256,128]{1,0:T(8,128)(2,1)S(1)}, u32[]{:S(2)}, u32[]{:S(2)}) collective-permute-start(bf16[256,128]{1,0:T(8,128)(2,1)S(1)} %get-tuple-element.31), channel_id=1, source_target_pairs={{0,2},{1,3},{2,0},{3,1},{4,6},{5,7},{6,4},{7,5},{8,10},{9,11},{10,... | collective-permute-start | bytes 196616 | tf_op jit(solution)/shard_map/ppermute | solution.py:269
  9.3 4.3 %collective-permute-start.2 = (bf16[256,128]{1,0:T(8,128)(2,1)S(1)}, bf16[256,128]{1,0:T(8,128)(2,1)S(1)}, u32[]{:S(2)}, u32[]{:S(2)}) collective-permute-start(bf16[256,128]{1,0:T(8,128)(2,1)S(1)} %get-tuple-element.33), channel_id=1, source_target_pairs={{0,4},{1,5},{2,6},{3,7},{4,0},{5,1},{6,2},{7,3},{8,12},{9,13},{10,... | collective-permute-start | bytes 196616 | tf_op jit(solution)/shard_map/ppermute | solution.py:269
  13.7 5.2 %collective-permute-start.3 = (bf16[256,128]{1,0:T(8,128)(2,1)S(1)}, bf16[256,128]{1,0:T(8,128)(2,1)S(1)}, u32[]{:S(2)}, u32[]{:S(2)}) collective-permute-start(bf16[256,128]{1,0:T(8,128)(2,1)S(1)} %get-tuple-element.35), channel_id=1, source_target_pairs={{0,8},{1,9},{2,10},{3,11},{4,12},{5,13},{6,14},{7,15},{8,0},{9,1},... | collective-permute-start | bytes 196616 | tf_op jit(solution)/shard_map/ppermute | solution.py:269
  19.0 4.3 %collective-permute-start.4 = (bf16[256,128]{1,0:T(8,128)(2,1)S(1)}, bf16[256,128]{1,0:T(8,128)(2,1)S(1)}, u32[]{:S(2)}, u32[]{:S(2)}) collective-permute-start(bf16[256,128]{1,0:T(8,128)(2,1)S(1)} %get-tuple-element.38), channel_id=1, source_target_pairs={{0,2},{1,3},{2,0},{3,1},{4,6},{5,7},{6,4},{7,5},{8,10},{9,11},{10,... | collective-permute-start | bytes 196616 | tf_op jit(solution)/shard_map/ppermute | solution.py:269
  20.8 8.5 %collective-permute-start.6 = (bf16[256,128]{1,0:T(8,128)(2,1)S(1)}, bf16[256,128]{1,0:T(8,128)(2,1)S(1)}, u32[]{:S(2)}, u32[]{:S(2)}) collective-permute-start(bf16[256,128]{1,0:T(8,128)(2,1)S(1)} %get-tuple-element.49), channel_id=1, source_target_pairs={{0,1},{1,0},{2,3},{3,2},{4,5},{5,4},{6,7},{7,6},{8,9},{9,8},{10,11... | collective-permute-start | bytes 196616 | tf_op jit(solution)/shard_map/ppermute | solution.py:269
  23.3 8.1 %collective-permute-start.5 = (bf16[256,128]{1,0:T(8,128)(2,1)S(1)}, bf16[256,128]{1,0:T(8,128)(2,1)S(1)}, u32[]{:S(2)}, u32[]{:S(2)}) collective-permute-start(bf16[256,128]{1,0:T(8,128)(2,1)S(1)} %get-tuple-element.39), channel_id=1, source_target_pairs={{0,1},{1,0},{2,3},{3,2},{4,5},{5,4},{6,7},{7,6},{8,9},{9,8},{10,11... | collective-permute-start | bytes 196616 | tf_op jit(solution)/shard_map/ppermute | solution.py:269

commit v5 on v4

--- a/solution.py
+++ b/solution.py
@@ -63,27 +63,28 @@
             out_ref[pl.ds(base + (quad * 2 + p) * HEAD_DIM, HEAD_DIM), :] = packed.astype(out_ref.dtype)
 
 
-def state_kernel(k_hbm, v_hbm, *rest, slots, extra):
-    sources, rest = rest[: len(extra)], rest[len(extra) :]
-    state_ref, k_ref, v_ref, *more, sems, more_sems = rest
+def send_kernel(k_hbm, v_hbm, send_ref, k_lo, v_lo, k_hi, v_hi, sems):
+    part = k_lo.shape[1] // 2
+    loads = []
+    for slot in range(4):
+        for n, (src, dst) in enumerate(((k_hbm, k_lo if slot < 2 else k_hi), (v_hbm, v_lo if slot < 2 else v_hi))):
+            loads.append(load_slot(src, dst, slot, slot % 2, part, sems.at[slot, n]))
+    for slot in range(2):
+        loads[2 * slot].wait()
+        loads[2 * slot + 1].wait()
+        states_of(k_lo, v_lo, send_ref, slot, part)
+    for load in loads[4:]:
+        load.wait()
+
+
+def keep_kernel(k_ref, v_ref, q_hbm, gain_hbm, keep_ref, q_ref, gain_ref, sems):
     part = k_ref.shape[1] // 2
-    loads = []
-    for at, slot in enumerate(slots):
-        for n, (src, dst) in enumerate(((k_hbm, k_ref), (v_hbm, v_ref))):
-            loads.append(load_slot(src, dst, slot, at, part, sems.at[at, n]))
-    late = []
-    for n, (src, dst, kind) in enumerate(zip(sources, more, extra)):
-        if kind == "slots":
-            for at, slot in enumerate(slots):
-                late.append(load_slot(src, dst, slot, at, part, more_sems.at[n, at]))
-        else:
-            late.append(pltpu.make_async_copy(src, dst, more_sems.at[n, 0]))
-            late[-1].start()
+    loads = [load_slot(q_hbm, q_ref, 2 + at, at, part, sems.at[at]) for at in range(2)]
+    loads.append(pltpu.make_async_copy(gain_hbm, gain_ref, sems.at[2]))
+    loads[-1].start()
     for at in range(2):
-        loads[2 * at].wait()
-        loads[2 * at + 1].wait()
-        states_of(k_ref, v_ref, state_ref, at, part)
-    for load in late:
+        states_of(k_ref, v_ref, keep_ref, at, part)
+    for load in loads:
         load.wait()
 
 
@@ -271,27 +272,26 @@
     def small(dtype, n=quarter):
         return pltpu.VMEM((n, PAIR), dtype)
 
-    send, k_lo, v_lo = call(
-        functools.partial(state_kernel, slots=(0, 1), extra=()),
-        (small(BF16, rows), columns, columns),
+    send, *tiles = call(
+        send_kernel,
+        (small(BF16, rows), *[columns] * 4),
         (keys, values),
         specs=[HBM] * 2,
-        scratch=[DMA((2, 2)), DMA((1, 1))],
+        scratch=[DMA((4, 2))],
         cost=(150_000_000, 2_000_000),
     )
     got = swap(send, 0)
-    keep, k_hi, v_hi, q_hi, gain_vmem = call(
-        functools.partial(state_kernel, slots=(2, 3), extra=("slots", "whole")),
-        (small(F32, rows), columns, columns, columns, pltpu.VMEM((1, width), F32)),
-        (keys, values, queries, gain[None, :]),
-        specs=[HBM] * 4,
-        scratch=[DMA((2, 2)), DMA((2, 2))],
+    keep, q_hi, gain_vmem = call(
+        keep_kernel,
+        (small(F32, rows), columns, pltpu.VMEM((1, width), F32)),
+        (*tiles[2:], queries, gain[None, :]),
+        specs=[VMEM] * 2 + [HBM] * 2,
+        scratch=[DMA((3,))],
         cost=(150_000_000, 2_000_000),
     )
     pairs = width // PAIR
     cuts = (pairs // 2 + pairs // 8, pairs // 2 - pairs // 4, 0)
     groups = ((cuts[0], pairs), (cuts[1], cuts[0]), (cuts[2], cuts[1]))
-    tiles = (k_lo, v_lo, k_hi, v_hi)
     q_lo, parts = queries, []
     for n, (low, high) in enumerate(groups):
         load = n == 1

time: 32.8 us -> 32.3 us (0.985)
  Pallas kernels: 12.6 us -> 12.1 us
    pallas_call x14, Pallas kernels: 12.6 us -> 12.1 us  [call(): pl.pallas_call(kernel, out_shape=outs, in_specs=specs, out_specs=([VMEM]...]
  transfers between devices with their start and end apart: 7 -> 7, of which waited for: 4 -> 4; matrix products, arithmetic and copies ran while one was open for 0% -> 0% of each run, Pallas kernels for 30% -> 29%
where the time goes in v5:
time: 32.3 us; the launch traced here: 32.1 us
  Pallas kernels  12.1 us (37%)
  waiting for transfers between devices  9.99 us (31%)
  starting transfers between devices  9.87 us (31%)
    pallas_call x14, Pallas kernels, call(): pl.pallas_call(kernel, out_shape=outs, in_specs=specs, out_specs=([VMEM]...  12.1 us
    ppermute x7, waiting for transfers between devices, swap(): return lax.ppermute(x, AXIS, [(i, i ^ 1 << level) for i in range(size)])  9.99 us
    ppermute x7, starting transfers between devices, swap(): return lax.ppermute(x, AXIS, [(i, i ^ 1 << level) for i in range(size)])  9.87 us
  transfers between devices with their start and end apart: 7, of which 4 were waited for; matrix products, arithmetic and copies ran while one was open for 0% of the time, Pallas kernels for 29%

profile of v5, /device:TPU:0, one launch (start us, length us, event | category | flops | bytes accessed | tf_op | source)
XLA Modules:
  0.0 32.1 jit_solution(7297551873435539032)
XLA Ops:
  0.0 1.7 %shard_map.46 = (bf16[512,128]{1,0:T(8,128)(2,1)S(1)}, bf16[256,1024]{1,0:T(8,128)(2,1)S(1)}, bf16[256,1024]{1,0:T(8,128)(2,1)S(1)}, bf16[256,1024]{1,0:T(8,128)(2,1)S(1)}, bf16[256,1024]{1,0:T(8,128)(2,1)S(1)}) custom-call(bf16[256,2048]{1,0:T(8,128)(2,1)} %k_hbm.1, bf16[256,2048]{1,0:T(8,128)(2,1)} %v_hbm.1), custom_call_target="tpu_custom_call" | custom-call | flops 150000000 | bytes 2000000 | tf_op jit(solution)/shard_map/pallas_call | solution.py:246
  1.7 0.6 %collective-permute-start = (bf16[512,128]{1,0:T(8,128)(2,1)S(1)}, bf16[512,128]{1,0:T(8,128)(2,1)S(1)}, u32[]{:S(2)}, u32[]{:S(2)}) collective-permute-start(bf16[512,128]{1,0:T(8,128)(2,1)S(1)} %get-tuple-element.31), channel_id=1, source_target_pairs={{0,1},{1,0},{2,3},{3,2},{4,5},{5,4},{6,7},{7,6},{8,9},{9,8},{10,11... | collective-permute-start | bytes 393224 | tf_op jit(solution)/shard_map/ppermute | solution.py:270
  2.2 1.2 %shard_map.47 = (f32[512,128]{1,0:T(8,128)S(1)}, bf16[256,1024]{1,0:T(8,128)(2,1)S(1)}, f32[1,2048]{1,0:T(1,128)S(1)}) custom-call(bf16[256,1024]{1,0:T(8,128)(2,1)S(1)} %get-tuple-element.28.k_ref.refs_4_.refs_3_, bf16[256,1024]{1,0:T(8,128)(2,1)S(1)} %get-tuple-element.29.v_ref.refs_5_.refs_4_, bf16[256,2048]{1,0:T(8,128)(2,1)} %refs_0_.1, f32[1,2048]{1,0:T(1,128)} %bitcast.1), custom_call_target="tpu_custom_call" | custom-call | flops 150000000 | bytes 2000000 | tf_op jit(solution)/shard_map/pallas_call | solution.py:246
  3.4 0.0 collective-permute-done.got
  3.4 0.1 shard_map.48
  3.5 2.7 %collective-permute-start.1 = (bf16[256,128]{1,0:T(8,128)(2,1)S(1)}, bf16[256,128]{1,0:T(8,128)(2,1)S(1)}, u32[]{:S(2)}, u32[]{:S(2)}) collective-permute-start(bf16[256,128]{1,0:T(8,128)(2,1)S(1)} %get-tuple-element.33), channel_id=1, source_target_pairs={{0,2},{1,3},{2,0},{3,1},{4,6},{5,7},{6,4},{7,5},{8,10},{9,11},{10,... | collective-permute-start | bytes 196616 | tf_op jit(solution)/shard_map/ppermute | solution.py:270
  6.2 2.6 %collective-permute-done.1.got = bf16[256,128]{1,0:T(8,128)(2,1)S(1)} collective-permute-done((bf16[256,128]{1,0:T(8,128)(2,1)S(1)}, bf16[256,128]{1,0:T(8,128)(2,1)S(1)}, u32[]{:S(2)}, u32[]{:S(2)}) %collective-permute-start.1) | collective-permute-done | bytes 65568 | tf_op jit(solution)/shard_map/ppermute | solution.py:270
  8.9 1.9 %collective-permute-start.2 = (bf16[256,128]{1,0:T(8,128)(2,1)S(1)}, bf16[256,128]{1,0:T(8,128)(2,1)S(1)}, u32[]{:S(2)}, u32[]{:S(2)}) collective-permute-start(bf16[256,128]{1,0:T(8,128)(2,1)S(1)} %get-tuple-element.35), channel_id=1, source_target_pairs={{0,4},{1,5},{2,6},{3,7},{4,0},{5,1},{6,2},{7,3},{8,12},{9,13},{10,... | collective-permute-start | bytes 196616 | tf_op jit(solution)/shard_map/ppermute | solution.py:270
  10.7 2.5 %collective-permute-done.2.refs_1_ = bf16[256,128]{1,0:T(8,128)(2,1)S(1)} collective-permute-done((bf16[256,128]{1,0:T(8,128)(2,1)S(1)}, bf16[256,128]{1,0:T(8,128)(2,1)S(1)}, u32[]{:S(2)}, u32[]{:S(2)}) %collective-permute-start.2) | collective-permute-done | bytes 65568 | tf_op jit(solution)/shard_map/ppermute | solution.py:270
  13.2 2.9 %collective-permute-start.3 = (bf16[256,128]{1,0:T(8,128)(2,1)S(1)}, bf16[256,128]{1,0:T(8,128)(2,1)S(1)}, u32[]{:S(2)}, u32[]{:S(2)}) collective-permute-start(bf16[256,128]{1,0:T(8,128)(2,1)S(1)} %get-tuple-element.37), channel_id=1, source_target_pairs={{0,8},{1,9},{2,10},{3,11},{4,12},{5,13},{6,14},{7,15},{8,0},{9,1},... | collective-permute-start | bytes 196616 | tf_op jit(solution)/shard_map/ppermute | solution.py:270
  16.1 2.4 %collective-permute-done.3.refs_1_ = bf16[256,128]{1,0:T(8,128)(2,1)S(1)} collective-permute-done((bf16[256,128]{1,0:T(8,128)(2,1)S(1)}, bf16[256,128]{1,0:T(8,128)(2,1)S(1)}, u32[]{:S(2)}, u32[]{:S(2)}) %collective-permute-start.3) | collective-permute-done | bytes 65568 | tf_op jit(solution)/shard_map/ppermute | solution.py:270
  18.4 0.1 shard_map.51
  18.5 1.8 %collective-permute-start.4 = (bf16[256,128]{1,0:T(8,128)(2,1)S(1)}, bf16[256,128]{1,0:T(8,128)(2,1)S(1)}, u32[]{:S(2)}, u32[]{:S(2)}) collective-permute-start(bf16[256,128]{1,0:T(8,128)(2,1)S(1)} %get-tuple-element.40), channel_id=1, source_target_pairs={{0,2},{1,3},{2,0},{3,1},{4,6},{5,7},{6,4},{7,5},{8,10},{9,11},{10,... | collective-permute-start | bytes 196616 | tf_op jit(solution)/shard_map/ppermute | solution.py:270
  20.3 0.0 collective-permute-start.6
  20.3 2.5 %collective-permute-done.4.got = bf16[256,128]{1,0:T(8,128)(2,1)S(1)} collective-permute-done((bf16[256,128]{1,0:T(8,128)(2,1)S(1)}, bf16[256,128]{1,0:T(8,128)(2,1)S(1)}, u32[]{:S(2)}, u32[]{:S(2)}) %collective-permute-start.4) | collective-permute-done | bytes 65568 | tf_op jit(solution)/shard_map/ppermute | solution.py:270
  22.9 0.1 collective-permute-start.5
  22.9 2.4 %shard_map.53 = (f32[256,768]{1,0:T(8,128)S(1)}, bf16[256,1024]{1,0:T(8,128)(2,1)S(1)}) custom-call(bf16[256,2048]{1,0:T(8,128)(2,1)} %refs_0_.1, bf16[256,1024]{1,0:T(8,128)(2,1)S(1)} %get-tuple-element.42.refs_1_.refs_0_, bf16[256,1024]{1,0:T(8,128)(2,1)S(1)} %get-tuple-element.43.refs_2_.refs_1_, bf16[256,1024]{1,0:T(8,128)(2,1)S(1)} %get-tuple-element.44.refs_3_.refs_2_, ...), custom_call_target="tpu_custom_call" | custom-call | flops 200000000 | bytes 1500000 | tf_op jit(solution)/shard_map/pallas_call | solution.py:246
  25.3 1.4 %shard_map.55.refs_3_.refs_4_ = f32[256,768]{1,0:T(8,128)S(1)} custom-call(bf16[256,1024]{1,0:T(8,128)(2,1)S(1)} %get-tuple-element.42.refs_1_.refs_0_, bf16[256,1024]{1,0:T(8,128)(2,1)S(1)} %get-tuple-element.43.refs_2_.refs_1_, bf16[256,1024]{1,0:T(8,128)(2,1)S(1)} %get-tuple-element.44.refs_3_.refs_2_, ...), custom_call_target="tpu_custom_call" | custom-call | flops 200000000 | bytes 1500000 | tf_op jit(solution)/shard_map/pallas_call | solution.py:246
  26.7 1.0 %shard_map.54.refs_3_.refs_4_ = f32[256,512]{1,0:T(8,128)S(1)} custom-call(bf16[256,1024]{1,0:T(8,128)(2,1)S(1)} %get-tuple-element.45.refs_0_.refs_1_, bf16[256,1024]{1,0:T(8,128)(2,1)S(1)} %get-tuple-element.42.refs_1_.refs_0_, bf16[256,1024]{1,0:T(8,128)(2,1)S(1)} %get-tuple-element.43.refs_2_.refs_1_, ...), custom_call_target="tpu_custom_call" | custom-call | flops 200000000 | bytes 1500000 | tf_op jit(solution)/shard_map/pallas_call | solution.py:246
  27.7 1.1 %shard_map.56.refs_5_ = bf16[256,2048]{1,0:T(8,128)(2,1)} custom-call(bf16[256,128]{1,0:T(8,128)(2,1)S(1)} %get-tuple-element.50.refs_0_, bf16[256,1024]{1,0:T(8,128)(2,1)S(1)} %get-tuple-element.42.refs_1_.refs_0_, f32[1,2048]{1,0:T(1,128)S(1)} %get-tuple-element.46.refs_2_, f32[256,768]{1,0:T(8,128)S(1)} %shard_map.55.refs_3_.refs_4_, ...), custom_call_target="tpu_custom_call" | custom-call | flops 50000000 | bytes 1000000 | tf_op jit(solution)/shard_map/pallas_call | solution.py:246
  28.8 0.0 collective-permute-done.6.refs_0_
  28.8 1.1 %shard_map.57.refs_5_ = bf16[256,2048]{1,0:T(8,128)(2,1)} custom-call(bf16[256,128]{1,0:T(8,128)(2,1)S(1)} %collective-permute-done.6.refs_0_, bf16[256,1024]{1,0:T(8,128)(2,1)S(1)} %get-tuple-element.45.refs_0_.refs_1_, f32[1,2048]{1,0:T(1,128)S(1)} %get-tuple-element.46.refs_2_, ...), custom_call_target="tpu_custom_call", output_to_operand_aliasing={{}: (5, {})} | custom-call | flops 50000000 | bytes 1000000 | tf_op jit(solution)/shard_map/pallas_call | solution.py:246
  29.9 1.1 %shard_map.58.refs_5_ = bf16[256,2048]{1,0:T(8,128)(2,1)} custom-call(bf16[256,128]{1,0:T(8,128)(2,1)S(1)} %get-tuple-element.47.refs_0_, bf16[256,1024]{1,0:T(8,128)(2,1)S(1)} %get-tuple-element.42.refs_1_.refs_0_, f32[1,2048]{1,0:T(1,128)S(1)} %get-tuple-element.46.refs_2_, ...), custom_call_target="tpu_custom_call", output_to_operand_aliasing={{}: (5, {})} | custom-call | flops 50000000 | bytes 1000000 | tf_op jit(solution)/shard_map/pallas_call | solution.py:246
  31.0 0.0 collective-permute-done.5.refs_0_
  31.0 1.1 %shard_map.59 = bf16[256,2048]{1,0:T(8,128)(2,1)} custom-call(bf16[256,128]{1,0:T(8,128)(2,1)S(1)} %collective-permute-done.5.refs_0_, bf16[256,1024]{1,0:T(8,128)(2,1)S(1)} %get-tuple-element.45.refs_0_.refs_1_, f32[1,2048]{1,0:T(1,128)S(1)} %get-tuple-element.46.refs_2_, f32[256,512]{1,0:T(8,128)S(1)} %shard_map.54.refs_3_.refs_4_, ...), custom_call_target="tpu_custom_call", output_to_operand_aliasing={{}: (5, {})} | custom-call | flops 50000000 | bytes 1000000 | tf_op jit(solution)/shard_map/pallas_call | solution.py:246
  (3 shorter events, 0.1 us)
Async XLA Ops:
  1.7 1.8 %collective-permute-start = (bf16[512,128]{1,0:T(8,128)(2,1)S(1)}, bf16[512,128]{1,0:T(8,128)(2,1)S(1)}, u32[]{:S(2)}, u32[]{:S(2)}) collective-permute-start(bf16[512,128]{1,0:T(8,128)(2,1)S(1)} %get-tuple-element.31), channel_id=1, source_target_pairs={{0,1},{1,0},{2,3},{3,2},{4,5},{5,4},{6,7},{7,6},{8,9},{9,8},{10,11... | collective-permute-start | bytes 393224 | tf_op jit(solution)/shard_map/ppermute | solution.py:270
  3.5 5.3 %collective-permute-start.1 = (bf16[256,128]{1,0:T(8,128)(2,1)S(1)}, bf16[256,128]{1,0:T(8,128)(2,1)S(1)}, u32[]{:S(2)}, u32[]{:S(2)}) collective-permute-start(bf16[256,128]{1,0:T(8,128)(2,1)S(1)} %get-tuple-element.33), channel_id=1, source_target_pairs={{0,2},{1,3},{2,0},{3,1},{4,6},{5,7},{6,4},{7,5},{8,10},{9,11},{10,... | collective-permute-start | bytes 196616 | tf_op jit(solution)/shard_map/ppermute | solution.py:270
  8.9 4.3 %collective-permute-start.2 = (bf16[256,128]{1,0:T(8,128)(2,1)S(1)}, bf16[256,128]{1,0:T(8,128)(2,1)S(1)}, u32[]{:S(2)}, u32[]{:S(2)}) collective-permute-start(bf16[256,128]{1,0:T(8,128)(2,1)S(1)} %get-tuple-element.35), channel_id=1, source_target_pairs={{0,4},{1,5},{2,6},{3,7},{4,0},{5,1},{6,2},{7,3},{8,12},{9,13},{10,... | collective-permute-start | bytes 196616 | tf_op jit(solution)/shard_map/ppermute | solution.py:270
  13.2 5.2 %collective-permute-start.3 = (bf16[256,128]{1,0:T(8,128)(2,1)S(1)}, bf16[256,128]{1,0:T(8,128)(2,1)S(1)}, u32[]{:S(2)}, u32[]{:S(2)}) collective-permute-start(bf16[256,128]{1,0:T(8,128)(2,1)S(1)} %get-tuple-element.37), channel_id=1, source_target_pairs={{0,8},{1,9},{2,10},{3,11},{4,12},{5,13},{6,14},{7,15},{8,0},{9,1},... | collective-permute-start | bytes 196616 | tf_op jit(solution)/shard_map/ppermute | solution.py:270
  18.5 4.3 %collective-permute-start.4 = (bf16[256,128]{1,0:T(8,128)(2,1)S(1)}, bf16[256,128]{1,0:T(8,128)(2,1)S(1)}, u32[]{:S(2)}, u32[]{:S(2)}) collective-permute-start(bf16[256,128]{1,0:T(8,128)(2,1)S(1)} %get-tuple-element.40), channel_id=1, source_target_pairs={{0,2},{1,3},{2,0},{3,1},{4,6},{5,7},{6,4},{7,5},{8,10},{9,11},{10,... | collective-permute-start | bytes 196616 | tf_op jit(solution)/shard_map/ppermute | solution.py:270
  20.3 8.5 %collective-permute-start.6 = (bf16[256,128]{1,0:T(8,128)(2,1)S(1)}, bf16[256,128]{1,0:T(8,128)(2,1)S(1)}, u32[]{:S(2)}, u32[]{:S(2)}) collective-permute-start(bf16[256,128]{1,0:T(8,128)(2,1)S(1)} %get-tuple-element.49), channel_id=1, source_target_pairs={{0,1},{1,0},{2,3},{3,2},{4,5},{5,4},{6,7},{7,6},{8,9},{9,8},{10,11... | collective-permute-start | bytes 196616 | tf_op jit(solution)/shard_map/ppermute | solution.py:270
  22.9 8.1 %collective-permute-start.5 = (bf16[256,128]{1,0:T(8,128)(2,1)S(1)}, bf16[256,128]{1,0:T(8,128)(2,1)S(1)}, u32[]{:S(2)}, u32[]{:S(2)}) collective-permute-start(bf16[256,128]{1,0:T(8,128)(2,1)S(1)} %get-tuple-element.41), channel_id=1, source_target_pairs={{0,1},{1,0},{2,3},{3,2},{4,5},{5,4},{6,7},{7,6},{8,9},{9,8},{10,11... | collective-permute-start | bytes 196616 | tf_op jit(solution)/shard_map/ppermute | solution.py:270

commit v6 on v5

v6 whole, which is shorter than its diff:
```python
import functools

import jax
import jax.numpy as jnp
from jax import lax
from jax.experimental import pallas as pl
from jax.experimental.pallas import tpu as pltpu
from jax.sharding import PartitionSpec as P


HEAD_DIM = 64
PAIR = 2 * HEAD_DIM
QUAD = 4 * HEAD_DIM
EPS = 1e-05
AXIS = "seq"
BF16, F32 = jnp.bfloat16, jnp.float32


def core_bit():
    return lax.axis_index(AXIS) & 1


def side_bit():
    return (lax.axis_index(AXIS) >> 1) & 1


def aligned(index, by):
    return pl.multiple_of(index * by, by)


def first_lanes(shape):
    return lax.broadcasted_iota(jnp.int32, shape, len(shape) - 1) % PAIR < HEAD_DIM


def dot(a, b, dims):
    return lax.dot_general(a, b, (dims, ((), ())), preferred_element_type=F32)


def slot_start(slot, part):
    core, side = core_bit(), side_bit()
    quarter = 2 * (core if slot >= 2 else 1 - core) + (side if slot % 2 else 1 - side)
    return aligned(quarter, part)


def load_slot(src, dst, slot, sem):
    part = dst.shape[1]
    load = pltpu.make_async_copy(src.at[:, pl.ds(slot_start(slot, part), part)], dst, sem)
    load.start()
    return load


def wait_all(loads):
    for load in loads:
        load.wait()


def states_of(k_ref, v_ref, out_ref):
    first = first_lanes((HEAD_DIM, PAIR))
    for quad in range(k_ref.shape[1] // QUAD):
        lanes = pl.ds(quad * QUAD, QUAD)
        fk = jnp.maximum(k_ref[:, lanes], 0)
        full = dot(fk, v_ref[:, lanes], ((0,), (0,)))
        for p in range(2):
            top = p * PAIR
            rows = full[top : top + PAIR, top : top + PAIR]
            packed = jnp.where(first, rows[:HEAD_DIM], rows[HEAD_DIM:])
            out_ref[pl.ds((quad * 2 + p) * HEAD_DIM, HEAD_DIM), :] = packed.astype(out_ref.dtype)


def first_kernel(k_hbm, v_hbm, send, k0, v0, k2, v2, sems):
    loads = [
        load_slot(src, dst, slot, sems.at[n])
        for n, (src, dst, slot) in enumerate(((k_hbm, k0, 0), (v_hbm, v0, 0), (k_hbm, k2, 2), (v_hbm, v2, 2)))
    ]
    wait_all(loads[:2])
    states_of(k0, v0, send)
    wait_all(loads[2:])


def second_kernel(k_hbm, v_hbm, k2, v2, keep, k1, v1, k3, v3, sems):
    loads = [
        load_slot(src, dst, slot, sems.at[n])
        for n, (src, dst, slot) in enumerate(((k_hbm, k1, 1), (v_hbm, v1, 1), (k_hbm, k3, 3), (v_hbm, v3, 3)))
    ]
    states_of(k2, v2, keep)
    wait_all(loads)


def third_kernel(k1, v1, send):
    states_of(k1, v1, send)


def fourth_kernel(k3, v3, q_hbm, gain_hbm, keep, q2, q3, gain, sems):
    loads = [load_slot(q_hbm, q3, 3, sems.at[0]), load_slot(q_hbm, q2, 2, sems.at[1])]
    loads.append(pltpu.make_async_copy(gain_hbm, gain, sems.at[2]))
    loads[-1].start()
    states_of(k3, v3, keep)
    wait_all(loads)


def after_core(keep, got, send, ext):
    state, other = keep[...], got[...].astype(F32)
    send[...] = (state + other).astype(BF16)
    ext[...] = jnp.where(core_bit() == 0, state, other)


def after_side(keep, got_core, got, send, total, ext_core, ext_side):
    state, other = keep[...], got_core[...].astype(F32)
    own, from_side = state + other, got[...].astype(F32)
    value = own + from_side
    send[...] = value.astype(BF16)
    total[...] = value
    ext_core[...] = jnp.where(core_bit() == 0, state, other)
    ext_side[...] = jnp.where(side_bit() == 0, own, from_side)


def upper_part(before, got, level):
    upper = (lax.axis_index(AXIS) >> level) & 1
    value = jnp.where(upper == 1, got[...].astype(F32), 0.0)
    return value if before is None else before[...] + value


def after_outer(refs, *, level, start, more):
    refs = list(refs)
    total = refs.pop(0)
    before = None if start else refs.pop(0)
    got, send, before_out, *total_out = refs
    new = total[...] + got[...].astype(F32)
    send[...] = new.astype(BF16)
    before_out[...] = upper_part(before, got, level)
    if more:
        total_out[0][...] = new


def after_last(refs, *, level, start):
    refs = list(refs)
    before = None if start else refs.pop(0)
    got, ext_side, ext_core, send, send_core, prior = refs
    value = upper_part(before, got, level)
    both = value + ext_side[...]
    first = side_bit() == 0
    send[...] = jnp.where(first, both, value).astype(BF16)
    split_cores(jnp.where(first, value, both), ext_core[...], send_core, prior)


def split_cores(base, ext, send_core, prior):
    both = base + ext
    first = core_bit() == 0
    send_core[...] = jnp.where(first, both, base).astype(BF16)
    prior[...] = jnp.where(first, base, both).astype(BF16)


def after_base(got, ext_core, send_core, prior):
    split_cores(got[...].astype(F32), ext_core[...], send_core, prior)


def intra_kernel(refs, *, pairs, slots, fetch):
    refs = list(refs)
    q_hbm = refs.pop(0) if fetch else None
    tiles = {slot: [None, refs.pop(0), refs.pop(0)] for slot in slots}
    for slot in slots:
        if slot not in fetch:
            tiles[slot][0] = refs.pop(0)
    intra_ref = refs.pop(0)
    fetched = {slot: refs.pop(0) for slot in fetch}
    loads = {slot: load_slot(q_hbm, ref, slot, refs[-1].at[n]) for n, (slot, ref) in enumerate(fetched.items())}
    for slot in set(fetch) & set(slots):
        tiles[slot][0] = fetched[slot]
    count = intra_ref.shape[0]
    part = tiles[slots[0]][1].shape[1]
    mid = count // 2
    first = first_lanes((count, PAIR))
    rows = lax.broadcasted_iota(jnp.int32, (mid, mid), 0)
    cols = lax.broadcasted_iota(jnp.int32, (mid, mid), 1)
    causal = cols <= rows
    for p in pairs:
        lanes = pl.ds((p - min(pairs)) * PAIR, PAIR)
        slot = p * PAIR // part
        if slot in loads:
            loads.pop(slot).wait()
        q_ref, k_ref, v_ref = tiles[slot]
        there = pl.ds(p * PAIR % part, PAIR)
        fq = jnp.maximum(q_ref[:, there], 0)
        fk = jnp.maximum(k_ref[:, there], 0)
        val = v_ref[:, there]
        zero = jnp.zeros_like(fq)
        top, low, weights = [], [], []
        for h in range(2):
            mine = first if h == 0 else jnp.logical_not(first)
            mine_q = jnp.where(mine, fq, zero)
            s_top = dot(mine_q[:mid], fk[:mid], ((1,), (1,)))
            s_low = dot(mine_q[mid:], fk, ((1,), (1,)))
            s_top = jnp.where(causal, s_top, 0.0).astype(BF16)
            s_diag = jnp.where(causal, s_low[:, mid:], 0.0).astype(BF16)
            s_low = jnp.concatenate([s_low[:, :mid].astype(BF16), s_diag], axis=1)
            top.append(s_top)
            low.append(s_low)
            weights.append(jnp.where(mine, val, zero))
        w_top = jnp.concatenate([w[:mid] for w in weights], axis=0)
        intra_ref[:mid, lanes] = dot(jnp.concatenate(top, axis=1), w_top, ((1,), (0,)))
        w_low = jnp.concatenate(weights, axis=0)
        intra_ref[mid:, lanes] = dot(jnp.concatenate(low, axis=1), w_low, ((1,), (0,)))
    wait_all(loads.values())


def final_kernel(refs, *, slot, places):
    refs = list(refs)
    prior_ref, q_ref, gain_ref = refs[:3]
    intra_refs = refs[3 : 3 + 1 + max(which for which, _ in places)]
    out_hbm, out_buf, sems = refs[-3:]
    part = out_buf.shape[1]
    base = slot_start(slot, part)
    lane = lax.broadcasted_iota(jnp.int32, (PAIR, PAIR), 1) // HEAD_DIM
    row = lax.broadcasted_iota(jnp.int32, (PAIR, PAIR), 0) // HEAD_DIM
    same = lane == row
    ones = jnp.where(same, 1.0 / HEAD_DIM, 0.0).astype(BF16)
    copies = []
    for p, (which, at) in enumerate(places):
        lanes = pl.ds(p * PAIR, PAIR)
        state = prior_ref[pl.ds(p * HEAD_DIM, HEAD_DIM), :]
        block = jnp.concatenate([state, state], axis=0)
        block = jnp.where(same, block, jnp.zeros_like(block))
        there = pl.ds(pl.multiple_of(base + p * PAIR, PAIR), PAIR)
        fq = jnp.maximum(q_ref[:, lanes], 0)
        numer = dot(fq, block, ((1,), (0,))) + intra_refs[which][:, pl.ds(at, PAIR)]
        mean_sq = dot((numer * numer).astype(BF16), ones, ((1,), (0,)))
        normed = numer * lax.rsqrt(mean_sq + EPS) * gain_ref[:, there]
        out_buf[:, lanes] = normed.astype(BF16)
        copies.append(pltpu.make_async_copy(out_buf.at[:, lanes], out_hbm.at[:, there], sems.at[p]))
        copies[-1].start()
    wait_all(copies)


ANY = pl.BlockSpec(memory_space=pl.ANY)
HBM = pl.BlockSpec(memory_space=pltpu.HBM)
VMEM = pl.BlockSpec(memory_space=pltpu.VMEM)
DMA = pltpu.SemaphoreType.DMA


def call(kernel, outs, args, specs=None, out_specs=None, scratch=(), alias=None, cost=(10_000, 10_000)):
    specs = [VMEM] * len(args) if specs is None else specs
    args = [a if s is ANY else pltpu.with_memory_space_constraint(a, s.memory_space) for a, s in zip(args, specs)]
    many = isinstance(outs, (tuple, list))
    return pl.pallas_call(
        kernel,
        out_shape=outs,
        in_specs=specs,
        out_specs=([VMEM] * len(outs) if many else VMEM) if out_specs is None else out_specs,
        scratch_shapes=scratch,
        input_output_aliases=alias or {},
        compiler_params=pltpu.CompilerParams(vmem_limit_bytes=12 * 2**20),
        cost_estimate=pl.CostEstimate(flops=cost[0], transcendentals=0, bytes_accessed=cost[1]),
    )(*args)


def packed(kernel, **static):
    return lambda *refs: kernel(refs, **static)


def on_device(queries, keys, values, gain, *, size):
    count, width = queries.shape
    part = width // 4
    quarter = part // PAIR * HEAD_DIM
    tile = pltpu.VMEM((count, part), BF16)
    k, v, q = [None] * 4, [None] * 4, [None] * 4

    def swap(x, level):
        return lax.ppermute(x, AXIS, [(i, i ^ (1 << level)) for i in range(size)])

    def small(dtype):
        return pltpu.VMEM((quarter, PAIR), dtype)

    send, k[0], v[0], k[2], v[2] = call(
        first_kernel, (small(BF16), *[tile] * 4), (keys, values), specs=[HBM] * 2, scratch=[DMA((4,))]
    )
    got = swap(send, 0)
    keep, k[1], v[1], k[3], v[3] = call(
        second_kernel,
        (small(F32), *[tile] * 4),
        (keys, values, k[2], v[2]),
        specs=[HBM] * 2 + [VMEM] * 2,
        scratch=[DMA((4,))],
        cost=(80_000_000, 2_000_000),
    )
    send, ext_core2 = call(after_core, (small(BF16), small(F32)), (keep, got))
    got = swap(send, 1)
    send = call(third_kernel, small(BF16), (k[1], v[1]), cost=(80_000_000, 500_000))
    got_core = swap(send, 0)
    keep, q[2], q[3], gain_vmem = call(
        fourth_kernel,
        (small(F32), tile, tile, pltpu.VMEM((1, width), F32)),
        (k[3], v[3], queries, gain[None, :]),
        specs=[VMEM] * 2 + [HBM] * 2,
        scratch=[DMA((3,))],
        cost=(80_000_000, 1_000_000),
    )
    pairs = width // PAIR
    cuts = (pairs, pairs * 3 // 4, pairs * 3 // 8, 0)
    groups = tuple(zip(cuts[1:], cuts[:-1]))
    parts = []
    for n, (low, high) in enumerate(groups):
        order = tuple(range(high - 1, low - 1, -1))
        slots = tuple(sorted({p * PAIR // part for p in order}))
        fetch = (1, 0) if n == 1 else ()
        args = [queries] if fetch else []
        for slot in slots:
            args += [k[slot], v[slot]]
        args += [q[slot] for slot in slots if slot not in fetch]
        buffer = pltpu.VMEM((count, (high - low) * PAIR), F32)
        outs = call(
            packed(intra_kernel, pairs=order, slots=slots, fetch=fetch),
            (buffer, *[tile] * len(fetch)) if fetch else buffer,
            args,
            specs=[HBM] + [VMEM] * (len(args) - 1) if fetch else None,
            scratch=[DMA((len(fetch),))] if fetch else (),
            cost=(200_000_000, 1_500_000),
        )
        if fetch:
            outs, *found = outs
            for slot, value in zip(fetch, found):
                q[slot] = value
        parts.append(outs)

    send, total, ext_core3, ext_side = call(
        after_side, (small(BF16), *[small(F32)] * 3), (keep, got_core, got)
    )
    before = []
    level = 2
    while 1 << level < size:
        got = swap(send, level)
        if 1 << (level + 1) < size:
            more = 1 << (level + 2) < size
            send, *before = call(
                packed(after_outer, level=level, start=not before, more=more),
                (small(BF16), *[small(F32)] * (1 + more)),
                [total, *before, got],
            )
            if more:
                total = before.pop()
        else:
            send, send_core, prior3 = call(
                packed(after_last, level=level, start=not before),
                (small(BF16), small(BF16), small(BF16)),
                [*before, got, ext_side, ext_core3],
            )
        level += 1
    got = swap(send, 1)
    prior1 = swap(send_core, 0)
    send_core, prior2 = call(after_base, (small(BF16), small(BF16)), (got, ext_core2))
    prior0 = swap(send_core, 0)

    out = None
    for slot, prior in ((3, prior3), (1, prior1), (2, prior2), (0, prior0)):
        used, places = [], []
        for pair in range(slot * part // PAIR, (slot + 1) * part // PAIR):
            n = next(i for i, (low, high) in enumerate(groups) if low <= pair < high)
            if n not in used:
                used.append(n)
            places.append((used.index(n), (pair - groups[n][0]) * PAIR))
        args = [prior, q[slot], gain_vmem, *[parts[n] for n in used]]
        specs = [VMEM] * len(args)
        if out is not None:
            args.append(out)
            specs.append(ANY)
        out = call(
            packed(final_kernel, slot=slot, places=tuple(places)),
            jax.ShapeDtypeStruct((count, width), BF16),
            args,
            specs=specs,
            out_specs=ANY,
            scratch=[pltpu.VMEM((count, part), BF16), DMA((part // PAIR,))],
            alias={} if out is None else {len(args) - 1: 0},
            cost=(50_000_000, 1_000_000),
        )
    return out


def solution(mesh):
    return jax.shard_map(
        functools.partial(on_device, size=mesh.shape[AXIS]),
        mesh=mesh,
        in_specs=(
            P(("groups", "seq"), None),
            P(("groups", "seq"), None),
            P(("groups", "seq"), None),
            P(),
        ),
        out_specs=P(("groups", "seq"), None),
        check_vma=False,
    )
```

time: 32.3 us -> 32.5 us (level)
  waiting for transfers between devices: 9.99 us -> 8.05 us
  starting transfers between devices: 9.87 us -> 10.9 us
  Pallas kernels: 12.1 us -> 13.1 us
    ppermute x7 -> x8, waiting for transfers between devices: 9.99 us -> 8.05 us  [swap(): return lax.ppermute(x, AXIS, [(i, i ^ 1 << level) for i in range(size)])]
    ppermute x7 -> x8, starting transfers between devices: 9.87 us -> 10.9 us  [swap(): return lax.ppermute(x, AXIS, [(i, i ^ 1 << level) for i in range(size)])]
    pallas_call x14 -> x16, Pallas kernels: 12.1 us -> 13.1 us  [call(): pl.pallas_call(kernel, out_shape=outs, in_specs=specs, out_specs=([VMEM]...]
  transfers between devices with their start and end apart: 7 -> 8, of which waited for: 4 -> 4; matrix products, arithmetic and copies ran while one was open for 0% -> 0% of each run, Pallas kernels for 29% -> 33%
where the time goes in v6:
time: 32.5 us; the launch traced here: 32.2 us
  Pallas kernels  13.1 us (40%)
  starting transfers between devices  10.9 us (34%)
  waiting for transfers between devices  8.05 us (25%)
    pallas_call x16, Pallas kernels, call(): pl.pallas_call(kernel, out_shape=outs, in_specs=specs, out_specs=([VMEM]...  13.1 us
    ppermute x8, starting transfers between devices, swap(): return lax.ppermute(x, AXIS, [(i, i ^ 1 << level) for i in range(size)])  10.9 us
    ppermute x8, waiting for transfers between devices, swap(): return lax.ppermute(x, AXIS, [(i, i ^ 1 << level) for i in range(size)])  8.05 us
  transfers between devices with their start and end apart: 8, of which 4 were waited for; matrix products, arithmetic and copies ran while one was open for 0% of the time, Pallas kernels for 33%

profile of v6, /device:TPU:0, one launch (start us, length us, event | category | flops | bytes accessed | tf_op | source)
XLA Modules:
  0.0 32.2 jit_solution(2450206391581764749)
XLA Ops:
  0.0 1.4 %shard_map.46 = (bf16[256,128]{1,0:T(8,128)(2,1)S(1)}, bf16[256,512]{1,0:T(8,128)(2,1)S(1)}, bf16[256,512]{1,0:T(8,128)(2,1)S(1)}, bf16[256,512]{1,0:T(8,128)(2,1)S(1)}, bf16[256,512]{1,0:T(8,128)(2,1)S(1)}) custom-call(bf16[256,2048]{1,0:T(8,128)(2,1)} %k_hbm.3, bf16[256,2048]{1,0:T(8,128)(2,1)} %v_hbm.3), custom_call_target="tpu_custom_call" | custom-call | flops 10000 | bytes 10000 | tf_op jit(solution)/shard_map/pallas_call | solution.py:244
  1.4 0.6 %collective-permute-start.1 = (bf16[256,128]{1,0:T(8,128)(2,1)S(1)}, bf16[256,128]{1,0:T(8,128)(2,1)S(1)}, u32[]{:S(2)}, u32[]{:S(2)}) collective-permute-start(bf16[256,128]{1,0:T(8,128)(2,1)S(1)} %get-tuple-element.43), channel_id=1, source_target_pairs={{0,1},{1,0},{2,3},{3,2},{4,5},{5,4},{6,7},{7,6},{8,9},{9,8},{10,11... | collective-permute-start | bytes 196616 | tf_op jit(solution)/shard_map/ppermute | solution.py:268
  1.9 1.3 %shard_map.47 = (f32[256,128]{1,0:T(8,128)S(1)}, bf16[256,512]{1,0:T(8,128)(2,1)S(1)}, bf16[256,512]{1,0:T(8,128)(2,1)S(1)}, bf16[256,512]{1,0:T(8,128)(2,1)S(1)}, bf16[256,512]{1,0:T(8,128)(2,1)S(1)}) custom-call(bf16[256,2048]{1,0:T(8,128)(2,1)} %k_hbm.3, bf16[256,2048]{1,0:T(8,128)(2,1)} %v_hbm.3, bf16[256,512]{1,0:T(8,128)(2,1)S(1)} %get-tuple-element.35.k2.refs_3_, ...), custom_call_target="tpu_custom_call" | custom-call | flops 80000000 | bytes 2000000 | tf_op jit(solution)/shard_map/pallas_call | solution.py:244
  3.2 0.3 shard_map.49
  3.5 0.1 collective-permute-start
  3.6 0.0 collective-permute-done.1.got
  3.6 3.1 %collective-permute-start.2 = (bf16[256,128]{1,0:T(8,128)(2,1)S(1)}, bf16[256,128]{1,0:T(8,128)(2,1)S(1)}, u32[]{:S(2)}, u32[]{:S(2)}) collective-permute-start(bf16[256,128]{1,0:T(8,128)(2,1)S(1)} %get-tuple-element.44), channel_id=1, source_target_pairs={{0,2},{1,3},{2,0},{3,1},{4,6},{5,7},{6,4},{7,5},{8,10},{9,11},{10,... | collective-permute-start | bytes 196616 | tf_op jit(solution)/shard_map/ppermute | solution.py:268
  6.7 1.1 %shard_map.48 = (f32[256,128]{1,0:T(8,128)S(1)}, bf16[256,512]{1,0:T(8,128)(2,1)S(1)}, bf16[256,512]{1,0:T(8,128)(2,1)S(1)}, f32[1,2048]{1,0:T(1,128)S(1)}) custom-call(bf16[256,512]{1,0:T(8,128)(2,1)S(1)} %get-tuple-element.37.k3.refs_0_, bf16[256,512]{1,0:T(8,128)(2,1)S(1)} %get-tuple-element.38.v3.refs_1_, bf16[256,2048]{1,0:T(8,128)(2,1)} %refs_0_.1, ...), custom_call_target="tpu_custom_call" | custom-call | flops 80000000 | bytes 1000000 | tf_op jit(solution)/shard_map/pallas_call | solution.py:244
  7.8 0.0 collective-permute-done.got_core
  7.8 1.1 %collective-permute-done.2.got = bf16[256,128]{1,0:T(8,128)(2,1)S(1)} collective-permute-done((bf16[256,128]{1,0:T(8,128)(2,1)S(1)}, bf16[256,128]{1,0:T(8,128)(2,1)S(1)}, u32[]{:S(2)}, u32[]{:S(2)}) %collective-permute-start.2) | collective-permute-done | bytes 65568 | tf_op jit(solution)/shard_map/ppermute | solution.py:268
  9.0 2.1 %collective-permute-start.3 = (bf16[256,128]{1,0:T(8,128)(2,1)S(1)}, bf16[256,128]{1,0:T(8,128)(2,1)S(1)}, u32[]{:S(2)}, u32[]{:S(2)}) collective-permute-start(bf16[256,128]{1,0:T(8,128)(2,1)S(1)} %get-tuple-element.46), channel_id=1, source_target_pairs={{0,4},{1,5},{2,6},{3,7},{4,0},{5,1},{6,2},{7,3},{8,12},{9,13},{10,... | collective-permute-start | bytes 196616 | tf_op jit(solution)/shard_map/ppermute | solution.py:268
  11.1 2.2 %collective-permute-done.3.refs_1_ = bf16[256,128]{1,0:T(8,128)(2,1)S(1)} collective-permute-done((bf16[256,128]{1,0:T(8,128)(2,1)S(1)}, bf16[256,128]{1,0:T(8,128)(2,1)S(1)}, u32[]{:S(2)}, u32[]{:S(2)}) %collective-permute-start.3) | collective-permute-done | bytes 65568 | tf_op jit(solution)/shard_map/ppermute | solution.py:268
  13.4 3.1 %collective-permute-start.4 = (bf16[256,128]{1,0:T(8,128)(2,1)S(1)}, bf16[256,128]{1,0:T(8,128)(2,1)S(1)}, u32[]{:S(2)}, u32[]{:S(2)}) collective-permute-start(bf16[256,128]{1,0:T(8,128)(2,1)S(1)} %get-tuple-element.48), channel_id=1, source_target_pairs={{0,8},{1,9},{2,10},{3,11},{4,12},{5,13},{6,14},{7,15},{8,0},{9,1},... | collective-permute-start | bytes 196616 | tf_op jit(solution)/shard_map/ppermute | solution.py:268
  16.5 2.2 %collective-permute-done.4.refs_1_ = bf16[256,128]{1,0:T(8,128)(2,1)S(1)} collective-permute-done((bf16[256,128]{1,0:T(8,128)(2,1)S(1)}, bf16[256,128]{1,0:T(8,128)(2,1)S(1)}, u32[]{:S(2)}, u32[]{:S(2)}) %collective-permute-start.4) | collective-permute-done | bytes 65568 | tf_op jit(solution)/shard_map/ppermute | solution.py:268
  18.7 0.1 shard_map.53
  18.8 1.9 %collective-permute-start.5 = (bf16[256,128]{1,0:T(8,128)(2,1)S(1)}, bf16[256,128]{1,0:T(8,128)(2,1)S(1)}, u32[]{:S(2)}, u32[]{:S(2)}) collective-permute-start(bf16[256,128]{1,0:T(8,128)(2,1)S(1)} %get-tuple-element.51), channel_id=1, source_target_pairs={{0,2},{1,3},{2,0},{3,1},{4,6},{5,7},{6,4},{7,5},{8,10},{9,11},{10,... | collective-permute-start | bytes 196616 | tf_op jit(solution)/shard_map/ppermute | solution.py:268
  20.7 0.0 collective-permute-start.7
  20.7 2.4 %collective-permute-done.5.got = bf16[256,128]{1,0:T(8,128)(2,1)S(1)} collective-permute-done((bf16[256,128]{1,0:T(8,128)(2,1)S(1)}, bf16[256,128]{1,0:T(8,128)(2,1)S(1)}, u32[]{:S(2)}, u32[]{:S(2)}) %collective-permute-start.5) | collective-permute-done | bytes 65568 | tf_op jit(solution)/shard_map/ppermute | solution.py:268
  23.2 0.1 collective-permute-start.6
  23.2 1.0 %shard_map.57.refs_3_ = f32[256,512]{1,0:T(8,128)S(1)} custom-call(bf16[256,512]{1,0:T(8,128)(2,1)S(1)} %get-tuple-element.37.k3.refs_0_, bf16[256,512]{1,0:T(8,128)(2,1)S(1)} %get-tuple-element.38.v3.refs_1_, bf16[256,512]{1,0:T(8,128)(2,1)S(1)} %get-tuple-element.64.refs_2_.refs_1_), custom_call_target="tpu_custom_call" | custom-call | flops 200000000 | bytes 1500000 | tf_op jit(solution)/shard_map/pallas_call | solution.py:244
  24.2 2.2 %shard_map.55 = (f32[256,768]{1,0:T(8,128)S(1)}, bf16[256,512]{1,0:T(8,128)(2,1)S(1)}, bf16[256,512]{1,0:T(8,128)(2,1)S(1)}) custom-call(bf16[256,2048]{1,0:T(8,128)(2,1)} %refs_0_.1, bf16[256,512]{1,0:T(8,128)(2,1)S(1)} %get-tuple-element.40.k1.refs_1_.refs_2_, bf16[256,512]{1,0:T(8,128)(2,1)S(1)} %get-tuple-element.41.v1.refs_2_.refs_3_, ...), custom_call_target="tpu_custom_call" | custom-call | flops 200000000 | bytes 1500000 | tf_op jit(solution)/shard_map/pallas_call | solution.py:244
  26.5 1.4 %shard_map.56.refs_3_ = f32[256,768]{1,0:T(8,128)S(1)} custom-call(bf16[256,512]{1,0:T(8,128)(2,1)S(1)} %get-tuple-element.57.refs_0_, bf16[256,512]{1,0:T(8,128)(2,1)S(1)} %get-tuple-element.58.refs_1_, bf16[256,512]{1,0:T(8,128)(2,1)S(1)} %get-tuple-element.40.k1.refs_1_.refs_2_, bf16[256,512]{1,0:T(8,128)(2,1)S(1)} %get-tuple-element.41.v1.refs_2_.refs_3_, ...), custom_call_target="tpu_custom_call" | custom-call | flops 200000000 | bytes 1500000 | tf_op jit(solution)/shard_map/pallas_call | solution.py:244
  27.9 1.1 %shard_map.58.refs_5_ = bf16[256,2048]{1,0:T(8,128)(2,1)} custom-call(bf16[256,128]{1,0:T(8,128)(2,1)S(1)} %get-tuple-element.63.refs_0_, bf16[256,512]{1,0:T(8,128)(2,1)S(1)} %get-tuple-element.64.refs_2_.refs_1_, f32[1,2048]{1,0:T(1,128)S(1)} %get-tuple-element.56.refs_2_, f32[256,512]{1,0:T(8,128)S(1)} %shard_map.57.refs_3_), custom_call_target="tpu_custom_call" | custom-call | flops 50000000 | bytes 1000000 | tf_op jit(solution)/shard_map/pallas_call | solution.py:244
  29.0 0.0 collective-permute-done.7.refs_0_
  29.0 1.1 %shard_map.59.refs_4_ = bf16[256,2048]{1,0:T(8,128)(2,1)} custom-call(bf16[256,128]{1,0:T(8,128)(2,1)S(1)} %collective-permute-done.7.refs_0_, bf16[256,512]{1,0:T(8,128)(2,1)S(1)} %get-tuple-element.59.refs_5_.refs_1_, f32[1,2048]{1,0:T(1,128)S(1)} %get-tuple-element.56.refs_2_, f32[256,768]{1,0:T(8,128)S(1)} %shard_map.56.refs_3_, ...), custom_call_target="tpu_custom_call", output_to_operand_aliasing={{}: (5, {})} | custom-call | flops 50000000 | bytes 1000000 | tf_op jit(solution)/shard_map/pallas_call | solution.py:244
  30.1 1.1 %shard_map.60.refs_4_ = bf16[256,2048]{1,0:T(8,128)(2,1)} custom-call(bf16[256,128]{1,0:T(8,128)(2,1)S(1)} %get-tuple-element.60.refs_0_, bf16[256,512]{1,0:T(8,128)(2,1)S(1)} %get-tuple-element.54.refs_5_.refs_1_, f32[1,2048]{1,0:T(1,128)S(1)} %get-tuple-element.56.refs_2_, ...), custom_call_target="tpu_custom_call", output_to_operand_aliasing={{}: (4, {})} | custom-call | flops 50000000 | bytes 1000000 | tf_op jit(solution)/shard_map/pallas_call | solution.py:244
  31.1 0.0 collective-permute-done.6.refs_0_
  31.2 1.1 %shard_map.61 = bf16[256,2048]{1,0:T(8,128)(2,1)} custom-call(bf16[256,128]{1,0:T(8,128)(2,1)S(1)} %collective-permute-done.6.refs_0_, bf16[256,512]{1,0:T(8,128)(2,1)S(1)} %get-tuple-element.55.refs_4_.refs_1_, f32[1,2048]{1,0:T(1,128)S(1)} %get-tuple-element.56.refs_2_, f32[256,768]{1,0:T(8,128)S(1)} %shard_map.56.refs_3_, ...), custom_call_target="tpu_custom_call", output_to_operand_aliasing={{}: (4, {})} | custom-call | flops 50000000 | bytes 1000000 | tf_op jit(solution)/shard_map/pallas_call | solution.py:244
  (4 shorter events, 0.1 us)
Async XLA Ops:
  1.4 2.2 %collective-permute-start.1 = (bf16[256,128]{1,0:T(8,128)(2,1)S(1)}, bf16[256,128]{1,0:T(8,128)(2,1)S(1)}, u32[]{:S(2)}, u32[]{:S(2)}) collective-permute-start(bf16[256,128]{1,0:T(8,128)(2,1)S(1)} %get-tuple-element.43), channel_id=1, source_target_pairs={{0,1},{1,0},{2,3},{3,2},{4,5},{5,4},{6,7},{7,6},{8,9},{9,8},{10,11... | collective-permute-start | bytes 196616 | tf_op jit(solution)/shard_map/ppermute | solution.py:268
  3.5 4.3 %collective-permute-start = (bf16[256,128]{1,0:T(8,128)(2,1)S(1)}, bf16[256,128]{1,0:T(8,128)(2,1)S(1)}, u32[]{:S(2)}, u32[]{:S(2)}) collective-permute-start(bf16[256,128]{1,0:T(8,128)(2,1)S(1)} %shard_map.49), channel_id=1, source_target_pairs={{0,1},{1,0},{2,3},{3,2},{4,5},{5,4},{6,7},{7,6},{8,9},{9,8},{10,11... | collective-permute-start | bytes 196616 | tf_op jit(solution)/shard_map/ppermute | solution.py:268
  3.6 5.3 %collective-permute-start.2 = (bf16[256,128]{1,0:T(8,128)(2,1)S(1)}, bf16[256,128]{1,0:T(8,128)(2,1)S(1)}, u32[]{:S(2)}, u32[]{:S(2)}) collective-permute-start(bf16[256,128]{1,0:T(8,128)(2,1)S(1)} %get-tuple-element.44), channel_id=1, source_target_pairs={{0,2},{1,3},{2,0},{3,1},{4,6},{5,7},{6,4},{7,5},{8,10},{9,11},{10,... | collective-permute-start | bytes 196616 | tf_op jit(solution)/shard_map/ppermute | solution.py:268
  9.0 4.3 %collective-permute-start.3 = (bf16[256,128]{1,0:T(8,128)(2,1)S(1)}, bf16[256,128]{1,0:T(8,128)(2,1)S(1)}, u32[]{:S(2)}, u32[]{:S(2)}) collective-permute-start(bf16[256,128]{1,0:T(8,128)(2,1)S(1)} %get-tuple-element.46), channel_id=1, source_target_pairs={{0,4},{1,5},{2,6},{3,7},{4,0},{5,1},{6,2},{7,3},{8,12},{9,13},{10,... | collective-permute-start | bytes 196616 | tf_op jit(solution)/shard_map/ppermute | solution.py:268
  13.4 5.3 %collective-permute-start.4 = (bf16[256,128]{1,0:T(8,128)(2,1)S(1)}, bf16[256,128]{1,0:T(8,128)(2,1)S(1)}, u32[]{:S(2)}, u32[]{:S(2)}) collective-permute-start(bf16[256,128]{1,0:T(8,128)(2,1)S(1)} %get-tuple-element.48), channel_id=1, source_target_pairs={{0,8},{1,9},{2,10},{3,11},{4,12},{5,13},{6,14},{7,15},{8,0},{9,1},... | collective-permute-start | bytes 196616 | tf_op jit(solution)/shard_map/ppermute | solution.py:268
  18.8 4.3 %collective-permute-start.5 = (bf16[256,128]{1,0:T(8,128)(2,1)S(1)}, bf16[256,128]{1,0:T(8,128)(2,1)S(1)}, u32[]{:S(2)}, u32[]{:S(2)}) collective-permute-start(bf16[256,128]{1,0:T(8,128)(2,1)S(1)} %get-tuple-element.51), channel_id=1, source_target_pairs={{0,2},{1,3},{2,0},{3,1},{4,6},{5,7},{6,4},{7,5},{8,10},{9,11},{10,... | collective-permute-start | bytes 196616 | tf_op jit(solution)/shard_map/ppermute | solution.py:268
  20.7 8.3 %collective-permute-start.7 = (bf16[256,128]{1,0:T(8,128)(2,1)S(1)}, bf16[256,128]{1,0:T(8,128)(2,1)S(1)}, u32[]{:S(2)}, u32[]{:S(2)}) collective-permute-start(bf16[256,128]{1,0:T(8,128)(2,1)S(1)} %get-tuple-element.62), channel_id=1, source_target_pairs={{0,1},{1,0},{2,3},{3,2},{4,5},{5,4},{6,7},{7,6},{8,9},{9,8},{10,11... | collective-permute-start | bytes 196616 | tf_op jit(solution)/shard_map/ppermute | solution.py:268
  23.2 8.0 %collective-permute-start.6 = (bf16[256,128]{1,0:T(8,128)(2,1)S(1)}, bf16[256,128]{1,0:T(8,128)(2,1)S(1)}, u32[]{:S(2)}, u32[]{:S(2)}) collective-permute-start(bf16[256,128]{1,0:T(8,128)(2,1)S(1)} %get-tuple-element.53), channel_id=1, source_target_pairs={{0,1},{1,0},{2,3},{3,2},{4,5},{5,4},{6,7},{7,6},{8,9},{9,8},{10,11... | collective-permute-start | bytes 196616 | tf_op jit(solution)/shard_map/ppermute | solution.py:268

commit v7 on v6

--- a/solution.py
+++ b/solution.py
@@ -11,6 +11,8 @@
 HEAD_DIM = 64
 PAIR = 2 * HEAD_DIM
 QUAD = 4 * HEAD_DIM
+SHIFT = 6
+CORE, SIDE = 1, 2
 EPS = 1e-05
 AXIS = "seq"
 BF16, F32 = jnp.bfloat16, jnp.float32
@@ -29,7 +31,7 @@
 
 
 def first_lanes(shape):
-    return lax.broadcasted_iota(jnp.int32, shape, len(shape) - 1) % PAIR < HEAD_DIM
+    return lax.broadcasted_iota(jnp.int32, shape, len(shape) - 1) < HEAD_DIM
 
 
 def dot(a, b, dims):
@@ -98,10 +100,14 @@
     wait_all(loads)
 
 
-def after_core(keep, got, send, ext):
-    state, other = keep[...], got[...].astype(F32)
-    send[...] = (state + other).astype(BF16)
-    ext[...] = jnp.where(core_bit() == 0, state, other)
+def before_core(value):
+    return jnp.where(core_bit() == 1, value[...].astype(F32), 0.0)
+
+
+def after_core(keep, got, send, mine, ext):
+    send[...] = (keep[...] + got[...].astype(F32)).astype(BF16)
+    mine[...] = keep[...].astype(BF16)
+    ext[...] = before_core(got)
 
 
 def after_side(keep, got_core, got, send, total, ext_core, ext_side):
@@ -140,18 +146,11 @@
     both = value + ext_side[...]
     first = side_bit() == 0
     send[...] = jnp.where(first, both, value).astype(BF16)
-    split_cores(jnp.where(first, value, both), ext_core[...], send_core, prior)
-
-
-def split_cores(base, ext, send_core, prior):
-    both = base + ext
-    first = core_bit() == 0
-    send_core[...] = jnp.where(first, both, base).astype(BF16)
-    prior[...] = jnp.where(first, base, both).astype(BF16)
-
-
-def after_base(got, ext_core, send_core, prior):
-    split_cores(got[...].astype(F32), ext_core[...], send_core, prior)
+    base = jnp.where(first, value, both)
+    ahead = base + ext_core[...]
+    core = core_bit()
+    send_core[...] = jnp.where(core == 0, ahead, base).astype(BF16)
+    prior[...] = jnp.where(core == 0, base, ahead).astype(BF16)
 
 
 def intra_kernel(refs, *, pairs, slots, fetch):
@@ -203,31 +202,46 @@
     wait_all(loads.values())
 
 
-def final_kernel(refs, *, slot, places):
+def final_kernel(refs, *, slot, places, ext, ready):
     refs = list(refs)
     prior_ref, q_ref, gain_ref = refs[:3]
-    intra_refs = refs[3 : 3 + 1 + max(which for which, _ in places)]
-    out_hbm, out_buf, sems = refs[-3:]
-    part = out_buf.shape[1]
+    refs = refs[3:]
+    ext_ref = refs.pop(0) if ext else None
+    intra_refs = [refs.pop(0) for _ in range(1 + max(which for which, _ in places))]
+    done = [refs.pop(0) for _ in ready]
+    out = refs.pop(0)
+    part = q_ref.shape[1]
     base = slot_start(slot, part)
-    lane = lax.broadcasted_iota(jnp.int32, (PAIR, PAIR), 1) // HEAD_DIM
-    row = lax.broadcasted_iota(jnp.int32, (PAIR, PAIR), 0) // HEAD_DIM
+    copies = []
+    if ready:
+        out_hbm, (out, sems) = out, refs
+        for n, (other, src) in enumerate(zip(ready, done)):
+            there = pl.ds(slot_start(other, part), part)
+            copies.append(pltpu.make_async_copy(src, out_hbm.at[:, there], sems.at[1, n]))
+            copies[-1].start()
+    lane = lax.broadcasted_iota(jnp.int32, (QUAD, QUAD), 1) >> SHIFT
+    row = lax.broadcasted_iota(jnp.int32, (QUAD, QUAD), 0) >> SHIFT
     same = lane == row
     ones = jnp.where(same, 1.0 / HEAD_DIM, 0.0).astype(BF16)
-    copies = []
-    for p, (which, at) in enumerate(places):
-        lanes = pl.ds(p * PAIR, PAIR)
-        state = prior_ref[pl.ds(p * HEAD_DIM, HEAD_DIM), :]
-        block = jnp.concatenate([state, state], axis=0)
+    prior = prior_ref[...]
+    if ext:
+        prior = (prior.astype(F32) + ext_ref[...]).astype(BF16)
+    numers = []
+    for n, (which, at) in enumerate(places):
+        one = prior[n * PAIR : n * PAIR + HEAD_DIM]
+        two = prior[n * PAIR + HEAD_DIM : (n + 1) * PAIR]
+        block = jnp.concatenate([jnp.concatenate([one, two], axis=1)] * 4, axis=0)
         block = jnp.where(same, block, jnp.zeros_like(block))
-        there = pl.ds(pl.multiple_of(base + p * PAIR, PAIR), PAIR)
-        fq = jnp.maximum(q_ref[:, lanes], 0)
-        numer = dot(fq, block, ((1,), (0,))) + intra_refs[which][:, pl.ds(at, PAIR)]
+        fq = jnp.maximum(q_ref[:, pl.ds(n * QUAD, QUAD)], 0)
+        numers.append(dot(fq, block, ((1,), (0,))) + intra_refs[which][:, pl.ds(at, QUAD)])
+    for n, numer in enumerate(numers):
+        there = pl.ds(pl.multiple_of(base + n * QUAD, QUAD), QUAD)
+        lanes = pl.ds(n * QUAD, QUAD)
         mean_sq = dot((numer * numer).astype(BF16), ones, ((1,), (0,)))
-        normed = numer * lax.rsqrt(mean_sq + EPS) * gain_ref[:, there]
-        out_buf[:, lanes] = normed.astype(BF16)
-        copies.append(pltpu.make_async_copy(out_buf.at[:, lanes], out_hbm.at[:, there], sems.at[p]))
-        copies[-1].start()
+        out[:, lanes] = (numer * lax.rsqrt(mean_sq + EPS) * gain_ref[:, there]).astype(BF16)
+        if ready:
+            copies.append(pltpu.make_async_copy(out.at[:, lanes], out_hbm.at[:, there], sems.at[0, n]))
+            copies[-1].start()
     wait_all(copies)
 
 
@@ -264,8 +278,8 @@
     tile = pltpu.VMEM((count, part), BF16)
     k, v, q = [None] * 4, [None] * 4, [None] * 4
 
-    def swap(x, level):
-        return lax.ppermute(x, AXIS, [(i, i ^ (1 << level)) for i in range(size)])
+    def swap(x, bits):
+        return lax.ppermute(x, AXIS, [(i, i ^ bits) for i in range(size)])
 
     def small(dtype):
         return pltpu.VMEM((quarter, PAIR), dtype)
@@ -273,7 +287,7 @@
     send, k[0], v[0], k[2], v[2] = call(
         first_kernel, (small(BF16), *[tile] * 4), (keys, values), specs=[HBM] * 2, scratch=[DMA((4,))]
     )
-    got = swap(send, 0)
+    got = swap(send, CORE)
     keep, k[1], v[1], k[3], v[3] = call(
         second_kernel,
         (small(F32), *[tile] * 4),
@@ -282,10 +296,10 @@
         scratch=[DMA((4,))],
         cost=(80_000_000, 2_000_000),
     )
-    send, ext_core2 = call(after_core, (small(BF16), small(F32)), (keep, got))
-    got = swap(send, 1)
+    send, mine, ext2 = call(after_core, (small(BF16), small(BF16), small(F32)), (keep, got))
+    got = swap(send, SIDE)
     send = call(third_kernel, small(BF16), (k[1], v[1]), cost=(80_000_000, 500_000))
-    got_core = swap(send, 0)
+    got_core = swap(send, CORE)
     keep, q[2], q[3], gain_vmem = call(
         fourth_kernel,
         (small(F32), tile, tile, pltpu.VMEM((1, width), F32)),
@@ -321,13 +335,11 @@
                 q[slot] = value
         parts.append(outs)
 
-    send, total, ext_core3, ext_side = call(
-        after_side, (small(BF16), *[small(F32)] * 3), (keep, got_core, got)
-    )
+    send, total, ext_core3, ext_side = call(after_side, (small(BF16), *[small(F32)] * 3), (keep, got_core, got))
     before = []
     level = 2
     while 1 << level < size:
-        got = swap(send, level)
+        got = swap(send, 1 << level)
         if 1 << (level + 1) < size:
             more = 1 << (level + 2) < size
             send, *before = call(
@@ -343,35 +355,40 @@
                 (small(BF16), small(BF16), small(BF16)),
                 [*before, got, ext_side, ext_core3],
             )
+        if level == 2:
+            ext0 = swap(mine, CORE)
         level += 1
-    got = swap(send, 1)
-    prior1 = swap(send_core, 0)
-    send_core, prior2 = call(after_base, (small(BF16), small(BF16)), (got, ext_core2))
-    prior0 = swap(send_core, 0)
-
-    out = None
-    for slot, prior in ((3, prior3), (1, prior1), (2, prior2), (0, prior0)):
+    prior0 = swap(send, CORE | SIDE)
+    prior2 = swap(send, SIDE)
+    prior1 = swap(send_core, CORE)
+    ext0 = call(lambda a, b: b.__setitem__(..., before_core(a)), small(F32), (ext0,))
+
+    ready, done = [], []
+    for slot, prior, ext in ((3, prior3, None), (1, prior1, None), (0, prior0, ext0), (2, prior2, ext2)):
         used, places = [], []
-        for pair in range(slot * part // PAIR, (slot + 1) * part // PAIR):
+        for pair in range(slot * part // PAIR, (slot + 1) * part // PAIR, 2):
             n = next(i for i, (low, high) in enumerate(groups) if low <= pair < high)
             if n not in used:
                 used.append(n)
             places.append((used.index(n), (pair - groups[n][0]) * PAIR))
-        args = [prior, q[slot], gain_vmem, *[parts[n] for n in used]]
-        specs = [VMEM] * len(args)
-        if out is not None:
-            args.append(out)
-            specs.append(ANY)
+        last = len(ready) == 3
+        args = [prior, q[slot], gain_vmem, *([] if ext is None else [ext]), *[parts[n] for n in used]]
         out = call(
-            packed(final_kernel, slot=slot, places=tuple(places)),
-            jax.ShapeDtypeStruct((count, width), BF16),
-            args,
-            specs=specs,
-            out_specs=ANY,
-            scratch=[pltpu.VMEM((count, part), BF16), DMA((part // PAIR,))],
-            alias={} if out is None else {len(args) - 1: 0},
+            packed(
+                final_kernel,
+                slot=slot,
+                places=tuple(places),
+                ext=ext is not None,
+                ready=tuple(ready) if last else (),
+            ),
+            jax.ShapeDtypeStruct((count, width), BF16) if last else tile,
+            [*args, *done] if last else args,
+            out_specs=ANY if last else None,
+            scratch=[tile, DMA((2, 3))] if last else (),
             cost=(50_000_000, 1_000_000),
         )
+        ready.append(slot)
+        done.append(out)
     return out
 
 

time: 32.5 us -> 28.4 us (0.87)
  waiting for transfers between devices: 8.05 us -> 5.65 us
  Pallas kernels: 13.1 us -> 11.3 us
    ppermute x8 -> x9, waiting for transfers between devices: 8.05 us -> 5.65 us  [swap(): return lax.ppermute(x, AXIS, [(i, i ^ bits) for i in range(size)])]
    pallas_call x16, Pallas kernels: 13.1 us -> 11.3 us  [call(): pl.pallas_call(kernel, out_shape=outs, in_specs=specs, out_specs=([VMEM]...]
    ppermute x8 -> x9, starting transfers between devices: 10.9 us -> 11.1 us  [swap(): return lax.ppermute(x, AXIS, [(i, i ^ bits) for i in range(size)])]
  transfers between devices with their start and end apart: 8 -> 9, of which waited for: 4 -> 3; matrix products, arithmetic and copies ran while one was open for 0% -> 0% of each run, Pallas kernels for 33% -> 30%
where the time goes in v7:
time: 28.4 us; the launch traced here: 28.2 us
  Pallas kernels  11.3 us (40%)
  starting transfers between devices  11.1 us (39%)
  waiting for transfers between devices  5.65 us (20%)
    pallas_call x16, Pallas kernels, call(): pl.pallas_call(kernel, out_shape=outs, in_specs=specs, out_specs=([VMEM]...  11.3 us
    ppermute x9, starting transfers between devices, swap(): return lax.ppermute(x, AXIS, [(i, i ^ bits) for i in range(size)])  11.1 us
    ppermute x9, waiting for transfers between devices, swap(): return lax.ppermute(x, AXIS, [(i, i ^ bits) for i in range(size)])  5.65 us
  transfers between devices with their start and end apart: 9, of which 3 were waited for; matrix products, arithmetic and copies ran while one was open for 0% of the time, Pallas kernels for 30%

profile of v7, /device:TPU:0, one launch (start us, length us, event | category | flops | bytes accessed | tf_op | source)
XLA Modules:
  0.0 28.2 jit_solution(6272372415865048794)
XLA Ops:
  0.0 1.4 %shard_map.46 = (bf16[256,128]{1,0:T(8,128)(2,1)S(1)}, bf16[256,512]{1,0:T(8,128)(2,1)S(1)}, bf16[256,512]{1,0:T(8,128)(2,1)S(1)}, bf16[256,512]{1,0:T(8,128)(2,1)S(1)}, bf16[256,512]{1,0:T(8,128)(2,1)S(1)}) custom-call(bf16[256,2048]{1,0:T(8,128)(2,1)} %k_hbm.3, bf16[256,2048]{1,0:T(8,128)(2,1)} %v_hbm.3), custom_call_target="tpu_custom_call" | custom-call | flops 10000 | bytes 10000 | tf_op jit(solution)/shard_map/pallas_call | solution.py:258
  1.4 0.6 %collective-permute-start.1 = (bf16[256,128]{1,0:T(8,128)(2,1)S(1)}, bf16[256,128]{1,0:T(8,128)(2,1)S(1)}, u32[]{:S(2)}, u32[]{:S(2)}) collective-permute-start(bf16[256,128]{1,0:T(8,128)(2,1)S(1)} %get-tuple-element.42), channel_id=1, source_target_pairs={{0,1},{1,0},{2,3},{3,2},{4,5},{5,4},{6,7},{7,6},{8,9},{9,8},{10,11... | collective-permute-start | bytes 196616 | tf_op jit(solution)/shard_map/ppermute | solution.py:282
  1.9 1.3 %shard_map.47 = (f32[256,128]{1,0:T(8,128)S(1)}, bf16[256,512]{1,0:T(8,128)(2,1)S(1)}, bf16[256,512]{1,0:T(8,128)(2,1)S(1)}, bf16[256,512]{1,0:T(8,128)(2,1)S(1)}, bf16[256,512]{1,0:T(8,128)(2,1)S(1)}) custom-call(bf16[256,2048]{1,0:T(8,128)(2,1)} %k_hbm.3, bf16[256,2048]{1,0:T(8,128)(2,1)} %v_hbm.3, bf16[256,512]{1,0:T(8,128)(2,1)S(1)} %get-tuple-element.34.k2.refs_3_, ...), custom_call_target="tpu_custom_call" | custom-call | flops 80000000 | bytes 2000000 | tf_op jit(solution)/shard_map/pallas_call | solution.py:258
  3.2 0.3 shard_map.49
  3.5 0.1 collective-permute-start
  3.6 0.0 collective-permute-done.1.got
  3.6 3.1 %collective-permute-start.2 = (bf16[256,128]{1,0:T(8,128)(2,1)S(1)}, bf16[256,128]{1,0:T(8,128)(2,1)S(1)}, u32[]{:S(2)}, u32[]{:S(2)}) collective-permute-start(bf16[256,128]{1,0:T(8,128)(2,1)S(1)} %get-tuple-element.43), channel_id=1, source_target_pairs={{0,2},{1,3},{2,0},{3,1},{4,6},{5,7},{6,4},{7,5},{8,10},{9,11},{10,... | collective-permute-start | bytes 196616 | tf_op jit(solution)/shard_map/ppermute | solution.py:282
  6.7 1.1 %shard_map.48 = (f32[256,128]{1,0:T(8,128)S(1)}, bf16[256,512]{1,0:T(8,128)(2,1)S(1)}, bf16[256,512]{1,0:T(8,128)(2,1)S(1)}, f32[1,2048]{1,0:T(1,128)S(1)}) custom-call(bf16[256,512]{1,0:T(8,128)(2,1)S(1)} %get-tuple-element.36.k3.refs_0_, bf16[256,512]{1,0:T(8,128)(2,1)S(1)} %get-tuple-element.37.v3.refs_1_, bf16[256,2048]{1,0:T(8,128)(2,1)} %refs_0_.1, ...), custom_call_target="tpu_custom_call" | custom-call | flops 80000000 | bytes 1000000 | tf_op jit(solution)/shard_map/pallas_call | solution.py:258
  7.8 0.0 collective-permute-done.got_core
  7.8 1.1 %collective-permute-done.2.got = bf16[256,128]{1,0:T(8,128)(2,1)S(1)} collective-permute-done((bf16[256,128]{1,0:T(8,128)(2,1)S(1)}, bf16[256,128]{1,0:T(8,128)(2,1)S(1)}, u32[]{:S(2)}, u32[]{:S(2)}) %collective-permute-start.2) | collective-permute-done | bytes 65568 | tf_op jit(solution)/shard_map/ppermute | solution.py:282
  9.0 2.1 %collective-permute-start.3 = (bf16[256,128]{1,0:T(8,128)(2,1)S(1)}, bf16[256,128]{1,0:T(8,128)(2,1)S(1)}, u32[]{:S(2)}, u32[]{:S(2)}) collective-permute-start(bf16[256,128]{1,0:T(8,128)(2,1)S(1)} %get-tuple-element.45), channel_id=1, source_target_pairs={{0,4},{1,5},{2,6},{3,7},{4,0},{5,1},{6,2},{7,3},{8,12},{9,13},{10,... | collective-permute-start | bytes 196616 | tf_op jit(solution)/shard_map/ppermute | solution.py:282
  11.1 2.2 %collective-permute-done.3.refs_1_ = bf16[256,128]{1,0:T(8,128)(2,1)S(1)} collective-permute-done((bf16[256,128]{1,0:T(8,128)(2,1)S(1)}, bf16[256,128]{1,0:T(8,128)(2,1)S(1)}, u32[]{:S(2)}, u32[]{:S(2)}) %collective-permute-start.3) | collective-permute-done | bytes 65568 | tf_op jit(solution)/shard_map/ppermute | solution.py:282
  13.4 3.1 %collective-permute-start.4 = (bf16[256,128]{1,0:T(8,128)(2,1)S(1)}, bf16[256,128]{1,0:T(8,128)(2,1)S(1)}, u32[]{:S(2)}, u32[]{:S(2)}) collective-permute-start(bf16[256,128]{1,0:T(8,128)(2,1)S(1)} %get-tuple-element.47), channel_id=1, source_target_pairs={{0,8},{1,9},{2,10},{3,11},{4,12},{5,13},{6,14},{7,15},{8,0},{9,1},... | collective-permute-start | bytes 196616 | tf_op jit(solution)/shard_map/ppermute | solution.py:282
  16.5 0.0 collective-permute-start.8
  16.5 2.2 %collective-permute-done.4.refs_1_ = bf16[256,128]{1,0:T(8,128)(2,1)S(1)} collective-permute-done((bf16[256,128]{1,0:T(8,128)(2,1)S(1)}, bf16[256,128]{1,0:T(8,128)(2,1)S(1)}, u32[]{:S(2)}, u32[]{:S(2)}) %collective-permute-start.4) | collective-permute-done | bytes 65568 | tf_op jit(solution)/shard_map/ppermute | solution.py:282
  18.7 0.1 shard_map.53
  18.8 0.1 collective-permute-start.6
  18.9 2.0 %collective-permute-start.7 = (bf16[256,128]{1,0:T(8,128)(2,1)S(1)}, bf16[256,128]{1,0:T(8,128)(2,1)S(1)}, u32[]{:S(2)}, u32[]{:S(2)}) collective-permute-start(bf16[256,128]{1,0:T(8,128)(2,1)S(1)} %get-tuple-element.50), channel_id=1, source_target_pairs={{0,3},{1,2},{2,1},{3,0},{4,7},{5,6},{6,5},{7,4},{8,11},{9,10},{10,... | collective-permute-start | bytes 196616 | tf_op jit(solution)/shard_map/ppermute | solution.py:282
  20.8 0.2 collective-permute-start.5
  21.0 1.0 %shard_map.55.refs_3_ = f32[256,512]{1,0:T(8,128)S(1)} custom-call(bf16[256,512]{1,0:T(8,128)(2,1)S(1)} %get-tuple-element.36.k3.refs_0_, bf16[256,512]{1,0:T(8,128)(2,1)S(1)} %get-tuple-element.37.v3.refs_1_, bf16[256,512]{1,0:T(8,128)(2,1)S(1)} %get-tuple-element.56.refs_2_.refs_1_), custom_call_target="tpu_custom_call" | custom-call | flops 200000000 | bytes 1500000 | tf_op jit(solution)/shard_map/pallas_call | solution.py:258
  22.0 2.2 %shard_map.54 = (f32[256,768]{1,0:T(8,128)S(1)}, bf16[256,512]{1,0:T(8,128)(2,1)S(1)}, bf16[256,512]{1,0:T(8,128)(2,1)S(1)}) custom-call(bf16[256,2048]{1,0:T(8,128)(2,1)} %refs_0_.1, bf16[256,512]{1,0:T(8,128)(2,1)S(1)} %get-tuple-element.39.k1.refs_1_.refs_2_, bf16[256,512]{1,0:T(8,128)(2,1)S(1)} %get-tuple-element.40.v1.refs_2_.refs_3_, ...), custom_call_target="tpu_custom_call" | custom-call | flops 200000000 | bytes 1500000 | tf_op jit(solution)/shard_map/pallas_call | solution.py:258
  24.2 1.4 %shard_map.57.refs_3_.refs_4_ = f32[256,768]{1,0:T(8,128)S(1)} custom-call(bf16[256,512]{1,0:T(8,128)(2,1)S(1)} %get-tuple-element.59.refs_0_, bf16[256,512]{1,0:T(8,128)(2,1)S(1)} %get-tuple-element.60.refs_1_, bf16[256,512]{1,0:T(8,128)(2,1)S(1)} %get-tuple-element.39.k1.refs_1_.refs_2_, bf16[256,512]{1,0:T(8,128)(2,1)S(1)} %get-tuple-element.40.v1.refs_2_.refs_3_, ...), custom_call_target="tpu_custom_call" | custom-call | flops 200000000 | bytes 1500000 | tf_op jit(solution)/shard_map/pallas_call | solution.py:258
  25.7 0.0 collective-permute-done.8.a
  25.7 0.4 %shard_map.56.refs_5_ = bf16[256,512]{1,0:T(8,128)(2,1)S(1)} custom-call(bf16[256,128]{1,0:T(8,128)(2,1)S(1)} %get-tuple-element.55.refs_0_, bf16[256,512]{1,0:T(8,128)(2,1)S(1)} %get-tuple-element.56.refs_2_.refs_1_, f32[1,2048]{1,0:T(1,128)S(1)} %get-tuple-element.52.refs_2_, f32[256,512]{1,0:T(8,128)S(1)} %shard_map.55.refs_3_), custom_call_target="tpu_custom_call" | custom-call | flops 50000000 | bytes 1000000 | tf_op jit(solution)/shard_map/pallas_call | solution.py:258
  26.1 0.0 collective-permute-done.6.refs_0_
  26.1 0.4 %shard_map.58.refs_6_ = bf16[256,512]{1,0:T(8,128)(2,1)S(1)} custom-call(bf16[256,128]{1,0:T(8,128)(2,1)S(1)} %collective-permute-done.6.refs_0_, bf16[256,512]{1,0:T(8,128)(2,1)S(1)} %get-tuple-element.58.refs_5_.refs_1_, f32[1,2048]{1,0:T(1,128)S(1)} %get-tuple-element.52.refs_2_, f32[256,768]{1,0:T(8,128)S(1)} %shard_map.57.refs_3_.refs_4_, ...), custom_call_target="tpu_custom_call" | custom-call | flops 50000000 | bytes 1000000 | tf_op jit(solution)/shard_map/pallas_call | solution.py:258
  26.5 0.0 collective-permute-done.7.refs_0_
  26.5 0.4 %shard_map.60.refs_7_ = bf16[256,512]{1,0:T(8,128)(2,1)S(1)} custom-call(bf16[256,128]{1,0:T(8,128)(2,1)S(1)} %collective-permute-done.7.refs_0_, bf16[256,512]{1,0:T(8,128)(2,1)S(1)} %get-tuple-element.61.refs_4_.refs_1_, f32[1,2048]{1,0:T(1,128)S(1)} %get-tuple-element.52.refs_2_, f32[256,128]{1,0:T(8,128)S(1)} %shard_map.59.refs_3_, ...), custom_call_target="tpu_custom_call" | custom-call | flops 50000000 | bytes 1000000 | tf_op jit(solution)/shard_map/pallas_call | solution.py:258
  26.9 0.0 collective-permute-done.5.refs_0_
  26.9 1.3 %shard_map.61 = bf16[256,2048]{1,0:T(8,128)(2,1)} custom-call(bf16[256,128]{1,0:T(8,128)(2,1)S(1)} %collective-permute-done.5.refs_0_, bf16[256,512]{1,0:T(8,128)(2,1)S(1)} %get-tuple-element.51.refs_5_.refs_1_, f32[1,2048]{1,0:T(1,128)S(1)} %get-tuple-element.52.refs_2_, f32[256,128]{1,0:T(8,128)S(1)} %get-tuple-element.53.refs_3_, ...), custom_call_target="tpu_custom_call" | custom-call | flops 50000000 | bytes 1000000 | tf_op jit(solution)/shard_map/pallas_call | solution.py:258
  (4 shorter events, 0.1 us)
Async XLA Ops:
  1.4 2.2 %collective-permute-start.1 = (bf16[256,128]{1,0:T(8,128)(2,1)S(1)}, bf16[256,128]{1,0:T(8,128)(2,1)S(1)}, u32[]{:S(2)}, u32[]{:S(2)}) collective-permute-start(bf16[256,128]{1,0:T(8,128)(2,1)S(1)} %get-tuple-element.42), channel_id=1, source_target_pairs={{0,1},{1,0},{2,3},{3,2},{4,5},{5,4},{6,7},{7,6},{8,9},{9,8},{10,11... | collective-permute-start | bytes 196616 | tf_op jit(solution)/shard_map/ppermute | solution.py:282
  3.5 4.3 %collective-permute-start = (bf16[256,128]{1,0:T(8,128)(2,1)S(1)}, bf16[256,128]{1,0:T(8,128)(2,1)S(1)}, u32[]{:S(2)}, u32[]{:S(2)}) collective-permute-start(bf16[256,128]{1,0:T(8,128)(2,1)S(1)} %shard_map.49), channel_id=1, source_target_pairs={{0,1},{1,0},{2,3},{3,2},{4,5},{5,4},{6,7},{7,6},{8,9},{9,8},{10,11... | collective-permute-start | bytes 196616 | tf_op jit(solution)/shard_map/ppermute | solution.py:282
  3.6 5.4 %collective-permute-start.2 = (bf16[256,128]{1,0:T(8,128)(2,1)S(1)}, bf16[256,128]{1,0:T(8,128)(2,1)S(1)}, u32[]{:S(2)}, u32[]{:S(2)}) collective-permute-start(bf16[256,128]{1,0:T(8,128)(2,1)S(1)} %get-tuple-element.43), channel_id=1, source_target_pairs={{0,2},{1,3},{2,0},{3,1},{4,6},{5,7},{6,4},{7,5},{8,10},{9,11},{10,... | collective-permute-start | bytes 196616 | tf_op jit(solution)/shard_map/ppermute | solution.py:282
  9.0 4.3 %collective-permute-start.3 = (bf16[256,128]{1,0:T(8,128)(2,1)S(1)}, bf16[256,128]{1,0:T(8,128)(2,1)S(1)}, u32[]{:S(2)}, u32[]{:S(2)}) collective-permute-start(bf16[256,128]{1,0:T(8,128)(2,1)S(1)} %get-tuple-element.45), channel_id=1, source_target_pairs={{0,4},{1,5},{2,6},{3,7},{4,0},{5,1},{6,2},{7,3},{8,12},{9,13},{10,... | collective-permute-start | bytes 196616 | tf_op jit(solution)/shard_map/ppermute | solution.py:282
  13.4 5.3 %collective-permute-start.4 = (bf16[256,128]{1,0:T(8,128)(2,1)S(1)}, bf16[256,128]{1,0:T(8,128)(2,1)S(1)}, u32[]{:S(2)}, u32[]{:S(2)}) collective-permute-start(bf16[256,128]{1,0:T(8,128)(2,1)S(1)} %get-tuple-element.47), channel_id=1, source_target_pairs={{0,8},{1,9},{2,10},{3,11},{4,12},{5,13},{6,14},{7,15},{8,0},{9,1},... | collective-permute-start | bytes 196616 | tf_op jit(solution)/shard_map/ppermute | solution.py:282
  16.5 9.2 %collective-permute-start.8 = (bf16[256,128]{1,0:T(8,128)(2,1)S(1)}, bf16[256,128]{1,0:T(8,128)(2,1)S(1)}, u32[]{:S(2)}, u32[]{:S(2)}) collective-permute-start(bf16[256,128]{1,0:T(8,128)(2,1)S(1)} %get-tuple-element.62), channel_id=1, source_target_pairs={{0,1},{1,0},{2,3},{3,2},{4,5},{5,4},{6,7},{7,6},{8,9},{9,8},{10,11... | collective-permute-start | bytes 196616 | tf_op jit(solution)/shard_map/ppermute | solution.py:282
  18.8 7.3 %collective-permute-start.6 = (bf16[256,128]{1,0:T(8,128)(2,1)S(1)}, bf16[256,128]{1,0:T(8,128)(2,1)S(1)}, u32[]{:S(2)}, u32[]{:S(2)}) collective-permute-start(bf16[256,128]{1,0:T(8,128)(2,1)S(1)} %get-tuple-element.57), channel_id=1, source_target_pairs={{0,1},{1,0},{2,3},{3,2},{4,5},{5,4},{6,7},{7,6},{8,9},{9,8},{10,11... | collective-permute-start | bytes 196616 | tf_op jit(solution)/shard_map/ppermute | solution.py:282
  18.9 7.6 %collective-permute-start.7 = (bf16[256,128]{1,0:T(8,128)(2,1)S(1)}, bf16[256,128]{1,0:T(8,128)(2,1)S(1)}, u32[]{:S(2)}, u32[]{:S(2)}) collective-permute-start(bf16[256,128]{1,0:T(8,128)(2,1)S(1)} %get-tuple-element.50), channel_id=1, source_target_pairs={{0,3},{1,2},{2,1},{3,0},{4,7},{5,6},{6,5},{7,4},{8,11},{9,10},{10,... | collective-permute-start | bytes 196616 | tf_op jit(solution)/shard_map/ppermute | solution.py:282
  20.8 6.1 %collective-permute-start.5 = (bf16[256,128]{1,0:T(8,128)(2,1)S(1)}, bf16[256,128]{1,0:T(8,128)(2,1)S(1)}, u32[]{:S(2)}, u32[]{:S(2)}) collective-permute-start(bf16[256,128]{1,0:T(8,128)(2,1)S(1)} %get-tuple-element.50), channel_id=1, source_target_pairs={{0,2},{1,3},{2,0},{3,1},{4,6},{5,7},{6,4},{7,5},{8,10},{9,11},{10,... | collective-permute-start | bytes 196616 | tf_op jit(solution)/shard_map/ppermute | solution.py:282

commit v8 on v7

--- a/solution.py
+++ b/solution.py
@@ -202,18 +202,20 @@
     wait_all(loads.values())
 
 
-def final_kernel(refs, *, slot, places, ext, ready):
+def final_kernel(refs, *, slot, places, ext, ready, store, held):
     refs = list(refs)
     prior_ref, q_ref, gain_ref = refs[:3]
     refs = refs[3:]
     ext_ref = refs.pop(0) if ext else None
     intra_refs = [refs.pop(0) for _ in range(1 + max(which for which, _ in places))]
     done = [refs.pop(0) for _ in ready]
+    if held:
+        refs.pop(0)
     out = refs.pop(0)
     part = q_ref.shape[1]
     base = slot_start(slot, part)
     copies = []
-    if ready:
+    if store:
         out_hbm, (out, sems) = out, refs
         for n, (other, src) in enumerate(zip(ready, done)):
             there = pl.ds(slot_start(other, part), part)
@@ -239,7 +241,7 @@
         lanes = pl.ds(n * QUAD, QUAD)
         mean_sq = dot((numer * numer).astype(BF16), ones, ((1,), (0,)))
         out[:, lanes] = (numer * lax.rsqrt(mean_sq + EPS) * gain_ref[:, there]).astype(BF16)
-        if ready:
+        if store:
             copies.append(pltpu.make_async_copy(out.at[:, lanes], out_hbm.at[:, there], sems.at[0, n]))
             copies[-1].start()
     wait_all(copies)
@@ -358,37 +360,50 @@
         if level == 2:
             ext0 = swap(mine, CORE)
         level += 1
+    prior2 = swap(send, SIDE)
     prior0 = swap(send, CORE | SIDE)
-    prior2 = swap(send, SIDE)
     prior1 = swap(send_core, CORE)
     ext0 = call(lambda a, b: b.__setitem__(..., before_core(a)), small(F32), (ext0,))
 
-    ready, done = [], []
-    for slot, prior, ext in ((3, prior3, None), (1, prior1, None), (0, prior0, ext0), (2, prior2, ext2)):
+    out, ready, done, waiting = None, [], [], []
+    for slot, prior, ext in ((3, prior3, None), (1, prior1, None), (2, prior2, ext2), (0, prior0, ext0)):
         used, places = [], []
         for pair in range(slot * part // PAIR, (slot + 1) * part // PAIR, 2):
             n = next(i for i, (low, high) in enumerate(groups) if low <= pair < high)
             if n not in used:
                 used.append(n)
             places.append((used.index(n), (pair - groups[n][0]) * PAIR))
-        last = len(ready) == 3
-        args = [prior, q[slot], gain_vmem, *([] if ext is None else [ext]), *[parts[n] for n in used]]
-        out = call(
+        store = slot % 2 == 0
+        args = [prior, q[slot], gain_vmem, *([] if ext is None else [ext]), *[parts[n] for n in used], *done]
+        specs = [VMEM] * len(args)
+        alias = {}
+        if out is not None:
+            alias = {len(args): 0}
+            args, specs = [*args, out], [*specs, ANY]
+        result = call(
             packed(
                 final_kernel,
                 slot=slot,
                 places=tuple(places),
                 ext=ext is not None,
-                ready=tuple(ready) if last else (),
+                ready=tuple(ready),
+                store=store,
+                held=out is not None,
             ),
-            jax.ShapeDtypeStruct((count, width), BF16) if last else tile,
-            [*args, *done] if last else args,
-            out_specs=ANY if last else None,
-            scratch=[tile, DMA((2, 3))] if last else (),
+            jax.ShapeDtypeStruct((count, width), BF16) if store else tile,
+            args,
+            specs=specs,
+            out_specs=ANY if store else None,
+            scratch=[tile, DMA((2, 3))] if store else (),
+            alias=alias,
             cost=(50_000_000, 1_000_000),
         )
-        ready.append(slot)
-        done.append(out)
+        if store:
+            out, ready, done = result, [], []
+        else:
+            waiting.append((slot, result))
+            if len(waiting) == 2:
+                ready, done = [list(x) for x in zip(*waiting)]
     return out
 
 

time: 28.4 us -> 28.9 us (1.018)
  Pallas kernels: 11.3 us -> 12 us
    pallas_call x16, Pallas kernels: 11.3 us -> 12 us  [call(): pl.pallas_call(kernel, out_shape=outs, in_specs=specs, out_specs=([VMEM]...]
  transfers between devices with their start and end apart: 9 -> 9, of which waited for: 3 -> 3; matrix products, arithmetic and copies ran while one was open for 0% -> 0% of each run, Pallas kernels for 30% -> 33%
where the time goes in v8:
time: 28.9 us; the launch traced here: 28.7 us
  Pallas kernels  12 us (42%)
  starting transfers between devices  10.9 us (38%)
  waiting for transfers between devices  5.65 us (20%)
    pallas_call x16, Pallas kernels, call(): pl.pallas_call(kernel, out_shape=outs, in_specs=specs, out_specs=([VMEM]...  12 us
    ppermute x9, starting transfers between devices, swap(): return lax.ppermute(x, AXIS, [(i, i ^ bits) for i in range(size)])  10.9 us
    ppermute x9, waiting for transfers between devices, swap(): return lax.ppermute(x, AXIS, [(i, i ^ bits) for i in range(size)])  5.65 us
  transfers between devices with their start and end apart: 9, of which 3 were waited for; matrix products, arithmetic and copies ran while one was open for 0% of the time, Pallas kernels for 33%

profile of v8, /device:TPU:0, one launch (start us, length us, event | category | flops | bytes accessed | tf_op | source)
XLA Modules:
  0.0 28.7 jit_solution(11905273133261209510)
XLA Ops:
  0.0 1.4 %shard_map.46 = (bf16[256,128]{1,0:T(8,128)(2,1)S(1)}, bf16[256,512]{1,0:T(8,128)(2,1)S(1)}, bf16[256,512]{1,0:T(8,128)(2,1)S(1)}, bf16[256,512]{1,0:T(8,128)(2,1)S(1)}, bf16[256,512]{1,0:T(8,128)(2,1)S(1)}) custom-call(bf16[256,2048]{1,0:T(8,128)(2,1)} %k_hbm.3, bf16[256,2048]{1,0:T(8,128)(2,1)} %v_hbm.3), custom_call_target="tpu_custom_call" | custom-call | flops 10000 | bytes 10000 | tf_op jit(solution)/shard_map/pallas_call | solution.py:260
  1.4 0.6 %collective-permute-start.1 = (bf16[256,128]{1,0:T(8,128)(2,1)S(1)}, bf16[256,128]{1,0:T(8,128)(2,1)S(1)}, u32[]{:S(2)}, u32[]{:S(2)}) collective-permute-start(bf16[256,128]{1,0:T(8,128)(2,1)S(1)} %get-tuple-element.42), channel_id=1, source_target_pairs={{0,1},{1,0},{2,3},{3,2},{4,5},{5,4},{6,7},{7,6},{8,9},{9,8},{10,11... | collective-permute-start | bytes 196616 | tf_op jit(solution)/shard_map/ppermute | solution.py:284
  1.9 1.3 %shard_map.47 = (f32[256,128]{1,0:T(8,128)S(1)}, bf16[256,512]{1,0:T(8,128)(2,1)S(1)}, bf16[256,512]{1,0:T(8,128)(2,1)S(1)}, bf16[256,512]{1,0:T(8,128)(2,1)S(1)}, bf16[256,512]{1,0:T(8,128)(2,1)S(1)}) custom-call(bf16[256,2048]{1,0:T(8,128)(2,1)} %k_hbm.3, bf16[256,2048]{1,0:T(8,128)(2,1)} %v_hbm.3, bf16[256,512]{1,0:T(8,128)(2,1)S(1)} %get-tuple-element.34.k2.refs_3_, ...), custom_call_target="tpu_custom_call" | custom-call | flops 80000000 | bytes 2000000 | tf_op jit(solution)/shard_map/pallas_call | solution.py:260
  3.2 0.3 shard_map.49
  3.5 0.1 collective-permute-start
  3.6 0.0 collective-permute-done.1.got
  3.6 3.1 %collective-permute-start.2 = (bf16[256,128]{1,0:T(8,128)(2,1)S(1)}, bf16[256,128]{1,0:T(8,128)(2,1)S(1)}, u32[]{:S(2)}, u32[]{:S(2)}) collective-permute-start(bf16[256,128]{1,0:T(8,128)(2,1)S(1)} %get-tuple-element.43), channel_id=1, source_target_pairs={{0,2},{1,3},{2,0},{3,1},{4,6},{5,7},{6,4},{7,5},{8,10},{9,11},{10,... | collective-permute-start | bytes 196616 | tf_op jit(solution)/shard_map/ppermute | solution.py:284
  6.7 1.1 %shard_map.48 = (f32[256,128]{1,0:T(8,128)S(1)}, bf16[256,512]{1,0:T(8,128)(2,1)S(1)}, bf16[256,512]{1,0:T(8,128)(2,1)S(1)}, f32[1,2048]{1,0:T(1,128)S(1)}) custom-call(bf16[256,512]{1,0:T(8,128)(2,1)S(1)} %get-tuple-element.36.k3.refs_0_, bf16[256,512]{1,0:T(8,128)(2,1)S(1)} %get-tuple-element.37.v3.refs_1_, bf16[256,2048]{1,0:T(8,128)(2,1)} %refs_0_.1, ...), custom_call_target="tpu_custom_call" | custom-call | flops 80000000 | bytes 1000000 | tf_op jit(solution)/shard_map/pallas_call | solution.py:260
  7.8 0.0 collective-permute-done.got_core
  7.8 1.1 %collective-permute-done.2.got = bf16[256,128]{1,0:T(8,128)(2,1)S(1)} collective-permute-done((bf16[256,128]{1,0:T(8,128)(2,1)S(1)}, bf16[256,128]{1,0:T(8,128)(2,1)S(1)}, u32[]{:S(2)}, u32[]{:S(2)}) %collective-permute-start.2) | collective-permute-done | bytes 65568 | tf_op jit(solution)/shard_map/ppermute | solution.py:284
  9.0 2.1 %collective-permute-start.3 = (bf16[256,128]{1,0:T(8,128)(2,1)S(1)}, bf16[256,128]{1,0:T(8,128)(2,1)S(1)}, u32[]{:S(2)}, u32[]{:S(2)}) collective-permute-start(bf16[256,128]{1,0:T(8,128)(2,1)S(1)} %get-tuple-element.45), channel_id=1, source_target_pairs={{0,4},{1,5},{2,6},{3,7},{4,0},{5,1},{6,2},{7,3},{8,12},{9,13},{10,... | collective-permute-start | bytes 196616 | tf_op jit(solution)/shard_map/ppermute | solution.py:284
  11.1 2.2 %collective-permute-done.3.refs_1_ = bf16[256,128]{1,0:T(8,128)(2,1)S(1)} collective-permute-done((bf16[256,128]{1,0:T(8,128)(2,1)S(1)}, bf16[256,128]{1,0:T(8,128)(2,1)S(1)}, u32[]{:S(2)}, u32[]{:S(2)}) %collective-permute-start.3) | collective-permute-done | bytes 65568 | tf_op jit(solution)/shard_map/ppermute | solution.py:284
  13.4 3.1 %collective-permute-start.4 = (bf16[256,128]{1,0:T(8,128)(2,1)S(1)}, bf16[256,128]{1,0:T(8,128)(2,1)S(1)}, u32[]{:S(2)}, u32[]{:S(2)}) collective-permute-start(bf16[256,128]{1,0:T(8,128)(2,1)S(1)} %get-tuple-element.47), channel_id=1, source_target_pairs={{0,8},{1,9},{2,10},{3,11},{4,12},{5,13},{6,14},{7,15},{8,0},{9,1},... | collective-permute-start | bytes 196616 | tf_op jit(solution)/shard_map/ppermute | solution.py:284
  16.5 0.0 collective-permute-start.6
  16.5 2.2 %collective-permute-done.4.refs_1_ = bf16[256,128]{1,0:T(8,128)(2,1)S(1)} collective-permute-done((bf16[256,128]{1,0:T(8,128)(2,1)S(1)}, bf16[256,128]{1,0:T(8,128)(2,1)S(1)}, u32[]{:S(2)}, u32[]{:S(2)}) %collective-permute-start.4) | collective-permute-done | bytes 65568 | tf_op jit(solution)/shard_map/ppermute | solution.py:284
  18.7 0.1 shard_map.53
  18.8 0.1 collective-permute-start.8
  18.9 1.9 %collective-permute-start.7 = (bf16[256,128]{1,0:T(8,128)(2,1)S(1)}, bf16[256,128]{1,0:T(8,128)(2,1)S(1)}, u32[]{:S(2)}, u32[]{:S(2)}) collective-permute-start(bf16[256,128]{1,0:T(8,128)(2,1)S(1)} %get-tuple-element.50), channel_id=1, source_target_pairs={{0,2},{1,3},{2,0},{3,1},{4,6},{5,7},{6,4},{7,5},{8,10},{9,11},{10,... | collective-permute-start | bytes 196616 | tf_op jit(solution)/shard_map/ppermute | solution.py:284
  20.8 0.0 collective-permute-start.5
  20.8 1.0 %shard_map.57.refs_3_ = f32[256,512]{1,0:T(8,128)S(1)} custom-call(bf16[256,512]{1,0:T(8,128)(2,1)S(1)} %get-tuple-element.36.k3.refs_0_, bf16[256,512]{1,0:T(8,128)(2,1)S(1)} %get-tuple-element.37.v3.refs_1_, bf16[256,512]{1,0:T(8,128)(2,1)S(1)} %get-tuple-element.61.refs_2_.refs_1_), custom_call_target="tpu_custom_call" | custom-call | flops 200000000 | bytes 1500000 | tf_op jit(solution)/shard_map/pallas_call | solution.py:260
  21.8 2.2 %shard_map.54 = (f32[256,768]{1,0:T(8,128)S(1)}, bf16[256,512]{1,0:T(8,128)(2,1)S(1)}, bf16[256,512]{1,0:T(8,128)(2,1)S(1)}) custom-call(bf16[256,2048]{1,0:T(8,128)(2,1)} %refs_0_.1, bf16[256,512]{1,0:T(8,128)(2,1)S(1)} %get-tuple-element.39.k1.refs_1_.refs_2_, bf16[256,512]{1,0:T(8,128)(2,1)S(1)} %get-tuple-element.40.v1.refs_2_.refs_3_, ...), custom_call_target="tpu_custom_call" | custom-call | flops 200000000 | bytes 1500000 | tf_op jit(solution)/shard_map/pallas_call | solution.py:260
  24.1 1.4 %shard_map.56.refs_3_.refs_4_ = f32[256,768]{1,0:T(8,128)S(1)} custom-call(bf16[256,512]{1,0:T(8,128)(2,1)S(1)} %get-tuple-element.55.refs_0_, bf16[256,512]{1,0:T(8,128)(2,1)S(1)} %get-tuple-element.56.refs_1_, bf16[256,512]{1,0:T(8,128)(2,1)S(1)} %get-tuple-element.39.k1.refs_1_.refs_2_, bf16[256,512]{1,0:T(8,128)(2,1)S(1)} %get-tuple-element.40.v1.refs_2_.refs_3_, ...), custom_call_target="tpu_custom_call" | custom-call | flops 200000000 | bytes 1500000 | tf_op jit(solution)/shard_map/pallas_call | solution.py:260
  25.5 0.0 collective-permute-done.6.a
  25.5 0.4 %shard_map.58.refs_5_ = bf16[256,512]{1,0:T(8,128)(2,1)S(1)} custom-call(bf16[256,128]{1,0:T(8,128)(2,1)S(1)} %get-tuple-element.60.refs_0_, bf16[256,512]{1,0:T(8,128)(2,1)S(1)} %get-tuple-element.61.refs_2_.refs_1_, f32[1,2048]{1,0:T(1,128)S(1)} %get-tuple-element.53.refs_2_, f32[256,512]{1,0:T(8,128)S(1)} %shard_map.57.refs_3_), custom_call_target="tpu_custom_call" | custom-call | flops 50000000 | bytes 1000000 | tf_op jit(solution)/shard_map/pallas_call | solution.py:260
  25.9 0.0 collective-permute-done.8.refs_0_
  25.9 0.4 %shard_map.59.refs_6_ = bf16[256,512]{1,0:T(8,128)(2,1)S(1)} custom-call(bf16[256,128]{1,0:T(8,128)(2,1)S(1)} %collective-permute-done.8.refs_0_, bf16[256,512]{1,0:T(8,128)(2,1)S(1)} %get-tuple-element.57.refs_5_.refs_1_, f32[1,2048]{1,0:T(1,128)S(1)} %get-tuple-element.53.refs_2_, f32[256,768]{1,0:T(8,128)S(1)} %shard_map.56.refs_3_.refs_4_, ...), custom_call_target="tpu_custom_call" | custom-call | flops 50000000 | bytes 1000000 | tf_op jit(solution)/shard_map/pallas_call | solution.py:260
  26.3 0.0 collective-permute-done.7.refs_0_
  26.3 1.2 %shard_map.60.refs_5_ = bf16[256,2048]{1,0:T(8,128)(2,1)} custom-call(bf16[256,128]{1,0:T(8,128)(2,1)S(1)} %collective-permute-done.7.refs_0_, bf16[256,512]{1,0:T(8,128)(2,1)S(1)} %get-tuple-element.51.refs_5_.refs_1_, f32[1,2048]{1,0:T(1,128)S(1)} %get-tuple-element.53.refs_2_, f32[256,128]{1,0:T(8,128)S(1)} %get-tuple-element.58.refs_3_, ...), custom_call_target="tpu_custom_call" | custom-call | flops 50000000 | bytes 1000000 | tf_op jit(solution)/shard_map/pallas_call | solution.py:260
  27.5 0.0 collective-permute-done.5.refs_0_
  27.6 1.2 %shard_map.61 = bf16[256,2048]{1,0:T(8,128)(2,1)} custom-call(bf16[256,128]{1,0:T(8,128)(2,1)S(1)} %collective-permute-done.5.refs_0_, bf16[256,512]{1,0:T(8,128)(2,1)S(1)} %get-tuple-element.52.refs_4_.refs_1_, f32[1,2048]{1,0:T(1,128)S(1)} %get-tuple-element.53.refs_2_, f32[256,128]{1,0:T(8,128)S(1)} %shard_map.55.refs_3_, ...), custom_call_target="tpu_custom_call", output_to_operand_aliasing={{}: (5, {})} | custom-call | flops 50000000 | bytes 1000000 | tf_op jit(solution)/shard_map/pallas_call | solution.py:260
  (4 shorter events, 0.1 us)
Async XLA Ops:
  1.4 2.2 %collective-permute-start.1 = (bf16[256,128]{1,0:T(8,128)(2,1)S(1)}, bf16[256,128]{1,0:T(8,128)(2,1)S(1)}, u32[]{:S(2)}, u32[]{:S(2)}) collective-permute-start(bf16[256,128]{1,0:T(8,128)(2,1)S(1)} %get-tuple-element.42), channel_id=1, source_target_pairs={{0,1},{1,0},{2,3},{3,2},{4,5},{5,4},{6,7},{7,6},{8,9},{9,8},{10,11... | collective-permute-start | bytes 196616 | tf_op jit(solution)/shard_map/ppermute | solution.py:284
  3.5 4.3 %collective-permute-start = (bf16[256,128]{1,0:T(8,128)(2,1)S(1)}, bf16[256,128]{1,0:T(8,128)(2,1)S(1)}, u32[]{:S(2)}, u32[]{:S(2)}) collective-permute-start(bf16[256,128]{1,0:T(8,128)(2,1)S(1)} %shard_map.49), channel_id=1, source_target_pairs={{0,1},{1,0},{2,3},{3,2},{4,5},{5,4},{6,7},{7,6},{8,9},{9,8},{10,11... | collective-permute-start | bytes 196616 | tf_op jit(solution)/shard_map/ppermute | solution.py:284
  3.6 5.3 %collective-permute-start.2 = (bf16[256,128]{1,0:T(8,128)(2,1)S(1)}, bf16[256,128]{1,0:T(8,128)(2,1)S(1)}, u32[]{:S(2)}, u32[]{:S(2)}) collective-permute-start(bf16[256,128]{1,0:T(8,128)(2,1)S(1)} %get-tuple-element.43), channel_id=1, source_target_pairs={{0,2},{1,3},{2,0},{3,1},{4,6},{5,7},{6,4},{7,5},{8,10},{9,11},{10,... | collective-permute-start | bytes 196616 | tf_op jit(solution)/shard_map/ppermute | solution.py:284
  9.0 4.3 %collective-permute-start.3 = (bf16[256,128]{1,0:T(8,128)(2,1)S(1)}, bf16[256,128]{1,0:T(8,128)(2,1)S(1)}, u32[]{:S(2)}, u32[]{:S(2)}) collective-permute-start(bf16[256,128]{1,0:T(8,128)(2,1)S(1)} %get-tuple-element.45), channel_id=1, source_target_pairs={{0,4},{1,5},{2,6},{3,7},{4,0},{5,1},{6,2},{7,3},{8,12},{9,13},{10,... | collective-permute-start | bytes 196616 | tf_op jit(solution)/shard_map/ppermute | solution.py:284
  13.4 5.3 %collective-permute-start.4 = (bf16[256,128]{1,0:T(8,128)(2,1)S(1)}, bf16[256,128]{1,0:T(8,128)(2,1)S(1)}, u32[]{:S(2)}, u32[]{:S(2)}) collective-permute-start(bf16[256,128]{1,0:T(8,128)(2,1)S(1)} %get-tuple-element.47), channel_id=1, source_target_pairs={{0,8},{1,9},{2,10},{3,11},{4,12},{5,13},{6,14},{7,15},{8,0},{9,1},... | collective-permute-start | bytes 196616 | tf_op jit(solution)/shard_map/ppermute | solution.py:284
  16.5 9.0 %collective-permute-start.6 = (bf16[256,128]{1,0:T(8,128)(2,1)S(1)}, bf16[256,128]{1,0:T(8,128)(2,1)S(1)}, u32[]{:S(2)}, u32[]{:S(2)}) collective-permute-start(bf16[256,128]{1,0:T(8,128)(2,1)S(1)} %get-tuple-element.54), channel_id=1, source_target_pairs={{0,1},{1,0},{2,3},{3,2},{4,5},{5,4},{6,7},{7,6},{8,9},{9,8},{10,11... | collective-permute-start | bytes 196616 | tf_op jit(solution)/shard_map/ppermute | solution.py:284
  18.8 7.1 %collective-permute-start.8 = (bf16[256,128]{1,0:T(8,128)(2,1)S(1)}, bf16[256,128]{1,0:T(8,128)(2,1)S(1)}, u32[]{:S(2)}, u32[]{:S(2)}) collective-permute-start(bf16[256,128]{1,0:T(8,128)(2,1)S(1)} %get-tuple-element.62), channel_id=1, source_target_pairs={{0,1},{1,0},{2,3},{3,2},{4,5},{5,4},{6,7},{7,6},{8,9},{9,8},{10,11... | collective-permute-start | bytes 196616 | tf_op jit(solution)/shard_map/ppermute | solution.py:284
  18.9 7.5 %collective-permute-start.7 = (bf16[256,128]{1,0:T(8,128)(2,1)S(1)}, bf16[256,128]{1,0:T(8,128)(2,1)S(1)}, u32[]{:S(2)}, u32[]{:S(2)}) collective-permute-start(bf16[256,128]{1,0:T(8,128)(2,1)S(1)} %get-tuple-element.50), channel_id=1, source_target_pairs={{0,2},{1,3},{2,0},{3,1},{4,6},{5,7},{6,4},{7,5},{8,10},{9,11},{10,... | collective-permute-start | bytes 196616 | tf_op jit(solution)/shard_map/ppermute | solution.py:284
  20.8 6.7 %collective-permute-start.5 = (bf16[256,128]{1,0:T(8,128)(2,1)S(1)}, bf16[256,128]{1,0:T(8,128)(2,1)S(1)}, u32[]{:S(2)}, u32[]{:S(2)}) collective-permute-start(bf16[256,128]{1,0:T(8,128)(2,1)S(1)} %get-tuple-element.50), channel_id=1, source_target_pairs={{0,3},{1,2},{2,1},{3,0},{4,7},{5,6},{6,5},{7,4},{8,11},{9,10},{10,... | collective-permute-start | bytes 196616 | tf_op jit(solution)/shard_map/ppermute | solution.py:284

commit v9 on v0

v9 whole, which is shorter than its diff:
```python
import functools

import jax
import jax.numpy as jnp
from jax import lax
from jax.experimental import pallas as pl
from jax.experimental.pallas import tpu as pltpu
from jax.sharding import PartitionSpec as P


HEAD_DIM = 64
PAIR = 2 * HEAD_DIM
QUAD = 4 * HEAD_DIM
SHIFT = 6
CORE, SIDE = 1, 2
EPS = 1e-05
AXIS = "seq"
BF16, F32 = jnp.bfloat16, jnp.float32


def bit_of(level):
    return (lax.axis_index(AXIS) >> level) & 1


def first_lanes(shape):
    return lax.broadcasted_iota(jnp.int32, shape, len(shape) - 1) < HEAD_DIM


def dot(a, b, dims):
    return lax.dot_general(a, b, (dims, ((), ())), preferred_element_type=F32)


def half_start(own, half):
    core = bit_of(0)
    return pl.multiple_of((core if own else 1 - core) * half, half)


def load_half(src, dst, own, sem, start=0, width=None):
    half = dst.shape[1]
    width = half if width is None else width
    there = pl.ds(pl.multiple_of(half_start(own, half) + start, width), width)
    load = pltpu.make_async_copy(src.at[:, there], dst.at[:, pl.ds(start, width)], sem)
    load.start()
    return load


def wait_all(loads):
    for load in loads:
        load.wait()


def states_of(k_ref, v_ref, out_ref, quads):
    first = first_lanes((HEAD_DIM, PAIR))
    for quad in quads:
        lanes = pl.ds(quad * QUAD, QUAD)
        fk = jnp.maximum(k_ref[:, lanes], 0)
        full = dot(fk, v_ref[:, lanes], ((0,), (0,)))
        for p in range(2):
            top = p * PAIR
            rows = full[top : top + PAIR, top : top + PAIR]
            packed = jnp.where(first, rows[:HEAD_DIM], rows[HEAD_DIM:])
            out_ref[pl.ds((quad * 2 + p) * HEAD_DIM, HEAD_DIM), :] = packed.astype(out_ref.dtype)


def first_kernel(k_hbm, v_hbm, send, k_other, v_other, k_own, v_own, sems):
    half = k_other.shape[1]
    part = half // 2
    loads = []
    for n in range(2):
        for m, (src, dst) in enumerate(((k_hbm, k_other), (v_hbm, v_other))):
            loads.append(load_half(src, dst, False, sems.at[n, m], n * part, part))
    late = [load_half(src, dst, True, sems.at[2, m]) for m, (src, dst) in enumerate(((k_hbm, k_own), (v_hbm, v_own)))]
    quads = part // QUAD
    for n in range(2):
        wait_all(loads[2 * n : 2 * n + 2])
        states_of(k_other, v_other, send, range(n * quads, (n + 1) * quads))
    wait_all(late)


def second_kernel(k_own, v_own, q_hbm, gain_hbm, keep, q_own, gain, sems):
    loads = [load_half(q_hbm, q_own, True, sems.at[0]), pltpu.make_async_copy(gain_hbm, gain, sems.at[1])]
    loads[1].start()
    states_of(k_own, v_own, keep, range(k_own.shape[1] // QUAD))
    wait_all(loads)


def after_core(keep, got, send, total, ext):
    state, other = keep[...], got[...].astype(F32)
    value = state + other
    send[...] = value.astype(BF16)
    total[...] = value
    ext[...] = jnp.where(bit_of(0) == 0, state, other)


def later_of(n, rounds):
    low = bit_of(1 + n)
    return jnp.where(bit_of(0) == 0, low, bit_of(2 + n)) if n + 1 < rounds else low


def with_got(before, got, n, rounds):
    value = got[...].astype(F32)
    taken = later_of(n, rounds) == 1
    if n + 1 == rounds:
        taken = jnp.logical_or(taken, bit_of(0) == 1)
    value = jnp.where(taken, value, 0.0)
    return value if before is None else before[...] + value


def after_round(refs, *, n, rounds):
    refs = list(refs)
    before = refs.pop(0) if n else None
    total, got, *refs = refs
    sent = total[...] + got[...].astype(F32)
    value = with_got(before, got, n, rounds)
    if n + 2 == rounds:
        chip, send, before_out = refs
        share = value + jnp.where(bit_of(1) == 0, chip[...], 0.0)
        send[...] = jnp.where(bit_of(0) == 0, sent, share).astype(BF16)
    else:
        send, before_out, total_out = refs
        send[...] = sent.astype(BF16)
        total_out[...] = sent
    before_out[...] = value


def after_last(before, got, ext, send, prior, *, n, rounds):
    base = with_got(before, got, n, rounds)
    ahead = base + ext[...]
    first = bit_of(0) == 0
    send[...] = jnp.where(first, ahead, base).astype(BF16)
    prior[...] = jnp.where(first, base, ahead).astype(BF16)


def intra_kernel(refs, *, fetch):
    q_hbm = refs[0] if fetch else None
    q_ref, k_ref, v_ref, intra_ref, *refs = refs[1:] if fetch else refs
    loads = [load_half(q_hbm, refs[0], False, refs[1].at[0])] if fetch else []
    count, half = intra_ref.shape
    mid = count // 2
    first = first_lanes((count, PAIR))
    rows = lax.broadcasted_iota(jnp.int32, (mid, mid), 0)
    cols = lax.broadcasted_iota(jnp.int32, (mid, mid), 1)
    causal = cols <= rows
    for p in range(half // PAIR):
        lanes = pl.ds(p * PAIR, PAIR)
        fq = jnp.maximum(q_ref[:, lanes], 0)
        fk = jnp.maximum(k_ref[:, lanes], 0)
        val = v_ref[:, lanes]
        zero = jnp.zeros_like(fq)
        top, low, weights = [], [], []
        for h in range(2):
            mine = first if h == 0 else jnp.logical_not(first)
            mine_q = jnp.where(mine, fq, zero)
            s_top = dot(mine_q[:mid], fk[:mid], ((1,), (1,)))
            s_low = dot(mine_q[mid:], fk, ((1,), (1,)))
            s_top = jnp.where(causal, s_top, 0.0).astype(BF16)
            s_diag = jnp.where(causal, s_low[:, mid:], 0.0).astype(BF16)
            s_low = jnp.concatenate([s_low[:, :mid].astype(BF16), s_diag], axis=1)
            top.append(s_top)
            low.append(s_low)
            weights.append(jnp.where(mine, val, zero))
        w_top = jnp.concatenate([w[:mid] for w in weights], axis=0)
        intra_ref[:mid, lanes] = dot(jnp.concatenate(top, axis=1), w_top, ((1,), (0,)))
        w_low = jnp.concatenate(weights, axis=0)
        intra_ref[mid:, lanes] = dot(jnp.concatenate(low, axis=1), w_low, ((1,), (0,)))
    wait_all(loads)


def final_kernel(refs, *, own):
    prior_ref, q_ref, gain_ref, intra_ref = refs[:4]
    out_hbm, out_buf, sems = refs[-3:]
    half = out_buf.shape[1]
    base = half_start(own, half)
    lane = lax.broadcasted_iota(jnp.int32, (QUAD, QUAD), 1) >> SHIFT
    row = lax.broadcasted_iota(jnp.int32, (QUAD, QUAD), 0) >> SHIFT
    same = lane == row
    ones = jnp.where(same, 1.0 / HEAD_DIM, 0.0).astype(BF16)
    copies = []
    GROUP = 2
    for start in range(0, half // QUAD, GROUP):
        numers = []
        for n in range(start, start + GROUP):
            one = prior_ref[pl.ds(n * PAIR, HEAD_DIM), :]
            two = prior_ref[pl.ds(n * PAIR + HEAD_DIM, HEAD_DIM), :]
            block = jnp.concatenate([jnp.concatenate([one, two], axis=1)] * 4, axis=0)
            block = jnp.where(same, block, jnp.zeros_like(block))
            lanes = pl.ds(n * QUAD, QUAD)
            fq = jnp.maximum(q_ref[:, lanes], 0)
            numers.append(dot(fq, block, ((1,), (0,))) + intra_ref[:, lanes])
        for n, numer in enumerate(numers, start):
            lanes = pl.ds(n * QUAD, QUAD)
            there = pl.ds(pl.multiple_of(base + n * QUAD, QUAD), QUAD)
            mean_sq = dot((numer * numer).astype(BF16), ones, ((1,), (0,)))
            out_buf[:, lanes] = (numer * lax.rsqrt(mean_sq + EPS) * gain_ref[:, there]).astype(BF16)
            copies.append(pltpu.make_async_copy(out_buf.at[:, lanes], out_hbm.at[:, there], sems.at[n]))
            copies[-1].start()
    wait_all(copies)


ANY = pl.BlockSpec(memory_space=pl.ANY)
HBM = pl.BlockSpec(memory_space=pltpu.HBM)
VMEM = pl.BlockSpec(memory_space=pltpu.VMEM)
DMA = pltpu.SemaphoreType.DMA


def call(kernel, outs, args, specs=None, out_specs=None, scratch=(), alias=None, cost=(10_000, 10_000)):
    specs = [VMEM] * len(args) if specs is None else specs
    args = [a if s is ANY else pltpu.with_memory_space_constraint(a, s.memory_space) for a, s in zip(args, specs)]
    many = isinstance(outs, (tuple, list))
    return pl.pallas_call(
        kernel,
        out_shape=outs,
        in_specs=specs,
        out_specs=([VMEM] * len(outs) if many else VMEM) if out_specs is None else out_specs,
        scratch_shapes=scratch,
        input_output_aliases=alias or {},
        compiler_params=pltpu.CompilerParams(vmem_limit_bytes=12 * 2**20),
        cost_estimate=pl.CostEstimate(flops=cost[0], transcendentals=0, bytes_accessed=cost[1]),
    )(*args)


def packed(kernel, **static):
    return lambda *refs: kernel(refs, **static)


def on_device(queries, keys, values, gain, *, size):
    count, width = queries.shape
    half = width // 2
    rows = half // PAIR * HEAD_DIM
    rounds = size.bit_length() - 2
    tile = pltpu.VMEM((count, half), BF16)
    small16, small32 = pltpu.VMEM((rows, PAIR), BF16), pltpu.VMEM((rows, PAIR), F32)

    def swap(x, even, odd):
        return lax.ppermute(x, AXIS, [(i, i ^ (odd if i & CORE else even)) for i in range(size)])

    send, k_other, v_other, k_own, v_own = call(
        first_kernel, (small16, *[tile] * 4), (keys, values), specs=[HBM] * 2, scratch=[DMA((3, 2))]
    )
    got = swap(send, CORE, CORE)
    keep, q_own, gain_vmem = call(
        second_kernel,
        (small32, tile, pltpu.VMEM((1, width), F32)),
        (k_own, v_own, queries, gain[None, :]),
        specs=[VMEM] * 2 + [HBM] * 2,
        scratch=[DMA((2,))],
        cost=(150_000_000, 2_000_000),
    )
    scores = pltpu.VMEM((count, half), F32)
    intra_own, q_other = call(
        packed(intra_kernel, fetch=True),
        (scores, tile),
        (queries, q_own, k_own, v_own),
        specs=[HBM] + [VMEM] * 3,
        scratch=[DMA((1,))],
        cost=(300_000_000, 2_000_000),
    )
    intra_other = call(
        packed(intra_kernel, fetch=False), scores, (q_other, k_other, v_other), cost=(300_000_000, 2_000_000)
    )

    send, chip, ext = call(after_core, (small16, small32, small32), (keep, got))
    total, before = chip, []
    for n in range(rounds):
        odd = 2 << (n + 1) if n + 1 < rounds else SIDE
        got = swap(send, SIDE << n, odd)
        if n + 1 == rounds:
            break
        last = n + 2 == rounds
        send, *before = call(
            packed(after_round, n=n, rounds=rounds),
            (small16, *[small32] * (1 if last else 2)),
            [*before[:1], total, got, *([chip] if last else [])],
        )
        if not last:
            total = before.pop()
    send, prior = call(
        functools.partial(after_last, n=rounds - 1, rounds=rounds), (small16, small16), [*before, got, ext]
    )
    got = swap(send, CORE, CORE)

    out = None
    for own, prior, q, intra in ((True, prior, q_own, intra_own), (False, got, q_other, intra_other)):
        args = [prior, q, gain_vmem, intra]
        specs = [VMEM] * 4
        alias = {}
        if out is not None:
            args, specs, alias = [*args, out], [*specs, ANY], {4: 0}
        out = call(
            packed(final_kernel, own=own),
            jax.ShapeDtypeStruct((count, width), BF16),
            args,
            specs=specs,
            out_specs=ANY,
            scratch=[tile, DMA((half // QUAD,))],
            alias=alias,
            cost=(100_000_000, 2_000_000),
        )
    return out


def solution(mesh):
    return jax.shard_map(
        functools.partial(on_device, size=mesh.shape[AXIS]),
        mesh=mesh,
        in_specs=(
            P(("groups", "seq"), None),
            P(("groups", "seq"), None),
            P(("groups", "seq"), None),
            P(),
        ),
        out_specs=P(("groups", "seq"), None),
        check_vma=False,
    )
```

time: 129 us -> 29.1 us (0.23)
  the two profiles are of different devices: /device:TPU:0 before, /device:TPU:29 now
where the time goes in v9:
time: 29.1 us; the launch traced here: 28.9 us
  waiting for transfers between devices  13.6 us (47%)
  Pallas kernels  10.1 us (35%)
  starting transfers between devices  5.15 us (18%)
    ppermute x5, waiting for transfers between devices, swap(): lax.ppermute(x, AXIS, [(i, i ^ (odd if i & CORE else even)) for i in rang...  13.6 us
    pallas_call x10, Pallas kernels, call(): pl.pallas_call(kernel, out_shape=outs, in_specs=specs, out_specs=([VMEM]...  10.1 us
    ppermute x5, starting transfers between devices, swap(): lax.ppermute(x, AXIS, [(i, i ^ (odd if i & CORE else even)) for i in rang...  5.15 us
  transfers between devices with their start and end apart: 5, of which 3 were waited for; matrix products, arithmetic and copies ran while one was open for 0% of the time, Pallas kernels for 24%

profile of v9, /device:TPU:29, one launch (start us, length us, event | category | flops | bytes accessed | tf_op | source)
XLA Modules:
  0.0 28.9 jit_solution(5462347731409345668)
XLA Ops:
  0.0 1.6 %shard_map.46 = (bf16[512,128]{1,0:T(8,128)(2,1)S(1)}, bf16[256,1024]{1,0:T(8,128)(2,1)S(1)}, bf16[256,1024]{1,0:T(8,128)(2,1)S(1)}, bf16[256,1024]{1,0:T(8,128)(2,1)S(1)}, bf16[256,1024]{1,0:T(8,128)(2,1)S(1)}) custom-call(bf16[256,2048]{1,0:T(8,128)(2,1)} %k_hbm.1, bf16[256,2048]{1,0:T(8,128)(2,1)} %v_hbm.1), custom_call_target="tpu_custom_call" | custom-call | flops 10000 | bytes 10000 | tf_op jit(solution)/shard_map/pallas_call | solution.py:210
  1.6 0.7 %collective-permute-start = (bf16[512,128]{1,0:T(8,128)(2,1)S(1)}, bf16[512,128]{1,0:T(8,128)(2,1)S(1)}, u32[]{:S(2)}, u32[]{:S(2)}) collective-permute-start(bf16[512,128]{1,0:T(8,128)(2,1)S(1)} %get-tuple-element.28), channel_id=1, source_target_pairs={{0,1},{1,0},{2,3},{3,2},{4,5},{5,4},{6,7},{7,6},{8,9},{9,8},{10,11... | collective-permute-start | bytes 393224 | tf_op jit(solution)/shard_map/ppermute | solution.py:235
  2.4 1.1 %shard_map.47 = (f32[512,128]{1,0:T(8,128)S(1)}, bf16[256,1024]{1,0:T(8,128)(2,1)S(1)}, f32[1,2048]{1,0:T(1,128)S(1)}) custom-call(bf16[256,1024]{1,0:T(8,128)(2,1)S(1)} %get-tuple-element.25.k_own.refs_2_, bf16[256,1024]{1,0:T(8,128)(2,1)S(1)} %get-tuple-element.26.v_own.refs_3_, bf16[256,2048]{1,0:T(8,128)(2,1)} %refs_0_.1, f32[1,2048]{1,0:T(1,128)} %bitcast.1), custom_call_target="tpu_custom_call" | custom-call | flops 150000000 | bytes 2000000 | tf_op jit(solution)/shard_map/pallas_call | solution.py:210
  3.5 0.0 collective-permute-done.got
  3.5 0.1 shard_map.48
  3.6 0.2 collective-permute-start.1
  3.8 3.9 %collective-permute-done.1.refs_1_ = bf16[512,128]{1,0:T(8,128)(2,1)S(1)} collective-permute-done((bf16[512,128]{1,0:T(8,128)(2,1)S(1)}, bf16[512,128]{1,0:T(8,128)(2,1)S(1)}, u32[]{:S(2)}, u32[]{:S(2)}) %collective-permute-start.1) | collective-permute-done | bytes 131104 | tf_op jit(solution)/shard_map/ppermute | solution.py:235
  7.8 0.1 collective-permute-start.2
  7.9 6.1 %collective-permute-done.2.refs_2_ = bf16[512,128]{1,0:T(8,128)(2,1)S(1)} collective-permute-done((bf16[512,128]{1,0:T(8,128)(2,1)S(1)}, bf16[512,128]{1,0:T(8,128)(2,1)S(1)}, u32[]{:S(2)}, u32[]{:S(2)}) %collective-permute-start.2) | collective-permute-done | bytes 131104 | tf_op jit(solution)/shard_map/ppermute | solution.py:235
  14.0 0.1 shard_map.50
  14.0 0.3 %collective-permute-start.3 = (bf16[512,128]{1,0:T(8,128)(2,1)S(1)}, bf16[512,128]{1,0:T(8,128)(2,1)S(1)}, u32[]{:S(2)}, u32[]{:S(2)}) collective-permute-start(bf16[512,128]{1,0:T(8,128)(2,1)S(1)} %get-tuple-element.35), channel_id=1, source_target_pairs={{0,8},{1,3},{2,10},{3,1},{4,12},{5,7},{6,14},{7,5},{8,0},{9,11},{1... | collective-permute-start | bytes 393224 | tf_op jit(solution)/shard_map/ppermute | solution.py:235
  14.3 3.6 %collective-permute-done.3.got = bf16[512,128]{1,0:T(8,128)(2,1)S(1)} collective-permute-done((bf16[512,128]{1,0:T(8,128)(2,1)S(1)}, bf16[512,128]{1,0:T(8,128)(2,1)S(1)}, u32[]{:S(2)}, u32[]{:S(2)}) %collective-permute-start.3) | collective-permute-done | bytes 131104 | tf_op jit(solution)/shard_map/ppermute | solution.py:235
  17.9 0.1 shard_map.51
  18.0 3.8 %collective-permute-start.4 = (bf16[512,128]{1,0:T(8,128)(2,1)S(1)}, bf16[512,128]{1,0:T(8,128)(2,1)S(1)}, u32[]{:S(2)}, u32[]{:S(2)}) collective-permute-start(bf16[512,128]{1,0:T(8,128)(2,1)S(1)} %get-tuple-element.37), channel_id=1, source_target_pairs={{0,1},{1,0},{2,3},{3,2},{4,5},{5,4},{6,7},{7,6},{8,9},{9,8},{10,11... | collective-permute-start | bytes 393224 | tf_op jit(solution)/shard_map/ppermute | solution.py:235
  21.8 2.5 %shard_map.52 = (f32[256,1024]{1,0:T(8,128)S(1)}, bf16[256,1024]{1,0:T(8,128)(2,1)S(1)}) custom-call(bf16[256,2048]{1,0:T(8,128)(2,1)} %refs_0_.1, bf16[256,1024]{1,0:T(8,128)(2,1)S(1)} %get-tuple-element.38.refs_1_, bf16[256,1024]{1,0:T(8,128)(2,1)S(1)} %get-tuple-element.25.k_own.refs_2_, bf16[256,1024]{1,0:T(8,128)(2,1)S(1)} %get-tuple-element.26.v_own.refs_3_), custom_call_target="tpu_custom_call" | custom-call | flops 300000000 | bytes 2000000 | tf_op jit(solution)/shard_map/pallas_call | solution.py:210
  24.3 1.8 %shard_map.53.refs_3_ = f32[256,1024]{1,0:T(8,128)S(1)} custom-call(bf16[256,1024]{1,0:T(8,128)(2,1)S(1)} %get-tuple-element.39.refs_0_.refs_1_, bf16[256,1024]{1,0:T(8,128)(2,1)S(1)} %get-tuple-element.41.refs_1_, bf16[256,1024]{1,0:T(8,128)(2,1)S(1)} %get-tuple-element.42.refs_2_), custom_call_target="tpu_custom_call" | custom-call | flops 300000000 | bytes 2000000 | tf_op jit(solution)/shard_map/pallas_call | solution.py:210
  26.1 1.4 %shard_map.54.refs_4_ = bf16[256,2048]{1,0:T(8,128)(2,1)} custom-call(bf16[512,128]{1,0:T(8,128)(2,1)S(1)} %get-tuple-element.43.refs_0_, bf16[256,1024]{1,0:T(8,128)(2,1)S(1)} %get-tuple-element.38.refs_1_, f32[1,2048]{1,0:T(1,128)S(1)} %get-tuple-element.40.refs_2_, f32[256,1024]{1,0:T(8,128)S(1)} %get-tuple-element.44.refs_3_), custom_call_target="tpu_custom_call" | custom-call | flops 100000000 | bytes 2000000 | tf_op jit(solution)/shard_map/pallas_call | solution.py:210
  27.5 0.0 collective-permute-done.4.refs_0_
  27.5 1.4 %shard_map.55 = bf16[256,2048]{1,0:T(8,128)(2,1)} custom-call(bf16[512,128]{1,0:T(8,128)(2,1)S(1)} %collective-permute-done.4.refs_0_, bf16[256,1024]{1,0:T(8,128)(2,1)S(1)} %get-tuple-element.39.refs_0_.refs_1_, f32[1,2048]{1,0:T(1,128)S(1)} %get-tuple-element.40.refs_2_, f32[256,1024]{1,0:T(8,128)S(1)} %shard_map.53.refs_3_, ...), custom_call_target="tpu_custom_call", output_to_operand_aliasing={{}: (4, {})} | custom-call | flops 100000000 | bytes 2000000 | tf_op jit(solution)/shard_map/pallas_call | solution.py:210
  (1 shorter events, 0.0 us)
Async XLA Ops:
  1.6 1.8 %collective-permute-start = (bf16[512,128]{1,0:T(8,128)(2,1)S(1)}, bf16[512,128]{1,0:T(8,128)(2,1)S(1)}, u32[]{:S(2)}, u32[]{:S(2)}) collective-permute-start(bf16[512,128]{1,0:T(8,128)(2,1)S(1)} %get-tuple-element.28), channel_id=1, source_target_pairs={{0,1},{1,0},{2,3},{3,2},{4,5},{5,4},{6,7},{7,6},{8,9},{9,8},{10,11... | collective-permute-start | bytes 393224 | tf_op jit(solution)/shard_map/ppermute | solution.py:235
  3.6 4.2 %collective-permute-start.1 = (bf16[512,128]{1,0:T(8,128)(2,1)S(1)}, bf16[512,128]{1,0:T(8,128)(2,1)S(1)}, u32[]{:S(2)}, u32[]{:S(2)}) collective-permute-start(bf16[512,128]{1,0:T(8,128)(2,1)S(1)} %get-tuple-element.30), channel_id=1, source_target_pairs={{0,2},{1,5},{2,0},{3,7},{4,6},{5,1},{6,4},{7,3},{8,10},{9,13},{10,... | collective-permute-start | bytes 393224 | tf_op jit(solution)/shard_map/ppermute | solution.py:235
  7.8 6.2 %collective-permute-start.2 = (bf16[512,128]{1,0:T(8,128)(2,1)S(1)}, bf16[512,128]{1,0:T(8,128)(2,1)S(1)}, u32[]{:S(2)}, u32[]{:S(2)}) collective-permute-start(bf16[512,128]{1,0:T(8,128)(2,1)S(1)} %get-tuple-element.33), channel_id=1, source_target_pairs={{0,4},{1,9},{2,6},{3,11},{4,0},{5,13},{6,2},{7,15},{8,12},{9,1},{1... | collective-permute-start | bytes 393224 | tf_op jit(solution)/shard_map/ppermute | solution.py:235
  14.0 3.9 %collective-permute-start.3 = (bf16[512,128]{1,0:T(8,128)(2,1)S(1)}, bf16[512,128]{1,0:T(8,128)(2,1)S(1)}, u32[]{:S(2)}, u32[]{:S(2)}) collective-permute-start(bf16[512,128]{1,0:T(8,128)(2,1)S(1)} %get-tuple-element.35), channel_id=1, source_target_pairs={{0,8},{1,3},{2,10},{3,1},{4,12},{5,7},{6,14},{7,5},{8,0},{9,11},{1... | collective-permute-start | bytes 393224 | tf_op jit(solution)/shard_map/ppermute | solution.py:235
  18.0 9.5 %collective-permute-start.4 = (bf16[512,128]{1,0:T(8,128)(2,1)S(1)}, bf16[512,128]{1,0:T(8,128)(2,1)S(1)}, u32[]{:S(2)}, u32[]{:S(2)}) collective-permute-start(bf16[512,128]{1,0:T(8,128)(2,1)S(1)} %get-tuple-element.37), channel_id=1, source_target_pairs={{0,1},{1,0},{2,3},{3,2},{4,5},{5,4},{6,7},{7,6},{8,9},{9,8},{10,11... | collective-permute-start | bytes 393224 | tf_op jit(solution)/shard_map/ppermute | solution.py:235

commit v10 on v9

--- a/solution.py
+++ b/solution.py
@@ -123,11 +123,13 @@
     before_out[...] = value
 
 
-def after_last(before, got, ext, send, prior, *, n, rounds):
+def after_last(before, got, ext, send0, send1, prior, *, n, rounds):
     base = with_got(before, got, n, rounds)
     ahead = base + ext[...]
     first = bit_of(0) == 0
-    send[...] = jnp.where(first, ahead, base).astype(BF16)
+    send = jnp.where(first, ahead, base).astype(BF16)
+    send0[...] = send[: send0.shape[0]]
+    send1[...] = send[send0.shape[0] :]
     prior[...] = jnp.where(first, base, ahead).astype(BF16)
 
 
@@ -166,34 +168,45 @@
     wait_all(loads)
 
 
-def final_kernel(refs, *, own):
+def final_kernel(refs, *, own, at, last):
+    refs = list(refs)
     prior_ref, q_ref, gain_ref, intra_ref = refs[:4]
-    out_hbm, out_buf, sems = refs[-3:]
-    half = out_buf.shape[1]
-    base = half_start(own, half)
+    half = q_ref.shape[1]
+    base = half_start(own, half) + at
+    copies = []
+    if last:
+        own_ref, part_ref, out_hbm, out, sems = refs[4:]
+        own_lanes = pl.ds(half_start(True, half), half)
+        copies.append(pltpu.make_async_copy(own_ref, out_hbm.at[:, own_lanes], sems.at[0]))
+        part_lanes = pl.ds(half_start(False, half), part_ref.shape[1])
+        copies.append(pltpu.make_async_copy(part_ref, out_hbm.at[:, part_lanes], sems.at[1]))
+        for copy in copies:
+            copy.start()
+    else:
+        out = refs[4]
+    width = out.shape[1]
     lane = lax.broadcasted_iota(jnp.int32, (QUAD, QUAD), 1) >> SHIFT
     row = lax.broadcasted_iota(jnp.int32, (QUAD, QUAD), 0) >> SHIFT
     same = lane == row
     ones = jnp.where(same, 1.0 / HEAD_DIM, 0.0).astype(BF16)
-    copies = []
-    GROUP = 2
-    for start in range(0, half // QUAD, GROUP):
+    for start in range(0, width // QUAD, 2):
         numers = []
-        for n in range(start, start + GROUP):
+        for n in range(start, start + 2):
             one = prior_ref[pl.ds(n * PAIR, HEAD_DIM), :]
             two = prior_ref[pl.ds(n * PAIR + HEAD_DIM, HEAD_DIM), :]
             block = jnp.concatenate([jnp.concatenate([one, two], axis=1)] * 4, axis=0)
             block = jnp.where(same, block, jnp.zeros_like(block))
-            lanes = pl.ds(n * QUAD, QUAD)
+            lanes = pl.ds(at + n * QUAD, QUAD)
             fq = jnp.maximum(q_ref[:, lanes], 0)
             numers.append(dot(fq, block, ((1,), (0,))) + intra_ref[:, lanes])
         for n, numer in enumerate(numers, start):
             lanes = pl.ds(n * QUAD, QUAD)
             there = pl.ds(pl.multiple_of(base + n * QUAD, QUAD), QUAD)
             mean_sq = dot((numer * numer).astype(BF16), ones, ((1,), (0,)))
-            out_buf[:, lanes] = (numer * lax.rsqrt(mean_sq + EPS) * gain_ref[:, there]).astype(BF16)
-            copies.append(pltpu.make_async_copy(out_buf.at[:, lanes], out_hbm.at[:, there], sems.at[n]))
-            copies[-1].start()
+            out[:, lanes] = (numer * lax.rsqrt(mean_sq + EPS) * gain_ref[:, there]).astype(BF16)
+            if last:
+                copies.append(pltpu.make_async_copy(out.at[:, lanes], out_hbm.at[:, there], sems.at[2 + n]))
+                copies[-1].start()
     wait_all(copies)
 
 
@@ -274,29 +287,30 @@
         )
         if not last:
             total = before.pop()
-    send, prior = call(
-        functools.partial(after_last, n=rounds - 1, rounds=rounds), (small16, small16), [*before, got, ext]
-    )
-    got = swap(send, CORE, CORE)
-
-    out = None
-    for own, prior, q, intra in ((True, prior, q_own, intra_own), (False, got, q_other, intra_other)):
-        args = [prior, q, gain_vmem, intra]
-        specs = [VMEM] * 4
-        alias = {}
-        if out is not None:
-            args, specs, alias = [*args, out], [*specs, ANY], {4: 0}
-        out = call(
-            packed(final_kernel, own=own),
-            jax.ShapeDtypeStruct((count, width), BF16),
-            args,
-            specs=specs,
-            out_specs=ANY,
-            scratch=[tile, DMA((half // QUAD,))],
-            alias=alias,
-            cost=(100_000_000, 2_000_000),
-        )
-    return out
+    quarter = pltpu.VMEM((rows // 2, PAIR), BF16)
+    send0, send1, prior = call(
+        functools.partial(after_last, n=rounds - 1, rounds=rounds), (quarter, quarter, small16), [*before, got, ext]
+    )
+    got0 = swap(send0, CORE, CORE)
+    got1 = swap(send1, CORE, CORE)
+
+    part = half // 2
+    left = pltpu.VMEM((count, part), BF16)
+    cost = (100_000_000, 2_000_000)
+    done_own = call(
+        packed(final_kernel, own=True, at=0, last=False), tile, (prior, q_own, gain_vmem, intra_own), cost=cost
+    )
+    done_part = call(
+        packed(final_kernel, own=False, at=0, last=False), left, (got0, q_other, gain_vmem, intra_other), cost=cost
+    )
+    return call(
+        packed(final_kernel, own=False, at=part, last=True),
+        jax.ShapeDtypeStruct((count, width), BF16),
+        (got1, q_other, gain_vmem, intra_other, done_own, done_part),
+        out_specs=ANY,
+        scratch=[left, DMA((2 + part // QUAD,))],
+        cost=cost,
+    )
 
 
 def solution(mesh):

time: 29.1 us -> 28.7 us (0.986)
  the two profiles are of different devices: /device:TPU:29 before, /device:TPU:0 now
where the time goes in v10:
time: 28.7 us; the launch traced here: 28.5 us
  waiting for transfers between devices  10.2 us (36%)
  Pallas kernels  9.59 us (33%)
  starting transfers between devices  8.66 us (30%)
    ppermute x6, waiting for transfers between devices, swap(): lax.ppermute(x, AXIS, [(i, i ^ (odd if i & CORE else even)) for i in rang...  10.2 us
    pallas_call x11, Pallas kernels, call(): pl.pallas_call(kernel, out_shape=outs, in_specs=specs, out_specs=([VMEM]...  9.59 us
    ppermute x6, starting transfers between devices, swap(): lax.ppermute(x, AXIS, [(i, i ^ (odd if i & CORE else even)) for i in rang...  8.66 us
  transfers between devices with their start and end apart: 6, of which 3 were waited for; matrix products, arithmetic and copies ran while one was open for 0% of the time, Pallas kernels for 23%

profile of v10, /device:TPU:0, one launch (start us, length us, event | category | flops | bytes accessed | tf_op | source)
XLA Modules:
  0.0 28.5 jit_solution(17847424231480624454)
XLA Ops:
  0.0 1.6 %shard_map.46 = (bf16[512,128]{1,0:T(8,128)(2,1)S(1)}, bf16[256,1024]{1,0:T(8,128)(2,1)S(1)}, bf16[256,1024]{1,0:T(8,128)(2,1)S(1)}, bf16[256,1024]{1,0:T(8,128)(2,1)S(1)}, bf16[256,1024]{1,0:T(8,128)(2,1)S(1)}) custom-call(bf16[256,2048]{1,0:T(8,128)(2,1)} %k_hbm.1, bf16[256,2048]{1,0:T(8,128)(2,1)} %v_hbm.1), custom_call_target="tpu_custom_call" | custom-call | flops 10000 | bytes 10000 | tf_op jit(solution)/shard_map/pallas_call | solution.py:223
  1.6 0.6 %collective-permute-start = (bf16[512,128]{1,0:T(8,128)(2,1)S(1)}, bf16[512,128]{1,0:T(8,128)(2,1)S(1)}, u32[]{:S(2)}, u32[]{:S(2)}) collective-permute-start(bf16[512,128]{1,0:T(8,128)(2,1)S(1)} %get-tuple-element.29), channel_id=1, source_target_pairs={{0,1},{1,0},{2,3},{3,2},{4,5},{5,4},{6,7},{7,6},{8,9},{9,8},{10,11... | collective-permute-start | bytes 393224 | tf_op jit(solution)/shard_map/ppermute | solution.py:248
  2.2 1.1 %shard_map.47 = (f32[512,128]{1,0:T(8,128)S(1)}, bf16[256,1024]{1,0:T(8,128)(2,1)S(1)}, f32[1,2048]{1,0:T(1,128)S(1)}) custom-call(bf16[256,1024]{1,0:T(8,128)(2,1)S(1)} %get-tuple-element.26.k_own.refs_2_, bf16[256,1024]{1,0:T(8,128)(2,1)S(1)} %get-tuple-element.27.v_own.refs_3_, bf16[256,2048]{1,0:T(8,128)(2,1)} %refs_0_.1, f32[1,2048]{1,0:T(1,128)} %bitcast.1), custom_call_target="tpu_custom_call" | custom-call | flops 150000000 | bytes 2000000 | tf_op jit(solution)/shard_map/pallas_call | solution.py:223
  3.3 0.0 collective-permute-done.got
  3.3 0.1 shard_map.48
  3.4 2.8 %collective-permute-start.1 = (bf16[512,128]{1,0:T(8,128)(2,1)S(1)}, bf16[512,128]{1,0:T(8,128)(2,1)S(1)}, u32[]{:S(2)}, u32[]{:S(2)}) collective-permute-start(bf16[512,128]{1,0:T(8,128)(2,1)S(1)} %get-tuple-element.31), channel_id=1, source_target_pairs={{0,2},{1,5},{2,0},{3,7},{4,6},{5,1},{6,4},{7,3},{8,10},{9,13},{10,... | collective-permute-start | bytes 393224 | tf_op jit(solution)/shard_map/ppermute | solution.py:248
  6.2 2.9 %collective-permute-done.1.refs_1_ = bf16[512,128]{1,0:T(8,128)(2,1)S(1)} collective-permute-done((bf16[512,128]{1,0:T(8,128)(2,1)S(1)}, bf16[512,128]{1,0:T(8,128)(2,1)S(1)}, u32[]{:S(2)}, u32[]{:S(2)}) %collective-permute-start.1) | collective-permute-done | bytes 131104 | tf_op jit(solution)/shard_map/ppermute | solution.py:248
  9.2 2.1 %collective-permute-start.2 = (bf16[512,128]{1,0:T(8,128)(2,1)S(1)}, bf16[512,128]{1,0:T(8,128)(2,1)S(1)}, u32[]{:S(2)}, u32[]{:S(2)}) collective-permute-start(bf16[512,128]{1,0:T(8,128)(2,1)S(1)} %get-tuple-element.34), channel_id=1, source_target_pairs={{0,4},{1,9},{2,6},{3,11},{4,0},{5,13},{6,2},{7,15},{8,12},{9,1},{1... | collective-permute-start | bytes 393224 | tf_op jit(solution)/shard_map/ppermute | solution.py:248
  11.3 3.9 %collective-permute-done.2.refs_2_ = bf16[512,128]{1,0:T(8,128)(2,1)S(1)} collective-permute-done((bf16[512,128]{1,0:T(8,128)(2,1)S(1)}, bf16[512,128]{1,0:T(8,128)(2,1)S(1)}, u32[]{:S(2)}, u32[]{:S(2)}) %collective-permute-start.2) | collective-permute-done | bytes 131104 | tf_op jit(solution)/shard_map/ppermute | solution.py:248
  15.2 0.1 shard_map.50
  15.3 2.6 %collective-permute-start.3 = (bf16[512,128]{1,0:T(8,128)(2,1)S(1)}, bf16[512,128]{1,0:T(8,128)(2,1)S(1)}, u32[]{:S(2)}, u32[]{:S(2)}) collective-permute-start(bf16[512,128]{1,0:T(8,128)(2,1)S(1)} %get-tuple-element.36), channel_id=1, source_target_pairs={{0,8},{1,3},{2,10},{3,1},{4,12},{5,7},{6,14},{7,5},{8,0},{9,11},{1... | collective-permute-start | bytes 393224 | tf_op jit(solution)/shard_map/ppermute | solution.py:248
  17.9 3.3 %collective-permute-done.3.got = bf16[512,128]{1,0:T(8,128)(2,1)S(1)} collective-permute-done((bf16[512,128]{1,0:T(8,128)(2,1)S(1)}, bf16[512,128]{1,0:T(8,128)(2,1)S(1)}, u32[]{:S(2)}, u32[]{:S(2)}) %collective-permute-start.3) | collective-permute-done | bytes 131104 | tf_op jit(solution)/shard_map/ppermute | solution.py:248
  21.2 0.1 shard_map.51
  21.3 0.1 collective-permute-start.4
  21.3 0.5 %collective-permute-start.5 = (bf16[256,128]{1,0:T(8,128)(2,1)S(1)}, bf16[256,128]{1,0:T(8,128)(2,1)S(1)}, u32[]{:S(2)}, u32[]{:S(2)}) collective-permute-start(bf16[256,128]{1,0:T(8,128)(2,1)S(1)} %get-tuple-element.46), channel_id=1, source_target_pairs={{0,1},{1,0},{2,3},{3,2},{4,5},{5,4},{6,7},{7,6},{8,9},{9,8},{10,11... | collective-permute-start | bytes 196616 | tf_op jit(solution)/shard_map/ppermute | solution.py:248
  21.8 2.5 %shard_map.52 = (f32[256,1024]{1,0:T(8,128)S(1)}, bf16[256,1024]{1,0:T(8,128)(2,1)S(1)}) custom-call(bf16[256,2048]{1,0:T(8,128)(2,1)} %refs_0_.1, bf16[256,1024]{1,0:T(8,128)(2,1)S(1)} %get-tuple-element.39.refs_1_, bf16[256,1024]{1,0:T(8,128)(2,1)S(1)} %get-tuple-element.26.k_own.refs_2_, bf16[256,1024]{1,0:T(8,128)(2,1)S(1)} %get-tuple-element.27.v_own.refs_3_), custom_call_target="tpu_custom_call" | custom-call | flops 300000000 | bytes 2000000 | tf_op jit(solution)/shard_map/pallas_call | solution.py:223
  24.4 1.8 %shard_map.53.refs_3_ = f32[256,1024]{1,0:T(8,128)S(1)} custom-call(bf16[256,1024]{1,0:T(8,128)(2,1)S(1)} %get-tuple-element.40.refs_0_.refs_1_, bf16[256,1024]{1,0:T(8,128)(2,1)S(1)} %get-tuple-element.42.refs_1_, bf16[256,1024]{1,0:T(8,128)(2,1)S(1)} %get-tuple-element.43.refs_2_), custom_call_target="tpu_custom_call" | custom-call | flops 300000000 | bytes 2000000 | tf_op jit(solution)/shard_map/pallas_call | solution.py:223
  26.2 0.6 %shard_map.54.refs_4_ = bf16[256,1024]{1,0:T(8,128)(2,1)S(1)} custom-call(bf16[512,128]{1,0:T(8,128)(2,1)S(1)} %get-tuple-element.44.refs_0_, bf16[256,1024]{1,0:T(8,128)(2,1)S(1)} %get-tuple-element.39.refs_1_, f32[1,2048]{1,0:T(1,128)S(1)} %get-tuple-element.41.refs_2_, f32[256,1024]{1,0:T(8,128)S(1)} %get-tuple-element.45.refs_3_), custom_call_target="tpu_custom_call" | custom-call | flops 100000000 | bytes 2000000 | tf_op jit(solution)/shard_map/pallas_call | solution.py:223
  26.8 0.0 collective-permute-done.5.refs_0_
  26.9 0.4 %shard_map.55.refs_5_ = bf16[256,512]{1,0:T(8,128)(2,1)S(1)} custom-call(bf16[256,128]{1,0:T(8,128)(2,1)S(1)} %collective-permute-done.5.refs_0_, bf16[256,1024]{1,0:T(8,128)(2,1)S(1)} %get-tuple-element.40.refs_0_.refs_1_, f32[1,2048]{1,0:T(1,128)S(1)} %get-tuple-element.41.refs_2_, f32[256,1024]{1,0:T(8,128)S(1)} %shard_map.53.refs_3_), custom_call_target="tpu_custom_call" | custom-call | flops 100000000 | bytes 2000000 | tf_op jit(solution)/shard_map/pallas_call | solution.py:223
  27.3 0.0 collective-permute-done.4.refs_0_
  27.3 1.2 %shard_map.56 = bf16[256,2048]{1,0:T(8,128)(2,1)} custom-call(bf16[256,128]{1,0:T(8,128)(2,1)S(1)} %collective-permute-done.4.refs_0_, bf16[256,1024]{1,0:T(8,128)(2,1)S(1)} %get-tuple-element.40.refs_0_.refs_1_, f32[1,2048]{1,0:T(1,128)S(1)} %get-tuple-element.41.refs_2_, f32[256,1024]{1,0:T(8,128)S(1)} %shard_map.53.refs_3_, ...), custom_call_target="tpu_custom_call" | custom-call | flops 100000000 | bytes 2000000 | tf_op jit(solution)/shard_map/pallas_call | solution.py:223
  (1 shorter events, 0.0 us)
Async XLA Ops:
  1.6 1.7 %collective-permute-start = (bf16[512,128]{1,0:T(8,128)(2,1)S(1)}, bf16[512,128]{1,0:T(8,128)(2,1)S(1)}, u32[]{:S(2)}, u32[]{:S(2)}) collective-permute-start(bf16[512,128]{1,0:T(8,128)(2,1)S(1)} %get-tuple-element.29), channel_id=1, source_target_pairs={{0,1},{1,0},{2,3},{3,2},{4,5},{5,4},{6,7},{7,6},{8,9},{9,8},{10,11... | collective-permute-start | bytes 393224 | tf_op jit(solution)/shard_map/ppermute | solution.py:248
  3.4 5.7 %collective-permute-start.1 = (bf16[512,128]{1,0:T(8,128)(2,1)S(1)}, bf16[512,128]{1,0:T(8,128)(2,1)S(1)}, u32[]{:S(2)}, u32[]{:S(2)}) collective-permute-start(bf16[512,128]{1,0:T(8,128)(2,1)S(1)} %get-tuple-element.31), channel_id=1, source_target_pairs={{0,2},{1,5},{2,0},{3,7},{4,6},{5,1},{6,4},{7,3},{8,10},{9,13},{10,... | collective-permute-start | bytes 393224 | tf_op jit(solution)/shard_map/ppermute | solution.py:248
  9.2 6.0 %collective-permute-start.2 = (bf16[512,128]{1,0:T(8,128)(2,1)S(1)}, bf16[512,128]{1,0:T(8,128)(2,1)S(1)}, u32[]{:S(2)}, u32[]{:S(2)}) collective-permute-start(bf16[512,128]{1,0:T(8,128)(2,1)S(1)} %get-tuple-element.34), channel_id=1, source_target_pairs={{0,4},{1,9},{2,6},{3,11},{4,0},{5,13},{6,2},{7,15},{8,12},{9,1},{1... | collective-permute-start | bytes 393224 | tf_op jit(solution)/shard_map/ppermute | solution.py:248
  15.3 5.9 %collective-permute-start.3 = (bf16[512,128]{1,0:T(8,128)(2,1)S(1)}, bf16[512,128]{1,0:T(8,128)(2,1)S(1)}, u32[]{:S(2)}, u32[]{:S(2)}) collective-permute-start(bf16[512,128]{1,0:T(8,128)(2,1)S(1)} %get-tuple-element.36), channel_id=1, source_target_pairs={{0,8},{1,3},{2,10},{3,1},{4,12},{5,7},{6,14},{7,5},{8,0},{9,11},{1... | collective-permute-start | bytes 393224 | tf_op jit(solution)/shard_map/ppermute | solution.py:248
  21.3 6.0 %collective-permute-start.4 = (bf16[256,128]{1,0:T(8,128)(2,1)S(1)}, bf16[256,128]{1,0:T(8,128)(2,1)S(1)}, u32[]{:S(2)}, u32[]{:S(2)}) collective-permute-start(bf16[256,128]{1,0:T(8,128)(2,1)S(1)} %get-tuple-element.38), channel_id=1, source_target_pairs={{0,1},{1,0},{2,3},{3,2},{4,5},{5,4},{6,7},{7,6},{8,9},{9,8},{10,11... | collective-permute-start | bytes 196616 | tf_op jit(solution)/shard_map/ppermute | solution.py:248
  21.3 5.5 %collective-permute-start.5 = (bf16[256,128]{1,0:T(8,128)(2,1)S(1)}, bf16[256,128]{1,0:T(8,128)(2,1)S(1)}, u32[]{:S(2)}, u32[]{:S(2)}) collective-permute-start(bf16[256,128]{1,0:T(8,128)(2,1)S(1)} %get-tuple-element.46), channel_id=1, source_target_pairs={{0,1},{1,0},{2,3},{3,2},{4,5},{5,4},{6,7},{7,6},{8,9},{9,8},{10,11... | collective-permute-start | bytes 196616 | tf_op jit(solution)/shard_map/ppermute | solution.py:248

commit v11 on v9

--- a/solution.py
+++ b/solution.py
@@ -13,6 +13,7 @@
 QUAD = 4 * HEAD_DIM
 SHIFT = 6
 CORE, SIDE = 1, 2
+BLOCKS = 2
 EPS = 1e-05
 AXIS = "seq"
 BF16, F32 = jnp.bfloat16, jnp.float32
@@ -77,9 +78,10 @@
     wait_all(late)
 
 
-def second_kernel(k_own, v_own, q_hbm, gain_hbm, keep, q_own, gain, sems):
-    loads = [load_half(q_hbm, q_own, True, sems.at[0]), pltpu.make_async_copy(gain_hbm, gain, sems.at[1])]
-    loads[1].start()
+def second_kernel(k_own, v_own, q_hbm, gain_hbm, keep, q_own, q_other, gain, sems):
+    loads = [load_half(q_hbm, q_own, True, sems.at[0]), load_half(q_hbm, q_other, False, sems.at[1])]
+    loads.append(pltpu.make_async_copy(gain_hbm, gain, sems.at[2]))
+    loads[-1].start()
     states_of(k_own, v_own, keep, range(k_own.shape[1] // QUAD))
     wait_all(loads)
 
@@ -131,10 +133,7 @@
     prior[...] = jnp.where(first, base, ahead).astype(BF16)
 
 
-def intra_kernel(refs, *, fetch):
-    q_hbm = refs[0] if fetch else None
-    q_ref, k_ref, v_ref, intra_ref, *refs = refs[1:] if fetch else refs
-    loads = [load_half(q_hbm, refs[0], False, refs[1].at[0])] if fetch else []
+def intra_kernel(q_ref, k_ref, v_ref, intra_ref):
     count, half = intra_ref.shape
     mid = count // 2
     first = first_lanes((count, PAIR))
@@ -163,7 +162,6 @@
         intra_ref[:mid, lanes] = dot(jnp.concatenate(top, axis=1), w_top, ((1,), (0,)))
         w_low = jnp.concatenate(weights, axis=0)
         intra_ref[mid:, lanes] = dot(jnp.concatenate(low, axis=1), w_low, ((1,), (0,)))
-    wait_all(loads)
 
 
 def final_kernel(refs, *, own):
@@ -176,23 +174,32 @@
     same = lane == row
     ones = jnp.where(same, 1.0 / HEAD_DIM, 0.0).astype(BF16)
     copies = []
-    GROUP = 2
-    for start in range(0, half // QUAD, GROUP):
-        numers = []
-        for n in range(start, start + GROUP):
-            one = prior_ref[pl.ds(n * PAIR, HEAD_DIM), :]
-            two = prior_ref[pl.ds(n * PAIR + HEAD_DIM, HEAD_DIM), :]
-            block = jnp.concatenate([jnp.concatenate([one, two], axis=1)] * 4, axis=0)
-            block = jnp.where(same, block, jnp.zeros_like(block))
-            lanes = pl.ds(n * QUAD, QUAD)
-            fq = jnp.maximum(q_ref[:, lanes], 0)
-            numers.append(dot(fq, block, ((1,), (0,))) + intra_ref[:, lanes])
-        for n, numer in enumerate(numers, start):
-            lanes = pl.ds(n * QUAD, QUAD)
-            there = pl.ds(pl.multiple_of(base + n * QUAD, QUAD), QUAD)
-            mean_sq = dot((numer * numer).astype(BF16), ones, ((1,), (0,)))
-            out_buf[:, lanes] = (numer * lax.rsqrt(mean_sq + EPS) * gain_ref[:, there]).astype(BF16)
-            copies.append(pltpu.make_async_copy(out_buf.at[:, lanes], out_hbm.at[:, there], sems.at[n]))
+
+    def numer_of(n):
+        one = prior_ref[pl.ds(n * PAIR, HEAD_DIM), :]
+        two = prior_ref[pl.ds(n * PAIR + HEAD_DIM, HEAD_DIM), :]
+        block = jnp.concatenate([jnp.concatenate([one, two], axis=1)] * 4, axis=0)
+        block = jnp.where(same, block, jnp.zeros_like(block))
+        lanes = pl.ds(n * QUAD, QUAD)
+        fq = jnp.maximum(q_ref[:, lanes], 0)
+        return dot(fq, block, ((1,), (0,))) + intra_ref[:, lanes]
+
+    quads = half // QUAD
+    numers = [numer_of(n) for n in range(quads)]
+    means = [dot((numer * numer).astype(BF16), ones, ((1,), (0,))) for numer in numers]
+    count = q_ref.shape[0]
+    rows = count // BLOCKS
+    for n in range(quads):
+        lanes = pl.ds(n * QUAD, QUAD)
+        there = pl.ds(pl.multiple_of(base + n * QUAD, QUAD), QUAD)
+        gain = gain_ref[:, there]
+        for m in range(BLOCKS):
+            tokens = pl.ds(m * rows, rows)
+            numer, mean_sq = (x[n][m * rows : (m + 1) * rows] for x in (numers, means))
+            out_buf[tokens, lanes] = (numer * lax.rsqrt(mean_sq + EPS) * gain).astype(BF16)
+            copies.append(
+                pltpu.make_async_copy(out_buf.at[tokens, lanes], out_hbm.at[tokens, there], sems.at[n, m])
+            )
             copies[-1].start()
     wait_all(copies)
 
@@ -238,26 +245,18 @@
         first_kernel, (small16, *[tile] * 4), (keys, values), specs=[HBM] * 2, scratch=[DMA((3, 2))]
     )
     got = swap(send, CORE, CORE)
-    keep, q_own, gain_vmem = call(
+    keep, q_own, q_other, gain_vmem = call(
         second_kernel,
-        (small32, tile, pltpu.VMEM((1, width), F32)),
+        (small32, tile, tile, pltpu.VMEM((1, width), F32)),
         (k_own, v_own, queries, gain[None, :]),
         specs=[VMEM] * 2 + [HBM] * 2,
-        scratch=[DMA((2,))],
+        scratch=[DMA((3,))],
         cost=(150_000_000, 2_000_000),
     )
     scores = pltpu.VMEM((count, half), F32)
-    intra_own, q_other = call(
-        packed(intra_kernel, fetch=True),
-        (scores, tile),
-        (queries, q_own, k_own, v_own),
-        specs=[HBM] + [VMEM] * 3,
-        scratch=[DMA((1,))],
-        cost=(300_000_000, 2_000_000),
-    )
-    intra_other = call(
-        packed(intra_kernel, fetch=False), scores, (q_other, k_other, v_other), cost=(300_000_000, 2_000_000)
-    )
+    cost = (300_000_000, 2_000_000)
+    intra_own = call(intra_kernel, scores, (q_own, k_own, v_own), cost=cost)
+    intra_other = call(intra_kernel, scores, (q_other, k_other, v_other), cost=cost)
 
     send, chip, ext = call(after_core, (small16, small32, small32), (keep, got))
     total, before = chip, []
@@ -292,7 +291,7 @@
             args,
             specs=specs,
             out_specs=ANY,
-            scratch=[tile, DMA((half // QUAD,))],
+            scratch=[tile, DMA((half // QUAD, BLOCKS))],
             alias=alias,
             cost=(100_000_000, 2_000_000),
         )

time: 29.1 us -> 28.1 us (0.966)
  the two profiles are of different devices: /device:TPU:29 before, /device:TPU:0 now
where the time goes in v11:
time: 28.1 us; the launch traced here: 27.8 us
  waiting for transfers between devices  10.6 us (38%)
  Pallas kernels  9.35 us (33%)
  starting transfers between devices  7.75 us (28%)
    ppermute x5, waiting for transfers between devices, swap(): lax.ppermute(x, AXIS, [(i, i ^ (odd if i & CORE else even)) for i in rang...  10.6 us
    pallas_call x10, Pallas kernels, call(): pl.pallas_call(kernel, out_shape=outs, in_specs=specs, out_specs=([VMEM]...  9.35 us
    ppermute x5, starting transfers between devices, swap(): lax.ppermute(x, AXIS, [(i, i ^ (odd if i & CORE else even)) for i in rang...  7.75 us
  transfers between devices with their start and end apart: 5, of which 3 were waited for; matrix products, arithmetic and copies ran while one was open for 0% of the time, Pallas kernels for 22%

profile of v11, /device:TPU:0, one launch (start us, length us, event | category | flops | bytes accessed | tf_op | source)
XLA Modules:
  0.0 27.8 jit_solution(17588485109584249556)
XLA Ops:
  0.0 1.6 %shard_map.46 = (bf16[512,128]{1,0:T(8,128)(2,1)S(1)}, bf16[256,1024]{1,0:T(8,128)(2,1)S(1)}, bf16[256,1024]{1,0:T(8,128)(2,1)S(1)}, bf16[256,1024]{1,0:T(8,128)(2,1)S(1)}, bf16[256,1024]{1,0:T(8,128)(2,1)S(1)}) custom-call(bf16[256,2048]{1,0:T(8,128)(2,1)} %k_hbm.1, bf16[256,2048]{1,0:T(8,128)(2,1)} %v_hbm.1), custom_call_target="tpu_custom_call" | custom-call | flops 10000 | bytes 10000 | tf_op jit(solution)/shard_map/pallas_call | solution.py:217
  1.6 0.6 %collective-permute-start = (bf16[512,128]{1,0:T(8,128)(2,1)S(1)}, bf16[512,128]{1,0:T(8,128)(2,1)S(1)}, u32[]{:S(2)}, u32[]{:S(2)}) collective-permute-start(bf16[512,128]{1,0:T(8,128)(2,1)S(1)} %get-tuple-element.27), channel_id=1, source_target_pairs={{0,1},{1,0},{2,3},{3,2},{4,5},{5,4},{6,7},{7,6},{8,9},{9,8},{10,11... | collective-permute-start | bytes 393224 | tf_op jit(solution)/shard_map/ppermute | solution.py:242
  2.2 1.4 %shard_map.47 = (f32[512,128]{1,0:T(8,128)S(1)}, bf16[256,1024]{1,0:T(8,128)(2,1)S(1)}, bf16[256,1024]{1,0:T(8,128)(2,1)S(1)}, f32[1,2048]{1,0:T(1,128)S(1)}) custom-call(bf16[256,1024]{1,0:T(8,128)(2,1)S(1)} %get-tuple-element.24.k_own.k_ref, bf16[256,1024]{1,0:T(8,128)(2,1)S(1)} %get-tuple-element.25.v_own.v_ref, bf16[256,2048]{1,0:T(8,128)(2,1)} %q_hbm.1, ...), custom_call_target="tpu_custom_call" | custom-call | flops 150000000 | bytes 2000000 | tf_op jit(solution)/shard_map/pallas_call | solution.py:217
  3.6 0.0 collective-permute-done.got
  3.6 0.1 shard_map.48
  3.6 2.6 %collective-permute-start.1 = (bf16[512,128]{1,0:T(8,128)(2,1)S(1)}, bf16[512,128]{1,0:T(8,128)(2,1)S(1)}, u32[]{:S(2)}, u32[]{:S(2)}) collective-permute-start(bf16[512,128]{1,0:T(8,128)(2,1)S(1)} %get-tuple-element.29), channel_id=1, source_target_pairs={{0,2},{1,5},{2,0},{3,7},{4,6},{5,1},{6,4},{7,3},{8,10},{9,13},{10,... | collective-permute-start | bytes 393224 | tf_op jit(solution)/shard_map/ppermute | solution.py:242
  6.2 2.9 %collective-permute-done.1.refs_1_ = bf16[512,128]{1,0:T(8,128)(2,1)S(1)} collective-permute-done((bf16[512,128]{1,0:T(8,128)(2,1)S(1)}, bf16[512,128]{1,0:T(8,128)(2,1)S(1)}, u32[]{:S(2)}, u32[]{:S(2)}) %collective-permute-start.1) | collective-permute-done | bytes 131104 | tf_op jit(solution)/shard_map/ppermute | solution.py:242
  9.2 2.1 %collective-permute-start.2 = (bf16[512,128]{1,0:T(8,128)(2,1)S(1)}, bf16[512,128]{1,0:T(8,128)(2,1)S(1)}, u32[]{:S(2)}, u32[]{:S(2)}) collective-permute-start(bf16[512,128]{1,0:T(8,128)(2,1)S(1)} %get-tuple-element.32), channel_id=1, source_target_pairs={{0,4},{1,9},{2,6},{3,11},{4,0},{5,13},{6,2},{7,15},{8,12},{9,1},{1... | collective-permute-start | bytes 393224 | tf_op jit(solution)/shard_map/ppermute | solution.py:242
  11.4 4.1 %collective-permute-done.2.refs_2_ = bf16[512,128]{1,0:T(8,128)(2,1)S(1)} collective-permute-done((bf16[512,128]{1,0:T(8,128)(2,1)S(1)}, bf16[512,128]{1,0:T(8,128)(2,1)S(1)}, u32[]{:S(2)}, u32[]{:S(2)}) %collective-permute-start.2) | collective-permute-done | bytes 131104 | tf_op jit(solution)/shard_map/ppermute | solution.py:242
  15.4 0.1 shard_map.50
  15.5 2.4 %collective-permute-start.3 = (bf16[512,128]{1,0:T(8,128)(2,1)S(1)}, bf16[512,128]{1,0:T(8,128)(2,1)S(1)}, u32[]{:S(2)}, u32[]{:S(2)}) collective-permute-start(bf16[512,128]{1,0:T(8,128)(2,1)S(1)} %get-tuple-element.34), channel_id=1, source_target_pairs={{0,8},{1,3},{2,10},{3,1},{4,12},{5,7},{6,14},{7,5},{8,0},{9,11},{1... | collective-permute-start | bytes 393224 | tf_op jit(solution)/shard_map/ppermute | solution.py:242
  17.9 3.5 %collective-permute-done.3.got = bf16[512,128]{1,0:T(8,128)(2,1)S(1)} collective-permute-done((bf16[512,128]{1,0:T(8,128)(2,1)S(1)}, bf16[512,128]{1,0:T(8,128)(2,1)S(1)}, u32[]{:S(2)}, u32[]{:S(2)}) %collective-permute-start.3) | collective-permute-done | bytes 131104 | tf_op jit(solution)/shard_map/ppermute | solution.py:242
  21.4 0.1 shard_map.51
  21.5 0.1 collective-permute-start.4
  21.6 1.8 %shard_map.53.refs_3_ = f32[256,1024]{1,0:T(8,128)S(1)} custom-call(bf16[256,1024]{1,0:T(8,128)(2,1)S(1)} %get-tuple-element.42.q_ref.refs_1_, bf16[256,1024]{1,0:T(8,128)(2,1)S(1)} %get-tuple-element.24.k_own.k_ref, bf16[256,1024]{1,0:T(8,128)(2,1)S(1)} %get-tuple-element.25.v_own.v_ref), custom_call_target="tpu_custom_call" | custom-call | flops 300000000 | bytes 2000000 | tf_op jit(solution)/shard_map/pallas_call | solution.py:217
  23.4 1.8 %shard_map.52.refs_3_ = f32[256,1024]{1,0:T(8,128)S(1)} custom-call(bf16[256,1024]{1,0:T(8,128)(2,1)S(1)} %get-tuple-element.37.q_ref.refs_1_, bf16[256,1024]{1,0:T(8,128)(2,1)S(1)} %get-tuple-element.39.k_ref, bf16[256,1024]{1,0:T(8,128)(2,1)S(1)} %get-tuple-element.40.v_ref), custom_call_target="tpu_custom_call" | custom-call | flops 300000000 | bytes 2000000 | tf_op jit(solution)/shard_map/pallas_call | solution.py:217
  25.3 1.2 %shard_map.54.refs_4_ = bf16[256,2048]{1,0:T(8,128)(2,1)} custom-call(bf16[512,128]{1,0:T(8,128)(2,1)S(1)} %get-tuple-element.41.refs_0_, bf16[256,1024]{1,0:T(8,128)(2,1)S(1)} %get-tuple-element.42.q_ref.refs_1_, f32[1,2048]{1,0:T(1,128)S(1)} %get-tuple-element.38.refs_2_, f32[256,1024]{1,0:T(8,128)S(1)} %shard_map.53.refs_3_), custom_call_target="tpu_custom_call" | custom-call | flops 100000000 | bytes 2000000 | tf_op jit(solution)/shard_map/pallas_call | solution.py:217
  26.5 0.0 collective-permute-done.4.refs_0_
  26.5 1.2 %shard_map.55 = bf16[256,2048]{1,0:T(8,128)(2,1)} custom-call(bf16[512,128]{1,0:T(8,128)(2,1)S(1)} %collective-permute-done.4.refs_0_, bf16[256,1024]{1,0:T(8,128)(2,1)S(1)} %get-tuple-element.37.q_ref.refs_1_, f32[1,2048]{1,0:T(1,128)S(1)} %get-tuple-element.38.refs_2_, f32[256,1024]{1,0:T(8,128)S(1)} %shard_map.52.refs_3_, ...), custom_call_target="tpu_custom_call", output_to_operand_aliasing={{}: (4, {})} | custom-call | flops 100000000 | bytes 2000000 | tf_op jit(solution)/shard_map/pallas_call | solution.py:217
  (1 shorter events, 0.0 us)
Async XLA Ops:
  1.6 1.9 %collective-permute-start = (bf16[512,128]{1,0:T(8,128)(2,1)S(1)}, bf16[512,128]{1,0:T(8,128)(2,1)S(1)}, u32[]{:S(2)}, u32[]{:S(2)}) collective-permute-start(bf16[512,128]{1,0:T(8,128)(2,1)S(1)} %get-tuple-element.27), channel_id=1, source_target_pairs={{0,1},{1,0},{2,3},{3,2},{4,5},{5,4},{6,7},{7,6},{8,9},{9,8},{10,11... | collective-permute-start | bytes 393224 | tf_op jit(solution)/shard_map/ppermute | solution.py:242
  3.6 5.5 %collective-permute-start.1 = (bf16[512,128]{1,0:T(8,128)(2,1)S(1)}, bf16[512,128]{1,0:T(8,128)(2,1)S(1)}, u32[]{:S(2)}, u32[]{:S(2)}) collective-permute-start(bf16[512,128]{1,0:T(8,128)(2,1)S(1)} %get-tuple-element.29), channel_id=1, source_target_pairs={{0,2},{1,5},{2,0},{3,7},{4,6},{5,1},{6,4},{7,3},{8,10},{9,13},{10,... | collective-permute-start | bytes 393224 | tf_op jit(solution)/shard_map/ppermute | solution.py:242
  9.2 6.2 %collective-permute-start.2 = (bf16[512,128]{1,0:T(8,128)(2,1)S(1)}, bf16[512,128]{1,0:T(8,128)(2,1)S(1)}, u32[]{:S(2)}, u32[]{:S(2)}) collective-permute-start(bf16[512,128]{1,0:T(8,128)(2,1)S(1)} %get-tuple-element.32), channel_id=1, source_target_pairs={{0,4},{1,9},{2,6},{3,11},{4,0},{5,13},{6,2},{7,15},{8,12},{9,1},{1... | collective-permute-start | bytes 393224 | tf_op jit(solution)/shard_map/ppermute | solution.py:242
  15.5 5.9 %collective-permute-start.3 = (bf16[512,128]{1,0:T(8,128)(2,1)S(1)}, bf16[512,128]{1,0:T(8,128)(2,1)S(1)}, u32[]{:S(2)}, u32[]{:S(2)}) collective-permute-start(bf16[512,128]{1,0:T(8,128)(2,1)S(1)} %get-tuple-element.34), channel_id=1, source_target_pairs={{0,8},{1,3},{2,10},{3,1},{4,12},{5,7},{6,14},{7,5},{8,0},{9,11},{1... | collective-permute-start | bytes 393224 | tf_op jit(solution)/shard_map/ppermute | solution.py:242
  21.5 5.0 %collective-permute-start.4 = (bf16[512,128]{1,0:T(8,128)(2,1)S(1)}, bf16[512,128]{1,0:T(8,128)(2,1)S(1)}, u32[]{:S(2)}, u32[]{:S(2)}) collective-permute-start(bf16[512,128]{1,0:T(8,128)(2,1)S(1)} %get-tuple-element.36), channel_id=1, source_target_pairs={{0,1},{1,0},{2,3},{3,2},{4,5},{5,4},{6,7},{7,6},{8,9},{9,8},{10,11... | collective-permute-start | bytes 393224 | tf_op jit(solution)/shard_map/ppermute | solution.py:242

commit v12 on v11

--- a/solution.py
+++ b/solution.py
@@ -63,19 +63,27 @@
             out_ref[pl.ds((quad * 2 + p) * HEAD_DIM, HEAD_DIM), :] = packed.astype(out_ref.dtype)
 
 
-def first_kernel(k_hbm, v_hbm, send, k_other, v_other, k_own, v_own, sems):
-    half = k_other.shape[1]
-    part = half // 2
+def first_kernel(k_hbm, v_hbm, send, k_other, v_other, k_own, v_own, turned, sems):
     loads = []
-    for n in range(2):
-        for m, (src, dst) in enumerate(((k_hbm, k_other), (v_hbm, v_other))):
-            loads.append(load_half(src, dst, False, sems.at[n, m], n * part, part))
-    late = [load_half(src, dst, True, sems.at[2, m]) for m, (src, dst) in enumerate(((k_hbm, k_own), (v_hbm, v_own)))]
-    quads = part // QUAD
-    for n in range(2):
-        wait_all(loads[2 * n : 2 * n + 2])
-        states_of(k_other, v_other, send, range(n * quads, (n + 1) * quads))
-    wait_all(late)
+    for own, k_ref, v_ref in ((False, k_other, v_other), (True, k_own, v_own)):
+        for src, dst in ((k_hbm, k_ref), (v_hbm, v_ref)):
+            loads.append(load_half(src, dst, own, sems.at[len(loads)]))
+    first = first_lanes((HEAD_DIM, PAIR))
+    quads = k_other.shape[1] // QUAD
+    loads[0].wait()
+    for quad in range(quads):
+        lanes = pl.ds(quad * QUAD, QUAD)
+        turned[lanes, :] = jnp.transpose(jnp.maximum(k_other[:, lanes], 0))
+    loads[1].wait()
+    for quad in range(quads):
+        lanes = pl.ds(quad * QUAD, QUAD)
+        full = dot(turned[lanes, :], v_other[:, lanes], ((1,), (0,)))
+        for p in range(2):
+            top = p * PAIR
+            rows = full[top : top + PAIR, top : top + PAIR]
+            packed = jnp.where(first, rows[:HEAD_DIM], rows[HEAD_DIM:])
+            send[pl.ds((quad * 2 + p) * HEAD_DIM, HEAD_DIM), :] = packed.astype(send.dtype)
+    wait_all(loads[2:])
 
 
 def second_kernel(k_own, v_own, q_hbm, gain_hbm, keep, q_own, q_other, gain, sems):
@@ -242,7 +250,7 @@
         return lax.ppermute(x, AXIS, [(i, i ^ (odd if i & CORE else even)) for i in range(size)])
 
     send, k_other, v_other, k_own, v_own = call(
-        first_kernel, (small16, *[tile] * 4), (keys, values), specs=[HBM] * 2, scratch=[DMA((3, 2))]
+        first_kernel, (small16, *[tile] * 4), (keys, values), specs=[HBM] * 2, scratch=[pltpu.VMEM((half, count), BF16), DMA((4,))]
     )
     got = swap(send, CORE, CORE)
     keep, q_own, q_other, gain_vmem = call(

time: 28.1 us -> 28.1 us (level)
  transfers between devices with their start and end apart: 5 -> 5, of which waited for: 3 -> 3; matrix products, arithmetic and copies ran while one was open for 0% -> 0% of each run, Pallas kernels for 22% -> 23%
where the time goes in v12:
time: 28.1 us; the launch traced here: 27.7 us
  waiting for transfers between devices  10.6 us (38%)
  Pallas kernels  9.29 us (33%)
  starting transfers between devices  7.75 us (28%)
    ppermute x5, waiting for transfers between devices, swap(): lax.ppermute(x, AXIS, [(i, i ^ (odd if i & CORE else even)) for i in rang...  10.6 us
    pallas_call x10, Pallas kernels, call(): pl.pallas_call(kernel, out_shape=outs, in_specs=specs, out_specs=([VMEM]...  9.29 us
    ppermute x5, starting transfers between devices, swap(): lax.ppermute(x, AXIS, [(i, i ^ (odd if i & CORE else even)) for i in rang...  7.75 us
  transfers between devices with their start and end apart: 5, of which 3 were waited for; matrix products, arithmetic and copies ran while one was open for 0% of the time, Pallas kernels for 23%

profile of v12, /device:TPU:0, one launch (start us, length us, event | category | flops | bytes accessed | tf_op | source)
XLA Modules:
  0.0 27.7 jit_solution(5900591515398933889)
XLA Ops:
  0.0 1.6 %shard_map.46 = (bf16[512,128]{1,0:T(8,128)(2,1)S(1)}, bf16[256,1024]{1,0:T(8,128)(2,1)S(1)}, bf16[256,1024]{1,0:T(8,128)(2,1)S(1)}, bf16[256,1024]{1,0:T(8,128)(2,1)S(1)}, bf16[256,1024]{1,0:T(8,128)(2,1)S(1)}) custom-call(bf16[256,2048]{1,0:T(8,128)(2,1)} %k_hbm.1, bf16[256,2048]{1,0:T(8,128)(2,1)} %v_hbm.1), custom_call_target="tpu_custom_call" | custom-call | flops 10000 | bytes 10000 | tf_op jit(solution)/shard_map/pallas_call | solution.py:225
  1.6 0.6 %collective-permute-start = (bf16[512,128]{1,0:T(8,128)(2,1)S(1)}, bf16[512,128]{1,0:T(8,128)(2,1)S(1)}, u32[]{:S(2)}, u32[]{:S(2)}) collective-permute-start(bf16[512,128]{1,0:T(8,128)(2,1)S(1)} %get-tuple-element.27), channel_id=1, source_target_pairs={{0,1},{1,0},{2,3},{3,2},{4,5},{5,4},{6,7},{7,6},{8,9},{9,8},{10,11... | collective-permute-start | bytes 393224 | tf_op jit(solution)/shard_map/ppermute | solution.py:250
  2.1 1.4 %shard_map.47 = (f32[512,128]{1,0:T(8,128)S(1)}, bf16[256,1024]{1,0:T(8,128)(2,1)S(1)}, bf16[256,1024]{1,0:T(8,128)(2,1)S(1)}, f32[1,2048]{1,0:T(1,128)S(1)}) custom-call(bf16[256,1024]{1,0:T(8,128)(2,1)S(1)} %get-tuple-element.24.k_own.k_ref, bf16[256,1024]{1,0:T(8,128)(2,1)S(1)} %get-tuple-element.25.v_own.v_ref, bf16[256,2048]{1,0:T(8,128)(2,1)} %q_hbm.1, ...), custom_call_target="tpu_custom_call" | custom-call | flops 150000000 | bytes 2000000 | tf_op jit(solution)/shard_map/pallas_call | solution.py:225
  3.5 0.0 collective-permute-done.got
  3.5 0.1 shard_map.48
  3.6 2.6 %collective-permute-start.1 = (bf16[512,128]{1,0:T(8,128)(2,1)S(1)}, bf16[512,128]{1,0:T(8,128)(2,1)S(1)}, u32[]{:S(2)}, u32[]{:S(2)}) collective-permute-start(bf16[512,128]{1,0:T(8,128)(2,1)S(1)} %get-tuple-element.29), channel_id=1, source_target_pairs={{0,2},{1,5},{2,0},{3,7},{4,6},{5,1},{6,4},{7,3},{8,10},{9,13},{10,... | collective-permute-start | bytes 393224 | tf_op jit(solution)/shard_map/ppermute | solution.py:250
  6.2 2.9 %collective-permute-done.1.refs_1_ = bf16[512,128]{1,0:T(8,128)(2,1)S(1)} collective-permute-done((bf16[512,128]{1,0:T(8,128)(2,1)S(1)}, bf16[512,128]{1,0:T(8,128)(2,1)S(1)}, u32[]{:S(2)}, u32[]{:S(2)}) %collective-permute-start.1) | collective-permute-done | bytes 131104 | tf_op jit(solution)/shard_map/ppermute | solution.py:250
  9.2 2.1 %collective-permute-start.2 = (bf16[512,128]{1,0:T(8,128)(2,1)S(1)}, bf16[512,128]{1,0:T(8,128)(2,1)S(1)}, u32[]{:S(2)}, u32[]{:S(2)}) collective-permute-start(bf16[512,128]{1,0:T(8,128)(2,1)S(1)} %get-tuple-element.32), channel_id=1, source_target_pairs={{0,4},{1,9},{2,6},{3,11},{4,0},{5,13},{6,2},{7,15},{8,12},{9,1},{1... | collective-permute-start | bytes 393224 | tf_op jit(solution)/shard_map/ppermute | solution.py:250
  11.3 4.1 %collective-permute-done.2.refs_2_ = bf16[512,128]{1,0:T(8,128)(2,1)S(1)} collective-permute-done((bf16[512,128]{1,0:T(8,128)(2,1)S(1)}, bf16[512,128]{1,0:T(8,128)(2,1)S(1)}, u32[]{:S(2)}, u32[]{:S(2)}) %collective-permute-start.2) | collective-permute-done | bytes 131104 | tf_op jit(solution)/shard_map/ppermute | solution.py:250
  15.4 0.1 shard_map.50
  15.5 2.4 %collective-permute-start.3 = (bf16[512,128]{1,0:T(8,128)(2,1)S(1)}, bf16[512,128]{1,0:T(8,128)(2,1)S(1)}, u32[]{:S(2)}, u32[]{:S(2)}) collective-permute-start(bf16[512,128]{1,0:T(8,128)(2,1)S(1)} %get-tuple-element.34), channel_id=1, source_target_pairs={{0,8},{1,3},{2,10},{3,1},{4,12},{5,7},{6,14},{7,5},{8,0},{9,11},{1... | collective-permute-start | bytes 393224 | tf_op jit(solution)/shard_map/ppermute | solution.py:250
  17.8 3.5 %collective-permute-done.3.got = bf16[512,128]{1,0:T(8,128)(2,1)S(1)} collective-permute-done((bf16[512,128]{1,0:T(8,128)(2,1)S(1)}, bf16[512,128]{1,0:T(8,128)(2,1)S(1)}, u32[]{:S(2)}, u32[]{:S(2)}) %collective-permute-start.3) | collective-permute-done | bytes 131104 | tf_op jit(solution)/shard_map/ppermute | solution.py:250
  21.4 0.1 shard_map.51
  21.5 0.1 collective-permute-start.4
  21.6 1.8 %shard_map.53.refs_3_ = f32[256,1024]{1,0:T(8,128)S(1)} custom-call(bf16[256,1024]{1,0:T(8,128)(2,1)S(1)} %get-tuple-element.42.q_ref.refs_1_, bf16[256,1024]{1,0:T(8,128)(2,1)S(1)} %get-tuple-element.24.k_own.k_ref, bf16[256,1024]{1,0:T(8,128)(2,1)S(1)} %get-tuple-element.25.v_own.v_ref), custom_call_target="tpu_custom_call" | custom-call | flops 300000000 | bytes 2000000 | tf_op jit(solution)/shard_map/pallas_call | solution.py:225
  23.4 1.8 %shard_map.52.refs_3_ = f32[256,1024]{1,0:T(8,128)S(1)} custom-call(bf16[256,1024]{1,0:T(8,128)(2,1)S(1)} %get-tuple-element.37.q_ref.refs_1_, bf16[256,1024]{1,0:T(8,128)(2,1)S(1)} %get-tuple-element.39.k_ref, bf16[256,1024]{1,0:T(8,128)(2,1)S(1)} %get-tuple-element.40.v_ref), custom_call_target="tpu_custom_call" | custom-call | flops 300000000 | bytes 2000000 | tf_op jit(solution)/shard_map/pallas_call | solution.py:225
  25.2 1.2 %shard_map.54.refs_4_ = bf16[256,2048]{1,0:T(8,128)(2,1)} custom-call(bf16[512,128]{1,0:T(8,128)(2,1)S(1)} %get-tuple-element.41.refs_0_, bf16[256,1024]{1,0:T(8,128)(2,1)S(1)} %get-tuple-element.42.q_ref.refs_1_, f32[1,2048]{1,0:T(1,128)S(1)} %get-tuple-element.38.refs_2_, f32[256,1024]{1,0:T(8,128)S(1)} %shard_map.53.refs_3_), custom_call_target="tpu_custom_call" | custom-call | flops 100000000 | bytes 2000000 | tf_op jit(solution)/shard_map/pallas_call | solution.py:225
  26.4 0.0 collective-permute-done.4.refs_0_
  26.5 1.2 %shard_map.55 = bf16[256,2048]{1,0:T(8,128)(2,1)} custom-call(bf16[512,128]{1,0:T(8,128)(2,1)S(1)} %collective-permute-done.4.refs_0_, bf16[256,1024]{1,0:T(8,128)(2,1)S(1)} %get-tuple-element.37.q_ref.refs_1_, f32[1,2048]{1,0:T(1,128)S(1)} %get-tuple-element.38.refs_2_, f32[256,1024]{1,0:T(8,128)S(1)} %shard_map.52.refs_3_, ...), custom_call_target="tpu_custom_call", output_to_operand_aliasing={{}: (4, {})} | custom-call | flops 100000000 | bytes 2000000 | tf_op jit(solution)/shard_map/pallas_call | solution.py:225
  (1 shorter events, 0.0 us)
Async XLA Ops:
  1.6 1.9 %collective-permute-start = (bf16[512,128]{1,0:T(8,128)(2,1)S(1)}, bf16[512,128]{1,0:T(8,128)(2,1)S(1)}, u32[]{:S(2)}, u32[]{:S(2)}) collective-permute-start(bf16[512,128]{1,0:T(8,128)(2,1)S(1)} %get-tuple-element.27), channel_id=1, source_target_pairs={{0,1},{1,0},{2,3},{3,2},{4,5},{5,4},{6,7},{7,6},{8,9},{9,8},{10,11... | collective-permute-start | bytes 393224 | tf_op jit(solution)/shard_map/ppermute | solution.py:250
  3.6 5.5 %collective-permute-start.1 = (bf16[512,128]{1,0:T(8,128)(2,1)S(1)}, bf16[512,128]{1,0:T(8,128)(2,1)S(1)}, u32[]{:S(2)}, u32[]{:S(2)}) collective-permute-start(bf16[512,128]{1,0:T(8,128)(2,1)S(1)} %get-tuple-element.29), channel_id=1, source_target_pairs={{0,2},{1,5},{2,0},{3,7},{4,6},{5,1},{6,4},{7,3},{8,10},{9,13},{10,... | collective-permute-start | bytes 393224 | tf_op jit(solution)/shard_map/ppermute | solution.py:250
  9.2 6.2 %collective-permute-start.2 = (bf16[512,128]{1,0:T(8,128)(2,1)S(1)}, bf16[512,128]{1,0:T(8,128)(2,1)S(1)}, u32[]{:S(2)}, u32[]{:S(2)}) collective-permute-start(bf16[512,128]{1,0:T(8,128)(2,1)S(1)} %get-tuple-element.32), channel_id=1, source_target_pairs={{0,4},{1,9},{2,6},{3,11},{4,0},{5,13},{6,2},{7,15},{8,12},{9,1},{1... | collective-permute-start | bytes 393224 | tf_op jit(solution)/shard_map/ppermute | solution.py:250
  15.5 5.9 %collective-permute-start.3 = (bf16[512,128]{1,0:T(8,128)(2,1)S(1)}, bf16[512,128]{1,0:T(8,128)(2,1)S(1)}, u32[]{:S(2)}, u32[]{:S(2)}) collective-permute-start(bf16[512,128]{1,0:T(8,128)(2,1)S(1)} %get-tuple-element.34), channel_id=1, source_target_pairs={{0,8},{1,3},{2,10},{3,1},{4,12},{5,7},{6,14},{7,5},{8,0},{9,11},{1... | collective-permute-start | bytes 393224 | tf_op jit(solution)/shard_map/ppermute | solution.py:250
  21.5 5.0 %collective-permute-start.4 = (bf16[512,128]{1,0:T(8,128)(2,1)S(1)}, bf16[512,128]{1,0:T(8,128)(2,1)S(1)}, u32[]{:S(2)}, u32[]{:S(2)}) collective-permute-start(bf16[512,128]{1,0:T(8,128)(2,1)S(1)} %get-tuple-element.36), channel_id=1, source_target_pairs={{0,1},{1,0},{2,3},{3,2},{4,5},{5,4},{6,7},{7,6},{8,9},{9,8},{10,11... | collective-permute-start | bytes 393224 | tf_op jit(solution)/shard_map/ppermute | solution.py:250
